TPU v7x, 512 devices: a whole 4x4x16 slice. The times are simulated.
512 devices in a mesh: dp: 2 (over z_hi), fsdp: 16 (over z_lo, core), tile: 16 (over y, x).
Axes of the slice: x: 4, y: 4, z: 16 (z_hi: 2, z_lo: 8; z = z_hi * 8 + z_lo), core: 2. Of those that a mesh axis runs over, the one named last changes fastest.
Arguments:
- tokens: bfloat16 [32, 8, 512, 1536], P(('dp', 'fsdp'), None, 'tile'), may hold values from -6 to 6
- norm_gain: float32 [1536], replicated, may hold values from 0.25 to 1.75
- query_key_value_weight: bfloat16 [1536, 2304], P('fsdp'), may hold values from -5 to 5
- out_weight: bfloat16 [768, 1536], P('fsdp'), may hold values from -0.21875 to 0.21875
- head_weight: bfloat16 [1536, 320], P('fsdp'), may hold values from -0.15625 to 0.15625
- coarse: float32 [32, 20, 8, 512], P(('dp', 'fsdp'), None, None, 'tile'), may hold values from -36 to 36
- grad_fine: float32 [32, 20, 32, 2048], P(('dp', 'fsdp'), None, None, 'tile'), may hold values from -0.6 to 0.6
Outputs:
- fine_grid: float32 [32, 20, 32, 2048], P(('dp', 'fsdp'), None, None, 'tile')
- grad_tokens: bfloat16 [32, 8, 512, 1536], P(('dp', 'fsdp'), None, 'tile')
- grad_head: float32 [1536, 320], P('fsdp')
All inputs are finite; a program needn't handle non-finite values.
Results may differ from a plain program's by a relative error of at most 0.0059.
Values may be sent and summed in bfloat16 or wider, within the bound.
No kernel may reach another device: no remote copies, remote signals or barrier semaphores. Data moves between devices by JAX's collectives and lax.ppermute only.
A program may use at most 64 MiB of HBM per device.

v0:
```python
import jax
import jax.numpy as jnp
from jax import lax
from jax.sharding import PartitionSpec as P

D = 1536
HEADS = 8
HEAD_DIM = 96
VARS = 20
MARGIN = 8
INNER = 768
HEAD_OUT = 320


EPSILON = 1e-05


def with_halo(shard, sides, width):
    for axis, dim in sides:
        devices, length = (lax.axis_size(axis), shard.shape[dim])
        up = [(i, (i + 1) % devices) for i in range(devices)]
        down = [(j, i) for i, j in up]
        last = lax.slice_in_dim(shard, length - width, length, axis=dim)
        leading = lax.slice_in_dim(shard, 0, width, axis=dim)
        before = lax.ppermute(last, axis, up)
        after = lax.ppermute(leading, axis, down)
        shard = jnp.concatenate([before, shard, after], axis=dim)
    return shard


def from_behind(value, axis, steps):
    count = lax.axis_size(axis)
    pairs = [(source, (source + steps) % count) for source in range(count)]
    return lax.ppermute(value, axis, pairs)


def layer_norm(values):
    average = jnp.mean(values, axis=-1, keepdims=True)
    centred = values - average
    variance = jnp.mean(centred * centred, axis=-1, keepdims=True)
    inverse_dev = lax.rsqrt(variance + EPSILON)
    return (centred * inverse_dev, inverse_dev)


def norm_backward(grad_normed, standard, inverse_dev, norm_gain):
    grad_standard = grad_normed * norm_gain
    first_mean = jnp.mean(grad_standard, axis=-1, keepdims=True)
    second_mean = jnp.mean(grad_standard * standard, axis=-1, keepdims=True)
    return inverse_dev * (grad_standard - first_mean - standard * second_mean)


def attend_forward(queries, keys_values):
    query_count = queries.shape[0]
    key_count = keys_values.shape[0]
    score_scale = HEAD_DIM ** (-0.5)
    query_heads = queries.reshape(query_count, HEADS, HEAD_DIM)
    key_heads = keys_values[:, :INNER].reshape(key_count, HEADS, HEAD_DIM)
    value_heads = keys_values[:, INNER:].reshape(key_count, HEADS, HEAD_DIM)
    scores = (
        jnp.einsum("qhd,khd->hqk", query_heads, key_heads, preferred_element_type=jnp.float32)
        * score_scale
    )
    biggest = jnp.max(scores, axis=-1, keepdims=True)
    exponent = jnp.exp(scores - biggest)
    softmax_out = exponent / jnp.sum(exponent, axis=-1, keepdims=True)
    softmax_low = softmax_out.astype(jnp.bfloat16)
    attended = jnp.einsum(
        "hqk,khd->qhd", softmax_low, value_heads, preferred_element_type=jnp.float32
    )
    return (attended.astype(jnp.bfloat16).reshape(query_count, INNER), softmax_out)


def attend_backward(softmax_out, queries, keys_values, grad_attended):
    query_count = queries.shape[0]
    key_count = keys_values.shape[0]
    score_scale = HEAD_DIM ** (-0.5)
    query_heads = queries.reshape(query_count, HEADS, HEAD_DIM)
    key_heads = keys_values[:, :INNER].reshape(key_count, HEADS, HEAD_DIM)
    value_heads = keys_values[:, INNER:].reshape(key_count, HEADS, HEAD_DIM)
    grad_heads = grad_attended.reshape(query_count, HEADS, HEAD_DIM)
    softmax_low = softmax_out.astype(jnp.bfloat16)
    grad_values = jnp.einsum(
        "hqk,qhd->khd", softmax_low, grad_heads, preferred_element_type=jnp.float32
    )
    grad_weights = jnp.einsum(
        "qhd,khd->hqk", grad_heads, value_heads, preferred_element_type=jnp.float32
    )
    weighted = jnp.sum(softmax_out * grad_weights, axis=-1, keepdims=True)
    grad_scores = (softmax_out * (grad_weights - weighted)).astype(jnp.bfloat16)
    grad_queries = (
        jnp.einsum("hqk,khd->qhd", grad_scores, key_heads, preferred_element_type=jnp.float32)
        * score_scale
    )
    grad_keys = (
        jnp.einsum("hqk,qhd->khd", grad_scores, query_heads, preferred_element_type=jnp.float32)
        * score_scale
    )
    pair_gradient_rows = jnp.concatenate(
        [grad_keys.reshape(key_count, INNER), grad_values.reshape(key_count, INNER)], axis=1
    )
    return (grad_queries.astype(jnp.bfloat16).reshape(query_count, INNER), pair_gradient_rows)


def interp_weights(fine_index):
    coarse_cell = fine_index // 4
    phase_index = fine_index % 4
    lower_shift = (phase_index < 2).astype(jnp.int32)
    upper_weight = (2 * phase_index - 3 + 8 * lower_shift).astype(jnp.float32) / 8.0
    return (coarse_cell - lower_shift, upper_weight)


def build_matrix(lower_cell, upper_cell, upper_weight, count):
    columns = jnp.arange(count, dtype=jnp.int32)
    lower_part = jnp.where(
        columns[None, :] == lower_cell[:, None], 1.0 - upper_weight[:, None], 0.0
    )
    upper_portion = jnp.where(columns[None, :] == upper_cell[:, None], upper_weight[:, None], 0.0)
    return lower_part + upper_portion


def contract_last(left_side, right_side):
    return lax.dot_general(
        left_side, right_side, (((1,), (1,)), ((), ())), preferred_element_type=jnp.float32
    )


def shards(tokens, norm_gain, query_key_value_weight, out_weight, head_weight, coarse, grad_fine):
    lat_rows = tokens.shape[1]
    lon_cols = tokens.shape[2]
    row_count = lat_rows * lon_cols
    flattened_rows = tokens[0].reshape(row_count, D).astype(jnp.float32)
    standard, inverse_dev = layer_norm(flattened_rows)
    normed = (standard * norm_gain).astype(jnp.bfloat16)
    full_qkv = lax.all_gather(query_key_value_weight, "fsdp", axis=0, tiled=True)
    projected = jnp.dot(normed, full_qkv, preferred_element_type=jnp.float32).astype(jnp.bfloat16)
    queries = projected[:, :INNER]
    pairs_local = projected[:, INNER:]
    margin_pairs = with_halo(
        pairs_local.reshape(lat_rows, lon_cols, 2 * INNER), (("tile", 1),), MARGIN
    )
    keys_values = margin_pairs.reshape(lat_rows * (lon_cols + 2 * MARGIN), 2 * INNER)
    attended, softmax_out = attend_forward(queries, keys_values)
    full_out = lax.all_gather(out_weight, "fsdp", axis=0, tiled=True)
    mixed_out = jnp.dot(attended, full_out, preferred_element_type=jnp.float32)
    hidden = (flattened_rows + mixed_out).astype(jnp.bfloat16)
    full_head = lax.all_gather(head_weight, "fsdp", axis=0, tiled=True)
    head_out = jnp.dot(hidden, full_head, preferred_element_type=jnp.float32)
    fine_head = (
        head_out.reshape(lat_rows, lon_cols, VARS, 4, 4)
        .transpose(2, 0, 3, 1, 4)
        .reshape(VARS, 4 * lat_rows, 4 * lon_cols)
    )
    coarse_padded_grid = with_halo(coarse[0], (("tile", 2),), 1)
    lat_lower, lat_upper_weight = interp_weights(jnp.arange(4 * lat_rows, dtype=jnp.int32))
    latitude_matrix = build_matrix(
        jnp.clip(lat_lower, 0, lat_rows - 1),
        jnp.clip(lat_lower + 1, 0, lat_rows - 1),
        lat_upper_weight,
        lat_rows,
    )
    lon_lower, lon_upper_weight = interp_weights(jnp.arange(4 * lon_cols, dtype=jnp.int32))
    lon_matrix = build_matrix(lon_lower + 1, lon_lower + 2, lon_upper_weight, lon_cols + 2)
    incomplete_grid = jnp.einsum(
        "lj,kji->kli", latitude_matrix, coarse_padded_grid, precision=lax.Precision.HIGHEST
    )
    residual = jnp.einsum(
        "vrb,cb->vrc", incomplete_grid, lon_matrix, precision=lax.Precision.HIGHEST
    )
    fine_grid = fine_head + residual
    grad_rows = (
        grad_fine[0]
        .reshape(VARS, lat_rows, 4, lon_cols, 4)
        .transpose(1, 3, 0, 2, 4)
        .reshape(row_count, HEAD_OUT)
    )
    grad_rows = grad_rows.astype(jnp.bfloat16)
    head_term = lax.dot_general(
        hidden, grad_rows, (((0,), (0,)), ((), ())), preferred_element_type=jnp.float32
    )
    head_block = lax.psum_scatter(head_term, "fsdp", scatter_dimension=0, tiled=True)
    grad_head = lax.psum(head_block, ("dp", "tile"))
    grad_hidden = contract_last(grad_rows, full_head)
    grad_attended = contract_last(grad_hidden.astype(jnp.bfloat16), full_out).astype(jnp.bfloat16)
    grad_queries, pair_gradient_rows = attend_backward(
        softmax_out, queries, keys_values, grad_attended
    )
    pair_gradient_rows = pair_gradient_rows.reshape(lat_rows, lon_cols + 2 * MARGIN, 2 * INNER)
    from_left = from_behind(pair_gradient_rows[:, lon_cols + MARGIN :], "tile", 1)
    from_right = from_behind(pair_gradient_rows[:, :MARGIN], "tile", -1)
    own_cells = pair_gradient_rows[:, MARGIN : MARGIN + lon_cols]
    own_cells = own_cells + jnp.pad(from_left, ((0, 0), (0, lon_cols - MARGIN), (0, 0)))
    own_cells = own_cells + jnp.pad(from_right, ((0, 0), (lon_cols - MARGIN, 0), (0, 0)))
    grad_all = jnp.concatenate(
        [grad_queries, own_cells.reshape(row_count, 2 * INNER).astype(jnp.bfloat16)], axis=1
    )
    grad_normed = contract_last(grad_all, full_qkv)
    grad_input = grad_hidden + norm_backward(grad_normed, standard, inverse_dev, norm_gain)
    grad_tokens = grad_input.astype(jnp.bfloat16).reshape(1, lat_rows, lon_cols, D)
    return (fine_grid[None], grad_tokens, grad_head)


def solution(mesh):
    placed = (
        P(("dp", "fsdp"), None, "tile", None),
        P(),
        P("fsdp", None),
        P("fsdp", None),
        P("fsdp", None),
        P(("dp", "fsdp"), None, None, "tile"),
        P(("dp", "fsdp"), None, None, "tile"),
    )
    return jax.shard_map(
        shards,
        mesh=mesh,
        in_specs=placed,
        out_specs=(
            P(("dp", "fsdp"), None, None, "tile"),
            P(("dp", "fsdp"), None, "tile", None),
            P("fsdp", None),
        ),
        check_vma=False,
    )
```

profile of v0, /device:TPU:2, one launch (start us, length us, event | category | flops | bytes accessed | tf_op | source)
XLA Modules:
  0.0 943.6 jit_solution(4857148850893295786)
XLA Ops:
  10.4 3.4 collective-permute-start.2
  13.8 6.3 collective-permute-start.3
  25.7 46.6 %all_gather.11 = bf16[1536,320]{1,0:T(8,128)(2,1)S(1)} all-gather(bf16[96,320]{1,0:T(8,128)(2,1)} %param.11), channel_id=1, replica_groups=mesh['dp'=2,'fsdp'=16,'tile'=16] {'fsdp'}, dimensions={0}, use_global_device_ids=true | all-gather | bytes 1044480 | tf_op jit(solution)/shard_map/all_gather | solution.py:146
  77.8 55.1 %all-gather.3.cloned.1.call-done = bf16[1536,2304]{1,0:T(8,128)(2,1)} async-done(((bf16[96,2304]{1,0:T(8,128)(2,1)}), bf16[1536,2304]{1,0:T(8,128)(2,1)}) %all-gather.3.cloned.1.call-update) | async-done | bytes 7077904 | tf_op jit(solution)/shard_map/all_gather | solution.py:134
  132.9 5.3 convolution_convert_fusion
  140.0 3.2 collective-permute-start
  143.2 2.8 collective-permute-start.1
  146.0 86.6 %all-gather.5.cloned.1.call-done = bf16[768,1536]{1,0:T(8,128)(2,1)} async-done(((bf16[48,1536]{1,0:T(8,128)(2,1)}), bf16[768,1536]{1,0:T(8,128)(2,1)}) %all-gather.5.cloned.1.call-update) | async-done | bytes 2359312 | tf_op jit(solution)/shard_map/all_gather | solution.py:143
  232.6 3.2 convolution_convert_fusion.1
  248.2 4.0 fusion.57
  252.2 2.9 convolution_convert_fusion.2
  260.7 3.0 copy.20
  263.8 3.0 copy.21
  266.8 2.6 convolution_bitcast_fusion
  271.0 2.7 concatenate.20
  274.9 3.0 multiply_reduce_fusion
  287.6 3.4 collective-permute-start.4
  291.1 2.8 collective-permute-start.5
  296.7 3.5 collective-permute-done.4
  300.2 3.3 collective-permute-done.5
  305.2 6.3 fusion.52
  311.6 73.0 %reduce-scatter.2.cloned.1.call-done = f32[96,320]{1,0:T(8,128)} async-done(((f32[1536,320]{1,0:T(8,128)}), f32[96,320]{1,0:T(8,128)}) %reduce-scatter.2.cloned.1.call-update) | async-done | bytes 122896 | tf_op jit(solution)/shard_map/reduce_scatter | solution.py:180
  384.5 2.9 add_convert_fusion
  387.4 548.1 %all-reduce.4.cloned.1.call-done = f32[96,320]{1,0:T(8,128)} async-done(((f32[96,320]{1,0:T(8,128)}), f32[96,320]{1,0:T(8,128)}) %all-reduce.4.cloned.1.call-update) | async-done | bytes 122896 | tf_op jit(solution)/shard_map/psum | solution.py:181
  (109 shorter events, 52.5 us)
Async XLA Ops:
  7.2 14.4 %copy-start = (bf16[1,8,32,1536]{3,2,1,0:T(8,128)(2,1)S(1)}, bf16[1,8,32,1536]{3,2,1,0:T(8,128)(2,1)}, u32[]{:S(2)}) copy-start(bf16[1,8,32,1536]{3,2,1,0:T(8,128)(2,1)} %param.7) | copy-start | bytes 2359300
  7.2 14.8 %copy-start.19 = (f32[1,20,32,128]{3,2,1,0:T(8,128)S(1)}, f32[1,20,32,128]{3,2,1,0:T(8,128)}, u32[]{:S(2)}) copy-start(f32[1,20,32,128]{3,2,1,0:T(8,128)} %param.13) | copy-start | bytes 983044
  7.2 125.7 %all-gather.3.cloned.1.call-start = ((), (), s32[]{:S(2)}) async-start(), calls=%async_computation.1 | async-start | bytes 7520256 | tf_op jit(solution)/shard_map/all_gather | solution.py:134
  7.9 224.7 %all-gather.5.cloned.1.call-start = ((), (), s32[]{:S(2)}) async-start(), calls=%async_computation.2 | async-start | bytes 2506752 | tf_op jit(solution)/shard_map/all_gather | solution.py:143
  8.7 375.8 %reduce-scatter.2.cloned.1.call-start = ((), (), s32[]{:S(2)}) async-start(), calls=%async_computation.3 | async-start | bytes 2506752 | tf_op jit(solution)/shard_map/reduce_scatter | solution.py:180
  10.4 65.2 %collective-permute-start.2 = (f32[20,8,1]{2,1,0:T(8,128)}, f32[20,8,1]{2,1,0:T(8,128)}, u32[]{:S(2)}, u32[]{:S(2)}) collective-permute-start(f32[20,8,1]{2,1,0:T(8,128)} %get-tuple-element.11), channel_id=1, source_target_pairs={{0,1},{1,2},{2,3},{3,4},{4,5},{5,6},{6,7},{7,8},{8,9},{9,10},{10,1... | collective-permute-start | bytes 1928 | tf_op jit(solution)/shard_map/ppermute | solution.py:25
  13.8 61.8 %collective-permute-start.3 = (f32[20,8,1]{2,1,0:T(8,128)}, f32[20,8,1]{2,1,0:T(8,128)}, u32[]{:S(2)}, u32[]{:S(2)}) collective-permute-start(f32[20,8,1]{2,1,0:T(8,128)} %get-tuple-element.12), channel_id=1, source_target_pairs={{1,0},{2,1},{3,2},{4,3},{5,4},{6,5},{7,6},{8,7},{9,8},{10,9},{11,1... | collective-permute-start | bytes 1928 | tf_op jit(solution)/shard_map/ppermute | solution.py:26
  72.3 3.4 copy-start.15
  140.0 101.5 %collective-permute-start = (bf16[8,8,1536]{2,1,0:T(8,128)(2,1)}, bf16[8,8,1536]{2,1,0:T(8,128)(2,1)}, u32[]{:S(2)}, u32[]{:S(2)}) collective-permute-start(bf16[8,8,1536]{2,1,0:T(8,128)(2,1)} %get-tuple-element.9), channel_id=1, source_target_pairs={{0,1},{1,2},{2,3},{3,4},{4,5},{5,6},{6,7},{7,8},{8,9},{9,10},{10,1... | collective-permute-start | bytes 589832 | tf_op jit(solution)/shard_map/ppermute | solution.py:25
  143.2 98.3 %collective-permute-start.1 = (bf16[8,8,1536]{2,1,0:T(8,128)(2,1)}, bf16[8,8,1536]{2,1,0:T(8,128)(2,1)}, u32[]{:S(2)}, u32[]{:S(2)}) collective-permute-start(bf16[8,8,1536]{2,1,0:T(8,128)(2,1)} %get-tuple-element.10), channel_id=1, source_target_pairs={{1,0},{2,1},{3,2},{4,3},{5,4},{6,5},{7,6},{8,7},{9,8},{10,9},{11,1... | collective-permute-start | bytes 589832 | tf_op jit(solution)/shard_map/ppermute | solution.py:26
  273.7 661.8 %all-reduce.4.cloned.1.call-start = ((), (), s32[]{:S(2)}) async-start(), calls=%async_computation.4 | async-start | bytes 294912 | tf_op jit(solution)/shard_map/psum | solution.py:181
  274.9 3.0 copy-start.3
  285.0 8.9 copy-start.2
  285.0 8.9 copy-start.6
  287.6 12.6 %collective-permute-start.4 = (f32[8,8,1536]{2,1,0:T(8,128)}, f32[8,8,1536]{2,1,0:T(8,128)}, u32[]{:S(2)}, u32[]{:S(2)}) collective-permute-start(f32[8,8,1536]{2,1,0:T(8,128)} %get-tuple-element.5), channel_id=1, source_target_pairs={{0,1},{1,2},{2,3},{3,4},{4,5},{5,6},{6,7},{7,8},{8,9},{9,10},{10,1... | collective-permute-start | bytes 1179656 | tf_op jit(solution)/shard_map/ppermute | solution.py:34
  291.0 4.5 copy-start.11
  291.0 4.5 copy-start.13
  291.0 4.5 copy-start.22
  291.0 4.5 copy-start.23
  291.0 4.5 copy-start.24
  291.1 4.5 copy-start.25
  291.1 12.4 %collective-permute-start.5 = (f32[8,8,1536]{2,1,0:T(8,128)}, f32[8,8,1536]{2,1,0:T(8,128)}, u32[]{:S(2)}, u32[]{:S(2)}) collective-permute-start(f32[8,8,1536]{2,1,0:T(8,128)} %get-tuple-element.6), channel_id=1, source_target_pairs={{0,15},{1,0},{2,1},{3,2},{4,3},{5,4},{6,5},{7,6},{8,7},{9,8},{10,9... | collective-permute-start | bytes 1179656 | tf_op jit(solution)/shard_map/ppermute | solution.py:34
  296.7 8.5 copy-start.18
  296.7 8.6 copy-start.21
  (12 other events, 18.7 us)
Sparse Core Ops, SparseCore 0:
  10.1 122.7 all-gather.2
  135.0 97.5 all-gather.4
  273.8 110.6 reduce-scatter.1
  387.3 548.2 all-reduce.3
where the time goes:
time: 945 us; the launch traced here: 944 us
  waiting for transfers between devices  771 us (82%)
  blocking collectives  46.6 us (5%)
  local copies, waits for them, and re-layouts  41.8 us (4%)
  matrix products  37.3 us (4%)
  starting transfers between devices  22.1 us (2%)
  between operations  14.2 us (2%)
  other arithmetic  10.8 us (1%)
    psum x1, waiting for transfers between devices, shards(): grad_head = lax.psum(head_block, ('dp', 'tile'))  548 us
    all_gather x1, waiting for transfers between devices, shards(): full_out = lax.all_gather(out_weight, 'fsdp', axis=0, tiled=True)  86.6 us
    reduce_scatter x1, waiting for transfers between devices, shards(): lax.psum_scatter(head_term, 'fsdp', scatter_dimension=0, tiled=True)  73 us
    all_gather x1, waiting for transfers between devices, shards(): lax.all_gather(query_key_value_weight, 'fsdp', axis=0, tiled=True)  55.1 us
    all_gather x1, blocking collectives, shards(): full_head = lax.all_gather(head_weight, 'fsdp', axis=0, tiled=True)  46.6 us
  transfers between devices with their start and end apart: 10, of which 6 were waited for; matrix products, arithmetic and copies ran while one was open for 5% of the time, Pallas kernels for 0%

commit v1 on v0

--- a/solution.py
+++ b/solution.py
@@ -1,6 +1,7 @@
 import jax
 import jax.numpy as jnp
 from jax import lax
+from jax.sharding import Mesh
 from jax.sharding import PartitionSpec as P
 
 D = 1536
@@ -124,6 +125,48 @@
     )
 
 
+ZS = 8
+CORES = 2
+YS = 4
+XS = 4
+FSDP = ("z", "c")
+TILE = ("y", "x")
+HALF_QKV = 1152
+HALF_OUT = 768
+
+
+def gather_weights(qkv, out_w, head_w):
+    half = lax.axis_index("dp")
+    qkv_half = lax.dynamic_slice_in_dim(qkv, half * HALF_QKV, HALF_QKV, 1)
+    out_half = lax.dynamic_slice_in_dim(out_w, half * HALF_OUT, HALF_OUT, 1)
+    out_half = jnp.concatenate([out_half[:, :384], out_half[:, 384:]], axis=0)
+    head_half = lax.dynamic_slice_in_dim(head_w, half * 160, 160, 1)
+    packed = jnp.concatenate([qkv_half, out_half, head_half], axis=1)
+    full = lax.all_gather(packed, ("dp",) + FSDP, axis=0, tiled=True)
+    full = full.reshape(2, D, 1696)
+    full_qkv = jnp.concatenate([full[0, :, :HALF_QKV], full[1, :, :HALF_QKV]], axis=1)
+    out_part = full[:, :, HALF_QKV:1536].reshape(2, 16, 2, 48, 384)
+    full_out = out_part.transpose(1, 3, 0, 2, 4).reshape(INNER, D)
+    full_head = jnp.concatenate([full[0, :, 1536:], full[1, :, 1536:]], axis=1)
+    return full_qkv, full_out, full_head
+
+
+def reduce_head(head_term):
+    core = lax.axis_index("c")
+    parts = head_term.reshape(ZS, CORES, 96, HEAD_OUT)
+    own = lax.dynamic_index_in_dim(parts, core, 1, keepdims=False)
+    other = lax.dynamic_index_in_dim(parts, 1 - core, 1, keepdims=False)
+    pair = own + lax.ppermute(other, "c", [(0, 1), (1, 0)])
+    pieces = pair.reshape(ZS, 16, 6, HEAD_OUT).transpose(1, 0, 2, 3).astype(jnp.bfloat16)
+    pieces = lax.all_to_all(pieces, TILE, 0, 0, tiled=True)
+    over_tile = jnp.sum(pieces.astype(jnp.float32), axis=0)
+    both = jnp.broadcast_to(over_tile[None], (2, ZS, 6, HEAD_OUT)).reshape(2 * ZS, 6, HEAD_OUT)
+    both = lax.all_to_all(both, ("dp", "z"), 0, 0, tiled=True)
+    total = jnp.sum(both, axis=0)
+    spread = jnp.broadcast_to(total[None], (16, 6, HEAD_OUT))
+    return lax.all_to_all(spread, TILE, 0, 0, tiled=True).reshape(96, HEAD_OUT)
+
+
 def shards(tokens, norm_gain, query_key_value_weight, out_weight, head_weight, coarse, grad_fine):
     lat_rows = tokens.shape[1]
     lon_cols = tokens.shape[2]
@@ -131,26 +174,24 @@
     flattened_rows = tokens[0].reshape(row_count, D).astype(jnp.float32)
     standard, inverse_dev = layer_norm(flattened_rows)
     normed = (standard * norm_gain).astype(jnp.bfloat16)
-    full_qkv = lax.all_gather(query_key_value_weight, "fsdp", axis=0, tiled=True)
+    full_qkv, full_out, full_head = gather_weights(query_key_value_weight, out_weight, head_weight)
     projected = jnp.dot(normed, full_qkv, preferred_element_type=jnp.float32).astype(jnp.bfloat16)
     queries = projected[:, :INNER]
     pairs_local = projected[:, INNER:]
     margin_pairs = with_halo(
-        pairs_local.reshape(lat_rows, lon_cols, 2 * INNER), (("tile", 1),), MARGIN
+        pairs_local.reshape(lat_rows, lon_cols, 2 * INNER), ((TILE, 1),), MARGIN
     )
     keys_values = margin_pairs.reshape(lat_rows * (lon_cols + 2 * MARGIN), 2 * INNER)
     attended, softmax_out = attend_forward(queries, keys_values)
-    full_out = lax.all_gather(out_weight, "fsdp", axis=0, tiled=True)
     mixed_out = jnp.dot(attended, full_out, preferred_element_type=jnp.float32)
     hidden = (flattened_rows + mixed_out).astype(jnp.bfloat16)
-    full_head = lax.all_gather(head_weight, "fsdp", axis=0, tiled=True)
     head_out = jnp.dot(hidden, full_head, preferred_element_type=jnp.float32)
     fine_head = (
         head_out.reshape(lat_rows, lon_cols, VARS, 4, 4)
         .transpose(2, 0, 3, 1, 4)
         .reshape(VARS, 4 * lat_rows, 4 * lon_cols)
     )
-    coarse_padded_grid = with_halo(coarse[0], (("tile", 2),), 1)
+    coarse_padded_grid = with_halo(coarse[0], ((TILE, 2),), 1)
     lat_lower, lat_upper_weight = interp_weights(jnp.arange(4 * lat_rows, dtype=jnp.int32))
     latitude_matrix = build_matrix(
         jnp.clip(lat_lower, 0, lat_rows - 1),
@@ -177,16 +218,15 @@
     head_term = lax.dot_general(
         hidden, grad_rows, (((0,), (0,)), ((), ())), preferred_element_type=jnp.float32
     )
-    head_block = lax.psum_scatter(head_term, "fsdp", scatter_dimension=0, tiled=True)
-    grad_head = lax.psum(head_block, ("dp", "tile"))
+    grad_head = reduce_head(head_term)
     grad_hidden = contract_last(grad_rows, full_head)
     grad_attended = contract_last(grad_hidden.astype(jnp.bfloat16), full_out).astype(jnp.bfloat16)
     grad_queries, pair_gradient_rows = attend_backward(
         softmax_out, queries, keys_values, grad_attended
     )
     pair_gradient_rows = pair_gradient_rows.reshape(lat_rows, lon_cols + 2 * MARGIN, 2 * INNER)
-    from_left = from_behind(pair_gradient_rows[:, lon_cols + MARGIN :], "tile", 1)
-    from_right = from_behind(pair_gradient_rows[:, :MARGIN], "tile", -1)
+    from_left = from_behind(pair_gradient_rows[:, lon_cols + MARGIN :], TILE, 1)
+    from_right = from_behind(pair_gradient_rows[:, :MARGIN], TILE, -1)
     own_cells = pair_gradient_rows[:, MARGIN : MARGIN + lon_cols]
     own_cells = own_cells + jnp.pad(from_left, ((0, 0), (0, lon_cols - MARGIN), (0, 0)))
     own_cells = own_cells + jnp.pad(from_right, ((0, 0), (lon_cols - MARGIN, 0), (0, 0)))
@@ -200,23 +240,21 @@
 
 
 def solution(mesh):
+    fine_mesh = Mesh(mesh.devices.reshape(2, ZS, CORES, YS, XS), ("dp", "z", "c", "y", "x"))
+    samples = ("dp", "z", "c")
     placed = (
-        P(("dp", "fsdp"), None, "tile", None),
+        P(samples, None, TILE, None),
         P(),
-        P("fsdp", None),
-        P("fsdp", None),
-        P("fsdp", None),
-        P(("dp", "fsdp"), None, None, "tile"),
-        P(("dp", "fsdp"), None, None, "tile"),
+        P(FSDP, None),
+        P(FSDP, None),
+        P(FSDP, None),
+        P(samples, None, None, TILE),
+        P(samples, None, None, TILE),
     )
     return jax.shard_map(
         shards,
-        mesh=mesh,
+        mesh=fine_mesh,
         in_specs=placed,
-        out_specs=(
-            P(("dp", "fsdp"), None, None, "tile"),
-            P(("dp", "fsdp"), None, "tile", None),
-            P("fsdp", None),
-        ),
+        out_specs=(P(samples, None, None, TILE), P(samples, None, TILE, None), P(FSDP, None)),
         check_vma=False,
     )

time: 945 us -> 270 us (0.29)
  the two profiles are of different devices: /device:TPU:2 before, /device:TPU:32 now
where the time goes in v1:
time: 270 us; the launch traced here: 269 us
  waiting for transfers between devices  95.1 us (35%)
  local copies, waits for them, and re-layouts  67.9 us (25%)
  starting transfers between devices  45.3 us (17%)
  matrix products  33.3 us (12%)
  between operations  14.6 us (5%)
  other arithmetic  12.4 us (5%)
    all_gather x1, waiting for transfers between devices, gather_weights(): full = lax.all_gather(packed, ('dp',) + FSDP, axis=0, tiled=True)  70.3 us
    ppermute x2, starting transfers between devices, with_halo(): after = lax.ppermute(leading, axis, down)  11.7 us
    dot_general x3, matrix products, contract_last(): lax.dot_general(left_side, right_side, (((1,), (1,)), ((), ())), preferre...  10.5 us
    ppermute x2, starting transfers between devices, from_behind(): return lax.ppermute(value, axis, pairs)  9.37 us
    all_to_all x1, waiting for transfers between devices, reduce_head(): pieces = lax.all_to_all(pieces, TILE, 0, 0, tiled=True)  9.29 us
    unnamed x61, local copies, waits for them, and re-layouts  9.08 us
    all_to_all x1, waiting for transfers between devices, reduce_head(): both = lax.all_to_all(both, ('dp', 'z'), 0, 0, tiled=True)  8.76 us
    all_to_all x1, starting transfers between devices, reduce_head(): both = lax.all_to_all(both, ('dp', 'z'), 0, 0, tiled=True)  7.69 us
  transfers between devices with their start and end apart: 11, of which 5 were waited for; matrix products, arithmetic and copies ran while one was open for 19% of the time, Pallas kernels for 0%

profile of v1, /device:TPU:32, one launch (start us, length us, event | category | flops | bytes accessed | tf_op | source)
XLA Modules:
  0.0 268.6 jit_solution(15269680158934245788)
XLA Ops:
  10.0 3.4 %collective-permute-start.2 = (f32[20,8,1]{2,1,0:T(8,128)S(1)}, f32[20,8,1]{2,1,0:T(8,128)S(1)}, u32[]{:S(2)}, u32[]{:S(2)}) collective-permute-start(f32[20,8,1]{2,1,0:T(8,128)S(1)} %get-tuple-element.17), channel_id=1, source_target_pairs={{0,1},{1,2},{2,3},{3,4},{4,5},{5,6},{6,7},{7,8},{8,9},{9,10},{10,1... | collective-permute-start | bytes 1928 | tf_op jit(solution)/shard_map/ppermute | solution.py:26
  13.4 5.8 %collective-permute-start.3 = (f32[20,8,1]{2,1,0:T(8,128)S(1)}, f32[20,8,1]{2,1,0:T(8,128)S(1)}, u32[]{:S(2)}, u32[]{:S(2)}) collective-permute-start(f32[20,8,1]{2,1,0:T(8,128)S(1)} %get-tuple-element.18), channel_id=1, source_target_pairs={{1,0},{2,1},{3,2},{4,3},{5,4},{6,5},{7,6},{8,7},{9,8},{10,9},{11,1... | collective-permute-start | bytes 1928 | tf_op jit(solution)/shard_map/ppermute | solution.py:27
  27.0 70.3 %all-gather.2.cloned.1.call-done = bf16[3072,1696]{1,0:T(8,128)(2,1)} async-done(((bf16[96,1696]{1,0:T(8,128)(2,1)}), bf16[3072,1696]{1,0:T(8,128)(2,1)}) %all-gather.2.cloned.1.call-update) | async-done | bytes 10420240 | tf_op jit(solution)/shard_map/all_gather | solution.py:145
  101.9 3.7 %slice_bitcast_fusion.1 = (bf16[1536,1152]{1,0:T(8,128)(2,1)S(1)}, bf16[1536,1152]{1,0:T(8,128)(2,1)S(1)}) fusion(bf16[2,1536,1696]{2,1,0:T(8,128)(2,1)} %bitcast.108), kind=kLoop, calls=%fused_computation.6 | loop fusion | bytes 14155776 | tf_op jit(solution)/shard_map/squeeze | solution.py:147
  105.6 3.8 %fusion.3 = bf16[256,2304]{1,0:T(8,128)(2,1)S(1)} fusion(bf16[256,1536]{1,0:T(8,128)(2,1)S(1)} %multiply_convert_fusion.1, bf16[1536,1152]{1,0:T(8,128)(2,1)S(1)} %get-tuple-element.8, bf16[1536,1152]{1,0:T(8,128)(2,1)S(1)} %get-tuple-element.7), kind=kOutput, calls=%fused_computation.4 | convolution fusion | flops 1826684928 | bytes 9043968 | tf_op jit(solution)/shard_map/dot_general | solution.py:178
  111.1 3.7 %copy.76 = bf16[16,48,2,2,384]{4,3,2,1,0:T(2,128)(2,1)} copy(bf16[16,48,2,2,384]{4,1,3,0,2:T(8,128)(2,1)S(1)} %bitcast.109) | data formatting | bytes 4718592 | tf_op jit(solution)/shard_map/transpose | solution.py:149
  114.8 5.3 %reshape.212 = bf16[768,1536]{1,0:T(8,128)(2,1)S(1)} reshape(bf16[16,48,2,2,384]{4,3,2,1,0:T(2,128)(2,1)} %copy.76) | data formatting | bytes 4718592 | tf_op jit(solution)/shard_map/reshape | solution.py:149
  123.1 3.4 %collective-permute-start = (bf16[8,8,1536]{2,1,0:T(8,128)(2,1)}, bf16[8,8,1536]{2,1,0:T(8,128)(2,1)}, u32[]{:S(2)}, u32[]{:S(2)}) collective-permute-start(bf16[8,8,1536]{2,1,0:T(8,128)(2,1)} %get-tuple-element.13), channel_id=1, source_target_pairs={{0,1},{1,2},{2,3},{3,4},{4,5},{5,6},{6,7},{7,8},{8,9},{9,10},{10,1... | collective-permute-start | bytes 589832 | tf_op jit(solution)/shard_map/ppermute | solution.py:26
  126.4 6.0 %collective-permute-start.1 = (bf16[8,8,1536]{2,1,0:T(8,128)(2,1)}, bf16[8,8,1536]{2,1,0:T(8,128)(2,1)}, u32[]{:S(2)}, u32[]{:S(2)}) collective-permute-start(bf16[8,8,1536]{2,1,0:T(8,128)(2,1)} %get-tuple-element.14), channel_id=1, source_target_pairs={{1,0},{2,1},{3,2},{4,3},{5,4},{6,5},{7,6},{8,7},{9,8},{10,9},{11,1... | collective-permute-start | bytes 589832 | tf_op jit(solution)/shard_map/ppermute | solution.py:27
  145.9 3.9 %fusion.68 = (f32[8,256]{1,0:T(8,128)S(1)}, f32[8,256,384]{2,1,0:T(8,128)}) fusion(bf16[256,8,96]{0,2,1:T(8,128)(2,1)S(1)} %bitcast.117, bf16[384,8,96]{0,2,1:T(8,128)(2,1)} %bitcast.111), kind=kOutput, calls=%fused_computation.133 | convolution fusion | flops 153354624 | bytes 4136960 | tf_op jit(solution)/shard_map/sub | solution.py:65
  149.8 2.9 %convolution_convert_fusion.1 = bf16[8,96,256]{2,1,0:T(8,128)(2,1)S(1)} fusion(bf16[384,8,96]{0,2,1:T(8,128)(2,1)} %bitcast.127, f32[8,256,384]{2,1,0:T(8,128)} %get-tuple-element.20, f32[8,256]{1,0:T(8,128)S(1)} %get-tuple-element.19), kind=kOutput, calls=%fused_computation.33 | convolution fusion | flops 152764416 | bytes 4136960 | tf_op jit(solution)/shard_map/hqk,khd->qhd/dot_general | solution.py:68
  170.7 3.1 %copy.77 = f32[8,32,20,4,4]{2,4,1,3,0:T(4,128)} copy(f32[8,32,20,4,4]{1,0,4,3,2:T(8,128)} %reshape.213) | data formatting | bytes 655360 | tf_op jit(solution)/shard_map/reshape | solution.py:190
  173.7 3.0 %copy.78 = f32[20,32,128]{2,1,0:T(8,128)} copy(f32[20,32,128]{0,2,1:T(8,128)} %bitcast.110) | data formatting | bytes 655360 | tf_op jit(solution)/shard_map/reshape | solution.py:192
  176.7 3.0 %copy.83 = f32[384,8,96]{2,1,0:T(8,128)} copy(f32[384,8,96]{0,2,1:T(8,128)} %convolution_bitcast_fusion.1) | data formatting | bytes 2359296 | tf_op jit(solution)/shard_map/hqk,qhd->khd/transpose | solution.py:83
  183.5 3.0 %copy.82 = f32[384,8,96]{2,1,0:T(8,128)} copy(f32[384,8,96]{0,2,1:T(8,128)} %fusion.13) | data formatting | bytes 2359296 | tf_op jit(solution)/shard_map/mul | solution.py:96
  195.3 7.5 %collective-permute-start.5 = (f32[8,8,1536]{2,1,0:T(8,128)}, f32[8,8,1536]{2,1,0:T(8,128)}, u32[]{:S(2)}, u32[]{:S(2)}) collective-permute-start(f32[8,8,1536]{2,1,0:T(8,128)} %get-tuple-element.10), channel_id=1, source_target_pairs={{0,15},{1,0},{2,1},{3,2},{4,3},{5,4},{6,5},{7,6},{8,7},{9,8},{10,9... | collective-permute-start | bytes 1179656 | tf_op jit(solution)/shard_map/ppermute | solution.py:35
  206.4 4.2 %all-to-all-start = ((bf16[16,8,6,320]{3,1,2,0:T(8,128)(2,1)}), bf16[16,8,6,320]{3,1,2,0:T(8,128)(2,1)}, u32[]{:S(2)}, u32[]{:S(2)}) async-start(bf16[16,8,6,320]{3,1,2,0:T(8,128)(2,1)} %bitcast.121), calls=%async_computation | async-start | bytes 1179648 | tf_op jit(solution)/shard_map/all_to_all | solution.py:161
  214.0 9.3 %all-to-all-done = bf16[16,8,6,320]{3,1,2,0:T(8,128)(2,1)} async-done(((bf16[16,8,6,320]{3,1,2,0:T(8,128)(2,1)}), bf16[16,8,6,320]{3,1,2,0:T(8,128)(2,1)}, u32[]{:S(2)}, u32[]{:S(2)}) %all-to-all-start) | async-done | bytes 491552 | tf_op jit(solution)/shard_map/all_to_all | solution.py:161
  225.2 7.7 %all-to-all-start.1 = ((f32[16,6,320]{2,1,0:T(8,128)}), f32[16,6,320]{2,1,0:T(8,128)S(1)}, u32[]{:S(2)}, u32[]{:S(2)}) async-start(f32[16,6,320]{2,1,0:T(8,128)} %bitcast.39), calls=%async_computation.1 | async-start | bytes 393216 | tf_op jit(solution)/shard_map/all_to_all | solution.py:164
  232.9 6.8 %fusion.63 = (f32[256]{0:T(256)S(1)}, f32[256]{0:T(256)S(1)}, f32[256,1536]{1,0:T(8,128)}) fusion(f32[256]{0:T(256)S(1)} %rsqrt.12, f32[256]{0:T(256)S(1)} %div.51, bf16[1,8,32,1536]{3,2,1,0:T(8,128)(2,1)S(1)} %copy-done.2, f32[1536]{0:T(1024)S(1)} %copy-done.24, bf16[1536,1152]{1,0:T(8,128)(2,1)} %copy-done.11, bf16[1536,1152]{1,0:T(8,128)(2,1)} %copy-done.10, ...), kind=kOutput, calls=%fused_computation.128 | convolution fusion | flops 1831206400 | bytes 10627072 | tf_op jit(solution)/shard_map/dot_general | solution.py:123
  239.7 8.8 %all-to-all-done.1 = f32[16,6,320]{2,1,0:T(8,128)S(1)} async-done(((f32[16,6,320]{2,1,0:T(8,128)}), f32[16,6,320]{2,1,0:T(8,128)S(1)}, u32[]{:S(2)}, u32[]{:S(2)}) %all-to-all-start.1) | async-done | bytes 122912 | tf_op jit(solution)/shard_map/all_to_all | solution.py:164
  249.2 3.5 %all-to-all-start.2 = ((f32[16,6,320]{2,1,0:T(8,128)}), f32[16,6,320]{2,1,0:T(8,128)S(1)}, u32[]{:S(2)}, u32[]{:S(2)}) async-start(f32[16,6,320]{2,1,0:T(8,128)} %broadcast_in_dim.80), calls=%async_computation.2 | async-start | bytes 393216 | tf_op jit(solution)/shard_map/all_to_all | solution.py:167
  252.8 2.9 %add_convert_fusion = bf16[256,1536]{1,0:T(8,128)(2,1)} fusion(f32[256,1536]{1,0:T(8,128)S(1)} %copy-done.4, f32[256,1536]{1,0:T(8,128)} %get-tuple-element.23, bf16[1,8,32,1536]{3,2,1,0:T(8,128)(2,1)S(1)} %copy-done.2, f32[256]{0:T(256)S(1)} %get-tuple-element.32, f32[256]{0:T(256)S(1)} %get-tuple-element.33, f32[256]{0:T(256)S(1)} %rsqrt.12, f32[256]{0:T(256)S(1)} %div.51), kind=kLoop, calls=%fused_computation.21 | loop fusion | flops 3538944 | bytes 4722688 | tf_op jit(solution)/shard_map/convert_element_type | solution.py:238
  255.7 5.4 %all-to-all-done.2 = f32[16,6,320]{2,1,0:T(8,128)S(1)} async-done(((f32[16,6,320]{2,1,0:T(8,128)}), f32[16,6,320]{2,1,0:T(8,128)S(1)}, u32[]{:S(2)}, u32[]{:S(2)}) %all-to-all-start.2) | async-done | bytes 122912 | tf_op jit(solution)/shard_map/all_to_all | solution.py:167
  (132 shorter events, 73.7 us)
Async XLA Ops:
  7.2 12.0 %copy-start.22 = (f32[1,20,32,128]{3,2,1,0:T(8,128)S(1)}, f32[1,20,32,128]{3,2,1,0:T(8,128)}, u32[]{:S(2)}) copy-start(f32[1,20,32,128]{3,2,1,0:T(8,128)} %param.13) | copy-start | bytes 983044
  7.2 90.1 %all-gather.2.cloned.1.call-start = ((), (), s32[]{:S(2)}) async-start(), calls=%async_computation.3 | async-start | bytes 11354112 | tf_op jit(solution)/shard_map/all_gather | solution.py:145
  10.0 15.7 %collective-permute-start.2 = (f32[20,8,1]{2,1,0:T(8,128)S(1)}, f32[20,8,1]{2,1,0:T(8,128)S(1)}, u32[]{:S(2)}, u32[]{:S(2)}) collective-permute-start(f32[20,8,1]{2,1,0:T(8,128)S(1)} %get-tuple-element.17), channel_id=1, source_target_pairs={{0,1},{1,2},{2,3},{3,4},{4,5},{5,6},{6,7},{7,8},{8,9},{9,10},{10,1... | collective-permute-start | bytes 1928 | tf_op jit(solution)/shard_map/ppermute | solution.py:26
  13.4 12.3 %collective-permute-start.3 = (f32[20,8,1]{2,1,0:T(8,128)S(1)}, f32[20,8,1]{2,1,0:T(8,128)S(1)}, u32[]{:S(2)}, u32[]{:S(2)}) collective-permute-start(f32[20,8,1]{2,1,0:T(8,128)S(1)} %get-tuple-element.18), channel_id=1, source_target_pairs={{1,0},{2,1},{3,2},{4,3},{5,4},{6,5},{7,6},{8,7},{9,8},{10,9},{11,1... | collective-permute-start | bytes 1928 | tf_op jit(solution)/shard_map/ppermute | solution.py:27
  21.3 4.2 %copy-start.23 = (f32[1536]{0:T(1024)S(1)}, f32[1536]{0:T(1024)}, u32[]{:S(2)}) copy-start(f32[1536]{0:T(1024)} %param.8) | copy-start | bytes 18436
  105.6 3.8 %copy-start.10 = (bf16[1536,1152]{1,0:T(8,128)(2,1)}, bf16[1536,1152]{1,0:T(8,128)(2,1)S(1)}, u32[]{:S(2)}) copy-start(bf16[1536,1152]{1,0:T(8,128)(2,1)S(1)} %get-tuple-element.7) | copy-start | bytes 10616836
  123.1 16.1 %collective-permute-start = (bf16[8,8,1536]{2,1,0:T(8,128)(2,1)}, bf16[8,8,1536]{2,1,0:T(8,128)(2,1)}, u32[]{:S(2)}, u32[]{:S(2)}) collective-permute-start(bf16[8,8,1536]{2,1,0:T(8,128)(2,1)} %get-tuple-element.13), channel_id=1, source_target_pairs={{0,1},{1,2},{2,3},{3,4},{4,5},{5,6},{6,7},{7,8},{8,9},{9,10},{10,1... | collective-permute-start | bytes 589832 | tf_op jit(solution)/shard_map/ppermute | solution.py:26
  126.4 12.7 %collective-permute-start.1 = (bf16[8,8,1536]{2,1,0:T(8,128)(2,1)}, bf16[8,8,1536]{2,1,0:T(8,128)(2,1)}, u32[]{:S(2)}, u32[]{:S(2)}) collective-permute-start(bf16[8,8,1536]{2,1,0:T(8,128)(2,1)} %get-tuple-element.14), channel_id=1, source_target_pairs={{1,0},{2,1},{3,2},{4,3},{5,4},{6,5},{7,6},{8,7},{9,8},{10,9},{11,1... | collective-permute-start | bytes 589832 | tf_op jit(solution)/shard_map/ppermute | solution.py:27
  166.3 37.7 %collective-permute-start.6 = (f32[8,96,320]{2,1,0:T(8,128)}, f32[8,96,320]{2,1,0:T(8,128)}, u32[]{:S(2)}, u32[]{:S(2)}) collective-permute-start(f32[8,96,320]{2,1,0:T(8,128)} %dynamic-slice_bitcast_fusion), channel_id=1, source_target_pairs={{0,16},{16,0},{1,17},{17,1},{2,18},{18,2},{3,19},{19,3},{4,20},{20... | collective-permute-start | bytes 2949128 | tf_op jit(solution)/shard_map/ppermute | solution.py:159
  190.8 12.0 %copy-start.16 = (f32[20,32,128]{2,1,0:T(8,128)S(1)}, f32[20,32,128]{2,1,0:T(8,128)}, u32[]{:S(2)}) copy-start(f32[20,32,128]{2,1,0:T(8,128)} %copy.78) | copy-start | bytes 983044
  190.8 12.0 %copy-start.17 = (f32[20,32,34]{2,1,0:T(8,128)S(1)}, f32[20,32,34]{2,1,0:T(8,128)}, u32[]{:S(2)}) copy-start(f32[20,32,34]{2,1,0:T(8,128)} %convolution_bitcast_fusion.2) | copy-start | bytes 261124
  190.8 12.0 %copy-start.25 = (s32[128]{0:T(128)S(1)}, s32[128]{0:T(128)}, u32[]{:S(2)}) copy-start(s32[128]{0:T(128)} %get-tuple-element.30) | copy-start | bytes 1540
  190.8 12.0 %copy-start.26 = (s32[128]{0:T(128)S(1)}, s32[128]{0:T(128)}, u32[]{:S(2)}) copy-start(s32[128]{0:T(128)} %get-tuple-element.31) | copy-start | bytes 1540
  190.8 12.1 %copy-start.27 = (f32[128]{0:T(128)S(1)}, f32[128]{0:T(128)}, u32[]{:S(2)}) copy-start(f32[128]{0:T(128)} %get-tuple-element.24) | copy-start | bytes 1540
  190.8 12.0 %copy-start.28 = (f32[128]{0:T(128)S(1)}, f32[128]{0:T(128)}, u32[]{:S(2)}) copy-start(f32[128]{0:T(128)} %get-tuple-element.25) | copy-start | bytes 1540
  193.4 17.3 %collective-permute-start.4 = (f32[8,8,1536]{2,1,0:T(8,128)}, f32[8,8,1536]{2,1,0:T(8,128)S(1)}, u32[]{:S(2)}, u32[]{:S(2)}) collective-permute-start(f32[8,8,1536]{2,1,0:T(8,128)} %get-tuple-element.9), channel_id=1, source_target_pairs={{0,1},{1,2},{2,3},{3,4},{4,5},{5,6},{6,7},{7,8},{8,9},{9,10},{10,1... | collective-permute-start | bytes 1179656 | tf_op jit(solution)/shard_map/ppermute | solution.py:35
  195.3 16.7 %collective-permute-start.5 = (f32[8,8,1536]{2,1,0:T(8,128)}, f32[8,8,1536]{2,1,0:T(8,128)}, u32[]{:S(2)}, u32[]{:S(2)}) collective-permute-start(f32[8,8,1536]{2,1,0:T(8,128)} %get-tuple-element.10), channel_id=1, source_target_pairs={{0,15},{1,0},{2,1},{3,2},{4,3},{5,4},{6,5},{7,6},{8,7},{9,8},{10,9... | collective-permute-start | bytes 1179656 | tf_op jit(solution)/shard_map/ppermute | solution.py:35
  205.4 6.6 %copy-start.7 = (f32[8,48,1536]{2,1,0:T(8,128)S(1)}, f32[8,48,1536]{2,1,0:T(8,128)}, u32[]{:S(2)}) copy-start(f32[8,48,1536]{2,1,0:T(8,128)} %copy-done.6) | copy-start | bytes 7077892
  206.4 16.9 %all-to-all-start = ((bf16[16,8,6,320]{3,1,2,0:T(8,128)(2,1)}), bf16[16,8,6,320]{3,1,2,0:T(8,128)(2,1)}, u32[]{:S(2)}, u32[]{:S(2)}) async-start(bf16[16,8,6,320]{3,1,2,0:T(8,128)(2,1)} %bitcast.121), calls=%async_computation | async-start | bytes 1179648 | tf_op jit(solution)/shard_map/all_to_all | solution.py:161
  210.7 22.2 %copy-start.24 = (f32[1536]{0:T(1024)S(1)}, f32[1536]{0:T(1024)}, u32[]{:S(2)}) copy-start(f32[1536]{0:T(1024)} %param.8) | copy-start | bytes 18436
  225.2 23.3 %all-to-all-start.1 = ((f32[16,6,320]{2,1,0:T(8,128)}), f32[16,6,320]{2,1,0:T(8,128)S(1)}, u32[]{:S(2)}, u32[]{:S(2)}) async-start(f32[16,6,320]{2,1,0:T(8,128)} %bitcast.39), calls=%async_computation.1 | async-start | bytes 393216 | tf_op jit(solution)/shard_map/all_to_all | solution.py:164
  232.9 19.9 %copy-start.4 = (f32[256,1536]{1,0:T(8,128)S(1)}, f32[256,1536]{1,0:T(8,128)}, u32[]{:S(2)}) copy-start(f32[256,1536]{1,0:T(8,128)} %copy-done.3) | copy-start | bytes 4718596
  249.2 11.8 %all-to-all-start.2 = ((f32[16,6,320]{2,1,0:T(8,128)}), f32[16,6,320]{2,1,0:T(8,128)S(1)}, u32[]{:S(2)}, u32[]{:S(2)}) async-start(f32[16,6,320]{2,1,0:T(8,128)} %broadcast_in_dim.80), calls=%async_computation.2 | async-start | bytes 393216 | tf_op jit(solution)/shard_map/all_to_all | solution.py:167
  252.8 9.0 %copy-start.1 = (bf16[96,2304]{1,0:T(8,128)(2,1)S(1)}, bf16[96,2304]{1,0:T(8,128)(2,1)}, u32[]{:S(2)}) copy-start(bf16[96,2304]{1,0:T(8,128)(2,1)} %param.9) | copy-start | bytes 1327108
  (16 other events, 39.6 us)
Sparse Core Ops, SparseCore 0:
  10.7 86.5 all-gather.1

commit v2 on v1

v2 whole, which is shorter than its diff:
```python
import functools
import jax
import jax.numpy as jnp
from jax import lax
from jax.experimental import pallas as pl
from jax.experimental.pallas import tpu as pltpu
from jax.sharding import Mesh
from jax.sharding import PartitionSpec as P

D = 1536
HEADS = 8
HEAD_DIM = 96
VARS = 20
MARGIN = 8
LAT = 8
LON_DEV = 32
INNER = 768
HEAD_OUT = 320
ROWS = 256
EDGE = 64
GROUP = 384
PAIR = 2 * INNER
ZS = 8
CORES = 2
YS = 4
XS = 4
TILES = 16
FSDP = ("z", "c")
TILE = ("y", "x")
HALF_QKV = 1152
HALF_OUT = 768
PACKED = 1696
PHASES = 4
CHANNELS = 80
LANES = 128
PADDED = PHASES * LANES
EPSILON = 1e-05
SCALE = HEAD_DIM ** (-0.5)
F32 = jnp.float32
BF16 = jnp.bfloat16
WHOLE = pl.BlockSpec(memory_space=pltpu.VMEM)


def dot(left, right):
    return lax.dot_general(left, right, (((1,), (0,)), ((), ())), preferred_element_type=F32)


def dot_last(left, right):
    return lax.dot_general(left, right, (((1,), (1,)), ((), ())), preferred_element_type=F32)


def dot_first(left, right):
    return lax.dot_general(left, right, (((0,), (0,)), ((), ())), preferred_element_type=F32)


def spread_matrix():
    row = lax.broadcasted_iota(jnp.int32, (LANES, LANES), 0)
    lane = lax.broadcasted_iota(jnp.int32, (LANES, LANES), 1)
    target = (row % LON_DEV) * PHASES + row // LON_DEV
    return jnp.where(lane == target, 1.0, 0.0).astype(BF16)


def prepare_kernel(tokens_ref, gain_ref, fine_ref, normed_ref, rows_ref):
    values = tokens_ref[...].astype(F32)
    average = jnp.mean(values, axis=-1, keepdims=True)
    centred = values - average
    variance = jnp.mean(centred * centred, axis=-1, keepdims=True)
    standard = centred * lax.rsqrt(variance + EPSILON)
    normed_ref[...] = (standard * gain_ref[...]).astype(BF16)
    select = spread_matrix()
    empty = jnp.zeros((LANES - CHANNELS, LANES), BF16)
    for lat in range(LAT):
        block = fine_ref[:, PHASES * lat : PHASES * (lat + 1), :].reshape(CHANNELS, LANES)
        block = jnp.concatenate([block.astype(BF16), empty], axis=0)
        picked = dot_last(select, block).astype(BF16)
        for phase in range(PHASES):
            rows_ref[lat * LON_DEV : (lat + 1) * LON_DEV, phase * LANES : (phase + 1) * LANES] = picked[
                phase * LON_DEV : (phase + 1) * LON_DEV
            ]


def prepare(tokens, gain, grad_fine):
    return pl.pallas_call(
        prepare_kernel,
        out_shape=(
            jax.ShapeDtypeStruct((ROWS, D), BF16),
            jax.ShapeDtypeStruct((ROWS, PADDED), BF16),
        ),
        in_specs=[WHOLE, WHOLE, WHOLE],
        out_specs=(WHOLE, WHOLE),
        name="prepare",
    )(tokens, gain, grad_fine)


def project_kernel(normed_ref, weight_ref, out_ref):
    out_ref[...] = dot(normed_ref[...], weight_ref[0]).astype(BF16)


def project(normed, full, first, count):
    return pl.pallas_call(
        project_kernel,
        out_shape=jax.ShapeDtypeStruct((ROWS, count * GROUP), BF16),
        grid=(count,),
        in_specs=[
            pl.BlockSpec((ROWS, D), lambda n: (0, 0)),
            pl.BlockSpec((1, D, GROUP), lambda n: ((n + first) // 3, 0, (n + first) % 3)),
        ],
        out_specs=pl.BlockSpec((ROWS, GROUP), lambda n: (0, n)),
        name="project",
    )(normed, full)


def out_quarter(weight_ref, part):
    block = weight_ref[0].reshape(16, 2, 48, GROUP)[:, part]
    return block.reshape(INNER, GROUP)


def hidden_grad_kernel(rows_ref, head_ref, low_out_ref, up_out_ref, hidden_ref, attended_ref):
    rows = rows_ref[...]
    grad_hidden = dot_last(rows[:, :256], head_ref[0]) + dot_last(rows[:, 256:], head_ref[1])
    hidden_ref[...] = grad_hidden
    low = grad_hidden.astype(BF16)
    total = None
    for quarter in range(4):
        weight = out_quarter(low_out_ref if quarter < 2 else up_out_ref, quarter % 2)
        term = dot_last(low[:, quarter * GROUP : (quarter + 1) * GROUP], weight)
        total = term if total is None else total + term
    attended_ref[...] = total.astype(BF16)


def out_specs_of(count):
    low = pl.BlockSpec((1, D, GROUP), lambda n: (0, 0, 3))
    up = pl.BlockSpec((1, D, GROUP), lambda n: (1, 0, 3))
    return [low, up][:count]


def whole_block(shape):
    return pl.BlockSpec(shape, lambda n: (0,) * len(shape))


def hidden_grad(rows, head, full):
    return pl.pallas_call(
        hidden_grad_kernel,
        out_shape=(
            jax.ShapeDtypeStruct((ROWS, D), F32),
            jax.ShapeDtypeStruct((ROWS, INNER), BF16),
        ),
        grid=(1,),
        in_specs=[whole_block((ROWS, PADDED)), whole_block((2, D, 256))] + out_specs_of(2),
        out_specs=(whole_block((ROWS, D)), whole_block((ROWS, INNER))),
        name="hidden_grad",
    )(rows, head, full, full)


def head_window(head):
    first = head * HEAD_DIM // LANES * LANES
    last = -(-(head + 1) * HEAD_DIM // LANES) * LANES
    lane = lax.broadcasted_iota(jnp.int32, (1, last - first), 1) + first
    inside = (lane >= head * HEAD_DIM) & (lane < (head + 1) * HEAD_DIM)
    return first, last, inside


def masked(values, inside):
    return jnp.where(inside, values, jnp.zeros_like(values))


def softmax_of(query, key):
    scores = dot_last(query, key) * SCALE
    biggest = jnp.max(scores, axis=-1, keepdims=True)
    exponent = jnp.exp(scores - biggest)
    return exponent / jnp.sum(exponent, axis=-1, keepdims=True)


def joined(own_ref, left_ref, right_ref):
    return jnp.concatenate([own_ref[...], left_ref[...], right_ref[...]], axis=0)


def forward_kernel(q_ref, k_ref, v_ref, kl_ref, vl_ref, kr_ref, vr_ref, out_ref):
    queries = q_ref[...]
    keys = joined(k_ref, kl_ref, kr_ref)
    values = joined(v_ref, vl_ref, vr_ref)
    parts = [None, None, None]
    for head in range(4):
        first, last, inside = head_window(head)
        softmax = softmax_of(masked(queries[:, first:last], inside), keys[:, first:last])
        result = dot(softmax.astype(BF16), masked(values[:, first:last], inside))
        for tile in range(first // LANES, last // LANES):
            piece = result[:, tile * LANES - first : (tile + 1) * LANES - first]
            parts[tile] = piece if parts[tile] is None else parts[tile] + piece
    for tile in range(3):
        out_ref[:, tile * LANES : (tile + 1) * LANES] = parts[tile].astype(BF16)


def attention_specs():
    def spec(rows, offset):
        return pl.BlockSpec((rows, GROUP), lambda n: (0, n + offset))

    return [spec(ROWS, 0), spec(ROWS, 0), spec(ROWS, 2), spec(EDGE, 0), spec(EDGE, 2), spec(EDGE, 0), spec(EDGE, 2)]


def attend_forward(queries, pairs, left, right):
    return pl.pallas_call(
        forward_kernel,
        out_shape=jax.ShapeDtypeStruct((ROWS, INNER), BF16),
        grid=(2,),
        in_specs=attention_specs(),
        out_specs=pl.BlockSpec((ROWS, GROUP), lambda n: (0, n)),
        name="attend_forward",
    )(queries, pairs, pairs, left, left, right, right)


def backward_kernel(
    q_ref, k_ref, v_ref, kl_ref, vl_ref, kr_ref, vr_ref, grad_ref,
    dq_ref, dk_ref, dv_ref, dkl_ref, dvl_ref, dkr_ref, dvr_ref,
):
    queries = q_ref[...]
    grads = grad_ref[...]
    keys = joined(k_ref, kl_ref, kr_ref)
    values = joined(v_ref, vl_ref, vr_ref)
    sums = [[None, None, None] for _ in range(3)]
    for head in range(4):
        first, last, inside = head_window(head)
        query = masked(queries[:, first:last], inside)
        grad = masked(grads[:, first:last], inside)
        softmax = softmax_of(query, keys[:, first:last])
        grad_weights = dot_last(grad, values[:, first:last])
        weighted = jnp.sum(softmax * grad_weights, axis=-1, keepdims=True)
        grad_scores = (softmax * (grad_weights - weighted)).astype(BF16)
        results = (
            dot(grad_scores, masked(keys[:, first:last], inside)),
            dot_first(grad_scores, query),
            dot_first(softmax.astype(BF16), grad),
        )
        for kept, result in zip(sums, results):
            for tile in range(first // LANES, last // LANES):
                piece = result[:, tile * LANES - first : (tile + 1) * LANES - first]
                kept[tile] = piece if kept[tile] is None else kept[tile] + piece
    for tile in range(3):
        at = slice(tile * LANES, (tile + 1) * LANES)
        dq_ref[:, at] = (sums[0][tile] * SCALE).astype(BF16)
        grad_keys = sums[1][tile] * SCALE
        grad_values = sums[2][tile]
        for grads_of, own, left, right in (
            (grad_keys, dk_ref, dkl_ref, dkr_ref),
            (grad_values, dv_ref, dvl_ref, dvr_ref),
        ):
            own[:, at] = grads_of[:ROWS]
            left[:, at] = grads_of[ROWS : ROWS + EDGE]
            right[:, at] = grads_of[ROWS + EDGE :]


def attend_backward(queries, pairs, left, right, grad_attended):
    def block(rows):
        return pl.BlockSpec((rows, GROUP), lambda n: (0, n))

    def shape(rows, kind):
        return jax.ShapeDtypeStruct((rows, INNER), kind)

    return pl.pallas_call(
        backward_kernel,
        out_shape=(
            shape(ROWS, BF16),
            shape(ROWS, F32),
            shape(ROWS, F32),
            shape(EDGE, F32),
            shape(EDGE, F32),
            shape(EDGE, F32),
            shape(EDGE, F32),
        ),
        grid=(2,),
        in_specs=attention_specs() + [block(ROWS)],
        out_specs=(block(ROWS), block(ROWS), block(ROWS), block(EDGE), block(EDGE), block(EDGE), block(EDGE)),
        name="attend_backward",
    )(queries, pairs, pairs, left, left, right, right, grad_attended)


def hidden_kernel(
    tokens_ref, attended_ref, low_out_ref, up_out_ref, head_ref, rows_ref, residual_ref, fine_ref, pieces_ref
):
    attended = attended_ref[...]
    rows = rows_ref[...]
    head_out = [None, None]
    for quarter in range(4):
        weight = out_quarter(low_out_ref if quarter < 2 else up_out_ref, quarter % 2)
        at = slice(quarter * GROUP, (quarter + 1) * GROUP)
        hidden = (tokens_ref[:, at].astype(F32) + dot(attended, weight)).astype(BF16)
        for half in range(2):
            term = dot(hidden, head_ref[half, at, :])
            head_out[half] = term if head_out[half] is None else head_out[half] + term
        products = dot_first(hidden, rows).astype(BF16)
        for fsdp in range(4):
            place = quarter * 4 + fsdp
            for quad in range(4):
                top = fsdp * 96 + quad * 24
                for phase in range(PHASES):
                    pieces_ref[place % 2, quad * 4 + phase, place // 2] = products[
                        top : top + 24, phase * LANES : (phase + 1) * LANES
                    ]
    select = spread_matrix()
    for lat in range(LAT):
        at = slice(lat * LON_DEV, (lat + 1) * LON_DEV)
        stacked = jnp.concatenate(
            [head_out[phase // 2][at, phase % 2 * LANES : (phase % 2 + 1) * LANES] for phase in range(PHASES)],
            axis=0,
        )
        high = stacked.astype(BF16)
        low = (stacked - high.astype(F32)).astype(BF16)
        spread = dot_first(high, select) + dot_first(low, select)
        across = slice(PHASES * lat, PHASES * (lat + 1))
        fine_ref[:, across, :] = spread[:CHANNELS].reshape(VARS, PHASES, LANES) + residual_ref[:, across, :]


def hidden_and_head(tokens, attended, full, head, rows, residual):
    pieces = (CORES, TILES, ZS, 24, LANES)
    return pl.pallas_call(
        hidden_kernel,
        out_shape=(
            jax.ShapeDtypeStruct((VARS, 4 * LAT, LANES), F32),
            jax.ShapeDtypeStruct(pieces, BF16),
        ),
        grid=(1,),
        in_specs=[whole_block((ROWS, D)), whole_block((ROWS, INNER))]
        + out_specs_of(2)
        + [whole_block((2, D, 256)), whole_block((ROWS, PADDED)), whole_block((VARS, 4 * LAT, LANES))],
        out_specs=(whole_block((VARS, 4 * LAT, LANES)), whole_block(pieces)),
        name="hidden_and_head",
    )(tokens, attended, full, full, head, rows, residual)


def norm_grad_kernel(
    dq_ref, dk_ref, dv_ref, kl_ref, vl_ref, kr_ref, vr_ref, weight_ref, tokens_ref, gain_ref, hidden_ref, out_ref, total
):
    step = pl.program_id(0)

    def add(grad):
        term = dot_last(grad, weight_ref[0])

        @pl.when(step == 0)
        def _():
            total[...] = term

        @pl.when(step > 0)
        def _():
            total[...] += term

    def with_edges(own_ref, left_ref, right_ref):
        own = own_ref[...].reshape(LAT, LON_DEV, GROUP)
        left = left_ref[...].reshape(LAT, MARGIN, GROUP)
        right = right_ref[...].reshape(LAT, MARGIN, GROUP)
        own = jnp.concatenate(
            [own[:, :MARGIN] + left, own[:, MARGIN : LON_DEV - MARGIN], own[:, LON_DEV - MARGIN :] + right], axis=1
        )
        return own.reshape(ROWS, GROUP).astype(BF16)

    @pl.when(step < 2)
    def _():
        add(dq_ref[...])

    @pl.when((step >= 2) & (step < 4))
    def _():
        add(with_edges(dk_ref, kl_ref, kr_ref))

    @pl.when(step >= 4)
    def _():
        add(with_edges(dv_ref, vl_ref, vr_ref))

    @pl.when(step == 5)
    def _():
        values = tokens_ref[...].astype(F32)
        average = jnp.mean(values, axis=-1, keepdims=True)
        centred = values - average
        variance = jnp.mean(centred * centred, axis=-1, keepdims=True)
        inverse_dev = lax.rsqrt(variance + EPSILON)
        standard = centred * inverse_dev
        grad_standard = total[...] * gain_ref[...]
        first_mean = jnp.mean(grad_standard, axis=-1, keepdims=True)
        second_mean = jnp.mean(grad_standard * standard, axis=-1, keepdims=True)
        grad = inverse_dev * (grad_standard - first_mean - standard * second_mean)
        out_ref[...] = (hidden_ref[...] + grad).astype(BF16)


def norm_grad(dq, dk, dv, from_left, from_right, full, tokens, gain, grad_hidden):
    def spec(rows, first, offset):
        return pl.BlockSpec((rows, GROUP), lambda n: (0, jnp.clip(n - first, 0, 1) + offset))

    return pl.pallas_call(
        norm_grad_kernel,
        out_shape=jax.ShapeDtypeStruct((ROWS, D), BF16),
        grid=(6,),
        in_specs=[
            spec(ROWS, 0, 0),
            spec(ROWS, 2, 0),
            spec(ROWS, 4, 0),
            spec(EDGE, 2, 0),
            spec(EDGE, 4, 2),
            spec(EDGE, 2, 0),
            spec(EDGE, 4, 2),
            pl.BlockSpec((1, D, GROUP), lambda n: (n // 3, 0, n % 3)),
            whole_block((ROWS, D)),
            whole_block((1, D)),
            whole_block((ROWS, D)),
        ],
        out_specs=whole_block((ROWS, D)),
        scratch_shapes=[pltpu.VMEM((ROWS, D), F32)],
        name="norm_grad",
    )(dq, dk, dv, from_left, from_left, from_right, from_right, full, tokens, gain, grad_hidden)


def interp_weights(fine_index):
    coarse_cell = fine_index // 4
    phase_index = fine_index % 4
    lower_shift = (phase_index < 2).astype(jnp.int32)
    upper_weight = (2 * phase_index - 3 + 8 * lower_shift).astype(F32) / 8.0
    return (coarse_cell - lower_shift, upper_weight)


def build_matrix(lower_cell, upper_cell, upper_weight, count):
    columns = jnp.arange(count, dtype=jnp.int32)
    lower_part = jnp.where(columns[None, :] == lower_cell[:, None], 1.0 - upper_weight[:, None], 0.0)
    upper_portion = jnp.where(columns[None, :] == upper_cell[:, None], upper_weight[:, None], 0.0)
    return lower_part + upper_portion


def shifted(value, steps):
    return lax.ppermute(value, TILE, [(i, (i + steps) % TILES) for i in range(TILES)])


def residual_of(coarse):
    before = shifted(coarse[:, :, -1:], 1)
    after = shifted(coarse[:, :, :1], -1)
    padded = jnp.concatenate([before, coarse, after], axis=2)
    lat_lower, lat_upper_weight = interp_weights(jnp.arange(4 * LAT, dtype=jnp.int32))
    latitude_matrix = build_matrix(
        jnp.clip(lat_lower, 0, LAT - 1), jnp.clip(lat_lower + 1, 0, LAT - 1), lat_upper_weight, LAT
    )
    lon_lower, lon_upper_weight = interp_weights(jnp.arange(4 * LON_DEV, dtype=jnp.int32))
    lon_matrix = build_matrix(lon_lower + 1, lon_lower + 2, lon_upper_weight, LON_DEV + 2)
    incomplete_grid = jnp.einsum("lj,kji->kli", latitude_matrix, padded, precision=lax.Precision.HIGHEST)
    return jnp.einsum("vrb,cb->vrc", incomplete_grid, lon_matrix, precision=lax.Precision.HIGHEST)


def head_columns():
    target = jnp.arange(PADDED, dtype=jnp.int32)
    phase, channel = target // LANES, target % LANES
    source = jnp.where(channel < CHANNELS, channel * PHASES + phase, -1)
    return (jnp.arange(HEAD_OUT, dtype=jnp.int32)[:, None] == source[None, :]).astype(F32)


def gather_weights(qkv, out_w, head_w):
    half = lax.axis_index("dp")
    qkv_half = lax.dynamic_slice_in_dim(qkv, half * HALF_QKV, HALF_QKV, 1)
    out_half = lax.dynamic_slice_in_dim(out_w, half * HALF_OUT, HALF_OUT, 1)
    out_half = jnp.concatenate([out_half[:, :GROUP], out_half[:, GROUP:]], axis=0)
    head_half = lax.dynamic_slice_in_dim(head_w, half * 160, 160, 1)
    packed = jnp.concatenate([qkv_half, out_half, head_half], axis=1)
    full = lax.all_gather(packed, ("dp",) + FSDP, axis=0, tiled=True)
    return full.reshape(2, D, PACKED)


def head_of(full):
    columns = head_columns().astype(BF16)
    low = full[0, :, 4 * GROUP :]
    up = full[1, :, 4 * GROUP :]
    parts = [
        (dot(low, columns[:160, at : at + 256]) + dot(up, columns[160:, at : at + 256])).astype(BF16)
        for at in (0, 256)
    ]
    return jnp.stack(parts)


def reduce_head(pieces):
    pieces = lax.all_to_all(pieces.reshape(CORES * TILES, ZS, 24, LANES), ("c",) + TILE, 0, 0, tiled=True)
    over_tile = jnp.sum(pieces.astype(F32), axis=0)
    both = jnp.broadcast_to(over_tile[None], (2, ZS, 24, LANES)).reshape(2 * ZS, 24, LANES)
    both = lax.all_to_all(both, ("dp", "z"), 0, 0, tiled=True)
    total = jnp.sum(both, axis=0)
    spread = jnp.broadcast_to(total[None], (TILES, 24, LANES))
    spread = lax.all_to_all(spread, TILE, 0, 0, tiled=True)
    padded = spread.reshape(4, PHASES, 24, LANES).transpose(0, 2, 1, 3).reshape(96, PADDED)
    return lax.dot_general(
        padded, head_columns(), (((1,), (1,)), ((), ())), precision=lax.Precision.HIGHEST, preferred_element_type=F32
    )


def local_edges(pairs):
    grid = pairs.reshape(LAT, LON_DEV, PAIR)
    return grid[:, :MARGIN].reshape(EDGE, PAIR), grid[:, LON_DEV - MARGIN :].reshape(EDGE, PAIR)


def shards(tokens, norm_gain, query_key_value_weight, out_weight, head_weight, coarse, grad_fine):
    tokens = tokens[0].reshape(ROWS, D)
    gain = norm_gain.reshape(1, D)
    full = gather_weights(query_key_value_weight, out_weight, head_weight)
    residual = residual_of(coarse[0])
    normed, rows = prepare(tokens, gain, grad_fine[0])
    pairs = project(normed, full, 2, 4)
    leading, last = local_edges(pairs)
    left = shifted(last, 1)
    right = shifted(leading, -1)
    normed_later = lax.optimization_barrier((normed, pairs))[0]
    queries = project(normed_later, full, 0, 2)
    head = head_of(full)
    grad_hidden, grad_attended = hidden_grad(rows, head, full)
    attended = attend_forward(queries, pairs, left, right)
    fine_grid, pieces = hidden_and_head(tokens, attended, full, head, rows, residual)
    grad_head = reduce_head(pieces)
    dq, dk, dv, dkl, dvl, dkr, dvr = attend_backward(queries, pairs, left, right, grad_attended)
    from_right = shifted(jnp.concatenate([dkl, dvl], axis=1), -1)
    from_left = shifted(jnp.concatenate([dkr, dvr], axis=1), 1)
    grad_tokens = norm_grad(dq, dk, dv, from_left, from_right, full, tokens, gain, grad_hidden)
    return (fine_grid[None], grad_tokens.reshape(1, LAT, LON_DEV, D), grad_head)


def solution(mesh):
    fine_mesh = Mesh(mesh.devices.reshape(2, ZS, CORES, YS, XS), ("dp", "z", "c", "y", "x"))
    samples = ("dp", "z", "c")
    placed = (
        P(samples, None, TILE, None),
        P(),
        P(FSDP, None),
        P(FSDP, None),
        P(FSDP, None),
        P(samples, None, None, TILE),
        P(samples, None, None, TILE),
    )
    return jax.shard_map(
        shards,
        mesh=fine_mesh,
        in_specs=placed,
        out_specs=(P(samples, None, None, TILE), P(samples, None, TILE, None), P(FSDP, None)),
        check_vma=False,
    )
```

time: 270 us -> 232 us (0.86)
  local copies, waits for them, and re-layouts: 67.9 us -> 5.49 us
  Pallas kernels: 0 us -> 45.3 us
  blocking collectives: 0 us -> 27.2 us
  matrix products: 33.3 us -> 10.4 us
  waiting for transfers between devices: 95.1 us -> 85.8 us
  other arithmetic: 12.4 us -> 4.53 us
  starting transfers between devices: 45.3 us -> 37.5 us
    pallas_call x0 -> x8, Pallas kernels: none -> 45.3 us  [the longest x1 10.7 us: norm_grad(): pl.pallas_call(norm_grad_kernel, out_shape=jax.ShapeDtypeStruct((ROWS, D)...]
    all_to_all x0 -> x1, blocking collectives: none -> 27.2 us  [reduce_head(): lax.all_to_all(pieces.reshape(CORES * TILES, ZS, 24, LANES), ('c',) + TIL...]
    dot_general x14 -> x7, matrix products: 29.3 us -> 10.4 us  [the longest x4 7.65 us: dot(): lax.dot_general(left, right, (((1,), (0,)), ((), ())), preferred_element_...]
    all_to_all x2 -> x1, waiting for transfers between devices: 14.7 us -> 0.01 us  [reduce_head(): spread = lax.all_to_all(spread, TILE, 0, 0, tiled=True)]
    reshape x6 -> x2, local copies, waits for them, and re-layouts: 14.4 us -> 0.62 us  [the longest x1 0.6 us: shards(): gain = norm_gain.reshape(1, D)]
    ppermute x7 -> x6, waiting for transfers between devices: 1.33 us -> 13.3 us  [shifted(): lax.ppermute(value, TILE, [(i, (i + steps) % TILES) for i in range(TILES)])]
    all_to_all x1, waiting for transfers between devices: 8.76 us -> 0.01 us  [reduce_head(): both = lax.all_to_all(both, ('dp', 'z'), 0, 0, tiled=True)]
    slice x9 -> x2, local copies, waits for them, and re-layouts: 9.48 us -> 0.89 us  [the longest x1 0.8 us: gather_weights(): out_half[:, :GROUP]]
  transfers between devices with their start and end apart: 11 -> 9, of which waited for: 5 -> 3; matrix products, arithmetic and copies ran while one was open for 19% -> 4% of each run, Pallas kernels for 0% -> 11%
where the time goes in v2:
time: 232 us; the launch traced here: 230 us
  waiting for transfers between devices  85.8 us (37%)
  Pallas kernels  45.3 us (20%)
  starting transfers between devices  37.5 us (16%)
  blocking collectives  27.2 us (12%)
  between operations  14.3 us (6%)
  matrix products  10.4 us (4%)
  local copies, waits for them, and re-layouts  5.49 us (2%)
  other arithmetic  4.53 us (2%)
    all_gather x1, waiting for transfers between devices, gather_weights(): full = lax.all_gather(packed, ('dp',) + FSDP, axis=0, tiled=True)  72.4 us
    all_to_all x1, blocking collectives, reduce_head(): lax.all_to_all(pieces.reshape(CORES * TILES, ZS, 24, LANES), ('c',) + TIL...  27.2 us
    ppermute x6, starting transfers between devices, shifted(): lax.ppermute(value, TILE, [(i, (i + steps) % TILES) for i in range(TILES)])  23.7 us
    ppermute x6, waiting for transfers between devices, shifted(): lax.ppermute(value, TILE, [(i, (i + steps) % TILES) for i in range(TILES)])  13.3 us
    pallas_call x1, Pallas kernels, norm_grad(): pl.pallas_call(norm_grad_kernel, out_shape=jax.ShapeDtypeStruct((ROWS, D)...  10.7 us
    pallas_call x2, Pallas kernels, project(): pl.pallas_call(project_kernel, out_shape=jax.ShapeDtypeStruct((ROWS, coun...  8.94 us
    all_to_all x1, starting transfers between devices, reduce_head(): both = lax.all_to_all(both, ('dp', 'z'), 0, 0, tiled=True)  7.7 us
    dot_general x4, matrix products, dot(): lax.dot_general(left, right, (((1,), (0,)), ((), ())), preferred_element_...  7.65 us
  transfers between devices with their start and end apart: 9, of which 3 were waited for; matrix products, arithmetic and copies ran while one was open for 4% of the time, Pallas kernels for 11%

profile of v2, /device:TPU:32, one launch (start us, length us, event | category | flops | bytes accessed | tf_op | source)
XLA Modules:
  0.0 230.4 jit_solution(4829904058534039019)
XLA Ops:
  10.0 3.4 %collective-permute-start.2 = (f32[20,8,1]{2,1,0:T(8,128)S(1)}, f32[20,8,1]{2,1,0:T(8,128)S(1)}, u32[]{:S(2)}, u32[]{:S(2)}) collective-permute-start(f32[20,8,1]{2,1,0:T(8,128)S(1)} %get-tuple-element.35), channel_id=1, source_target_pairs={{0,1},{1,2},{2,3},{3,4},{4,5},{5,6},{6,7},{7,8},{8,9},{9,10},{10,1... | collective-permute-start | bytes 1928 | tf_op jit(solution)/shard_map/ppermute | solution.py:425
  13.4 5.8 %collective-permute-start.3 = (f32[20,8,1]{2,1,0:T(8,128)S(1)}, f32[20,8,1]{2,1,0:T(8,128)S(1)}, u32[]{:S(2)}, u32[]{:S(2)}) collective-permute-start(f32[20,8,1]{2,1,0:T(8,128)S(1)} %get-tuple-element.36), channel_id=1, source_target_pairs={{0,15},{1,0},{2,1},{3,2},{4,3},{5,4},{6,5},{7,6},{8,7},{9,8},{10,9... | collective-permute-start | bytes 1928 | tf_op jit(solution)/shard_map/ppermute | solution.py:425
  19.9 2.8 %prepare.1 = (bf16[256,1536]{1,0:T(8,128)(2,1)}, bf16[256,512]{1,0:T(8,128)(2,1)}) custom-call(bf16[256,1536]{1,0:T(8,128)(2,1)} %bitcast.54, f32[1,1536]{1,0:T(1,128)} %reshape.141.gain_ref, f32[20,32,128]{2,1,0:T(8,128)} %bitcast.63), custom_call_target="tpu_custom_call" | custom-call | tf_op jit(solution)/shard_map/prepare/pallas_call | solution.py:83
  24.4 72.4 %all-gather.2.cloned.1.call-done = bf16[3072,1696]{1,0:T(8,128)(2,1)} async-done(((bf16[96,1696]{1,0:T(8,128)(2,1)}), bf16[3072,1696]{1,0:T(8,128)(2,1)}) %all-gather.2.cloned.1.call-update) | async-done | bytes 10420240 | tf_op jit(solution)/shard_map/all_gather | solution.py:456
  96.8 2.7 %fusion.4 = f32[1536,256]{1,0:T(8,128)} fusion(bf16[2,1536,1696]{2,1,0:T(8,128)(2,1)} %bitcast.42, bf16[320,512]{1,0:T(8,128)(2,1)S(1)} %convert_convert_fusion), kind=kOutput, calls=%fused_computation.11 | convolution fusion | flops 125829120 | bytes 2441216 | tf_op jit(solution)/shard_map/dot_general | solution.py:45
  99.4 1.5 fusion.5
  100.9 5.5 %project.2.k_ref.v_ref = bf16[256,1536]{1,0:T(8,128)(2,1)} custom-call(bf16[256,1536]{1,0:T(8,128)(2,1)} %get-tuple-element.18.normed_ref, bf16[2,1536,1696]{2,1,0:T(8,128)(2,1)} %bitcast.44), custom_call_target="tpu_custom_call" | custom-call | tf_op jit(solution)/shard_map/project/pallas_call | solution.py:100
  106.4 3.5 %project.3.q_ref = bf16[256,768]{1,0:T(8,128)(2,1)} custom-call(bf16[256,1536]{1,0:T(8,128)(2,1)} %get-tuple-element.18.normed_ref, bf16[2,1536,1696]{2,1,0:T(8,128)(2,1)} %bitcast.45), custom_call_target="tpu_custom_call" | custom-call | tf_op jit(solution)/shard_map/project/pallas_call | solution.py:100
  109.9 6.8 %collective-permute-start.1 = (bf16[64,1536]{1,0:T(8,128)(2,1)S(1)}, bf16[64,1536]{1,0:T(8,128)(2,1)S(1)}, u32[]{:S(2)}, u32[]{:S(2)}) collective-permute-start(bf16[64,1536]{1,0:T(8,128)(2,1)S(1)} %get-tuple-element.31), channel_id=1, source_target_pairs={{0,15},{1,0},{2,1},{3,2},{4,3},{5,4},{6,5},{7,6},{8,7},{9,8},{10,9... | collective-permute-start | bytes 589832 | tf_op jit(solution)/shard_map/ppermute | solution.py:425
  116.7 1.9 collective-permute-start
  118.6 2.0 fusion.2
  120.6 1.5 fusion.3
  123.4 5.2 %collective-permute-done.kl_ref.vl_ref = bf16[64,1536]{1,0:T(8,128)(2,1)S(1)} collective-permute-done((bf16[64,1536]{1,0:T(8,128)(2,1)S(1)}, bf16[64,1536]{1,0:T(8,128)(2,1)S(1)}, u32[]{:S(2)}, u32[]{:S(2)}) %collective-permute-start) | collective-permute-done | bytes 196640 | tf_op jit(solution)/shard_map/ppermute | solution.py:425
  129.3 4.6 %attend_forward.1.attended_ref = bf16[256,768]{1,0:T(8,128)(2,1)} custom-call(bf16[256,768]{1,0:T(8,128)(2,1)} %project.3.q_ref, bf16[256,1536]{1,0:T(8,128)(2,1)} %project.2.k_ref.v_ref, bf16[256,1536]{1,0:T(8,128)(2,1)} %project.2.k_ref.v_ref, bf16[64,1536]{1,0:T(8,128)(2,1)} %copy-done.3, bf16[64,1536]{1,0:T(8,128)(2,1)} %copy-done.3, ...), custom_call_target="tpu_custom_call" | custom-call | tf_op jit(solution)/shard_map/attend_forward/pallas_call | solution.py:202
  134.0 6.2 %hidden_and_head.1 = (f32[20,32,128]{2,1,0:T(8,128)}, bf16[2,16,8,24,128]{4,3,2,1,0:T(8,128)(2,1)}) custom-call(bf16[256,1536]{1,0:T(8,128)(2,1)} %bitcast.55, bf16[256,768]{1,0:T(8,128)(2,1)} %attend_forward.1.attended_ref, bf16[2,1536,1696]{2,1,0:T(8,128)(2,1)} %bitcast.48, bf16[2,1536,1696]{2,1,0:T(8,128)(2,1)} %bitcast.49, ...), custom_call_target="tpu_custom_call" | custom-call | tf_op jit(solution)/shard_map/hidden_and_head/pallas_call | solution.py:315
  140.2 27.2 %all_to_all.15 = bf16[32,8,24,128]{3,2,1,0:T(8,128)(2,1)S(1)} all-to-all(bf16[32,8,24,128]{3,2,1,0:T(8,128)(2,1)} %bitcast.57), channel_id=1, replica_groups=mesh['dp'=2,'z'=8,'c'=2,'y'=4,'x'=4] {'c','y','x'}, dimensions={0} | all-to-all | bytes 3145728 | tf_op jit(solution)/shard_map/all_to_all | solution.py:472
  168.3 7.7 %all-to-all-start.1 = ((f32[16,24,128]{2,1,0:T(8,128)}), f32[16,24,128]{2,1,0:T(8,128)S(1)}, u32[]{:S(2)}, u32[]{:S(2)}) async-start(f32[16,24,128]{2,1,0:T(8,128)} %bitcast.17), calls=%async_computation.1 | async-start | bytes 393216 | tf_op jit(solution)/shard_map/all_to_all | solution.py:475
  176.0 4.8 %hidden_grad.1 = (f32[256,1536]{1,0:T(8,128)}, bf16[256,768]{1,0:T(8,128)(2,1)}) custom-call(bf16[256,512]{1,0:T(8,128)(2,1)} %get-tuple-element.19.rows_ref, bf16[2,1536,256]{2,1,0:T(8,128)(2,1)} %pad_maximum_fusion.head_ref, bf16[2,1536,1696]{2,1,0:T(8,128)(2,1)} %bitcast.50, bf16[2,1536,1696]{2,1,0:T(8,128)(2,1)} %bitcast.51), custom_call_target="tpu_custom_call" | custom-call | tf_op jit(solution)/shard_map/hidden_grad/pallas_call | solution.py:142
  180.8 7.2 %attend_backward.1 = (bf16[256,768]{1,0:T(8,128)(2,1)}, f32[256,768]{1,0:T(8,128)}, f32[256,768]{1,0:T(8,128)}, f32[64,768]{1,0:T(8,128)}, f32[64,768]{1,0:T(8,1...) custom-call(bf16[256,768]{1,0:T(8,128)(2,1)} %project.3.q_ref, bf16[256,1536]{1,0:T(8,128)(2,1)} %project.2.k_ref.v_ref, ...), custom_call_target="tpu_custom_call" | custom-call | tf_op jit(solution)/shard_map/attend_backward/pallas_call | solution.py:259
  189.1 3.3 %collective-permute-start.5 = (f32[64,1536]{1,0:T(8,128)S(1)}, f32[64,1536]{1,0:T(8,128)S(1)}, u32[]{:S(2)}, u32[]{:S(2)}) collective-permute-start(f32[64,1536]{1,0:T(8,128)S(1)} %pad_maximum_fusion.2), channel_id=1, source_target_pairs={{0,15},{1,0},{2,1},{3,2},{4,3},{5,4},{6,5},{7,6},{8,7},{9,8},{10,9... | collective-permute-start | bytes 1179656 | tf_op jit(solution)/shard_map/ppermute | solution.py:425
  193.4 2.6 %collective-permute-start.4 = (f32[64,1536]{1,0:T(8,128)S(1)}, f32[64,1536]{1,0:T(8,128)S(1)}, u32[]{:S(2)}, u32[]{:S(2)}) collective-permute-start(f32[64,1536]{1,0:T(8,128)S(1)} %pad_maximum_fusion.1), channel_id=1, source_target_pairs={{0,1},{1,2},{2,3},{3,4},{4,5},{5,6},{6,7},{7,8},{8,9},{9,10},{10,1... | collective-permute-start | bytes 1179656 | tf_op jit(solution)/shard_map/ppermute | solution.py:425
  196.7 6.1 %all-to-all-start.2 = ((f32[16,24,128]{2,1,0:T(8,128)}), f32[16,24,128]{2,1,0:T(8,128)S(1)}, u32[]{:S(2)}, u32[]{:S(2)}) async-start(f32[16,24,128]{2,1,0:T(8,128)} %broadcast_in_dim.78), calls=%async_computation.2 | async-start | bytes 393216 | tf_op jit(solution)/shard_map/all_to_all | solution.py:478
  202.8 8.1 %collective-permute-done.4.kl_ref.vl_ref = f32[64,1536]{1,0:T(8,128)S(1)} collective-permute-done((f32[64,1536]{1,0:T(8,128)S(1)}, f32[64,1536]{1,0:T(8,128)S(1)}, u32[]{:S(2)}, u32[]{:S(2)}) %collective-permute-start.4) | collective-permute-done | bytes 393248 | tf_op jit(solution)/shard_map/ppermute | solution.py:425
  211.7 10.7 %norm_grad.1 = bf16[256,1536]{1,0:T(8,128)(2,1)} custom-call(bf16[256,768]{1,0:T(8,128)(2,1)} %get-tuple-element.22.dq_ref, f32[256,768]{1,0:T(8,128)} %get-tuple-element.23.dk_ref, f32[256,768]{1,0:T(8,128)} %get-tuple-element.24.dv_ref, f32[64,1536]{1,0:T(8,128)} %copy-done.5, f32[64,1536]{1,0:T(8,128)} %copy-done.5, f32[64,1536]{1,0:T(8,128)} %copy-done.4, ...), custom_call_target="tpu_custom_call" | custom-call | tf_op jit(solution)/shard_map/norm_grad/pallas_call | solution.py:386
  (48 shorter events, 12.9 us)
Async XLA Ops:
  7.2 1.9 copy-start
  7.2 2.7 %copy-start.6 = (f32[1,20,8,32]{3,2,1,0:T(8,128)S(1)}, f32[1,20,8,32]{3,2,1,0:T(8,128)}, u32[]{:S(2)}) copy-start(f32[1,20,8,32]{3,2,1,0:T(8,128)} %param.12) | copy-start | bytes 61444
  7.2 12.1 %copy-start.7 = (f32[1536]{0:T(1024)S(1)}, f32[1536]{0:T(1024)}, u32[]{:S(2)}) copy-start(f32[1536]{0:T(1024)} %param.8) | copy-start | bytes 18436
  7.2 89.6 %all-gather.2.cloned.1.call-start = ((), (), s32[]{:S(2)}) async-start(), calls=%async_computation.3 | async-start | bytes 11354112 | tf_op jit(solution)/shard_map/all_gather | solution.py:456
  10.0 12.7 %collective-permute-start.2 = (f32[20,8,1]{2,1,0:T(8,128)S(1)}, f32[20,8,1]{2,1,0:T(8,128)S(1)}, u32[]{:S(2)}, u32[]{:S(2)}) collective-permute-start(f32[20,8,1]{2,1,0:T(8,128)S(1)} %get-tuple-element.35), channel_id=1, source_target_pairs={{0,1},{1,2},{2,3},{3,4},{4,5},{5,6},{6,7},{7,8},{8,9},{9,10},{10,1... | collective-permute-start | bytes 1928 | tf_op jit(solution)/shard_map/ppermute | solution.py:425
  13.4 9.3 %collective-permute-start.3 = (f32[20,8,1]{2,1,0:T(8,128)S(1)}, f32[20,8,1]{2,1,0:T(8,128)S(1)}, u32[]{:S(2)}, u32[]{:S(2)}) collective-permute-start(f32[20,8,1]{2,1,0:T(8,128)S(1)} %get-tuple-element.36), channel_id=1, source_target_pairs={{0,15},{1,0},{2,1},{3,2},{4,3},{5,4},{6,5},{7,6},{8,7},{9,8},{10,9... | collective-permute-start | bytes 1928 | tf_op jit(solution)/shard_map/ppermute | solution.py:425
  106.4 3.5 %copy-start.1 = (bf16[256,1536]{1,0:T(8,128)(2,1)S(1)}, bf16[256,1536]{1,0:T(8,128)(2,1)}, u32[]{:S(2)}) copy-start(bf16[256,1536]{1,0:T(8,128)(2,1)} %project.2.k_ref.v_ref) | copy-start | bytes 2359300
  109.9 13.5 %collective-permute-start.1 = (bf16[64,1536]{1,0:T(8,128)(2,1)S(1)}, bf16[64,1536]{1,0:T(8,128)(2,1)S(1)}, u32[]{:S(2)}, u32[]{:S(2)}) collective-permute-start(bf16[64,1536]{1,0:T(8,128)(2,1)S(1)} %get-tuple-element.31), channel_id=1, source_target_pairs={{0,15},{1,0},{2,1},{3,2},{4,3},{5,4},{6,5},{7,6},{8,7},{9,8},{10,9... | collective-permute-start | bytes 589832 | tf_op jit(solution)/shard_map/ppermute | solution.py:425
  116.7 12.0 %collective-permute-start = (bf16[64,1536]{1,0:T(8,128)(2,1)S(1)}, bf16[64,1536]{1,0:T(8,128)(2,1)S(1)}, u32[]{:S(2)}, u32[]{:S(2)}) collective-permute-start(bf16[64,1536]{1,0:T(8,128)(2,1)S(1)} %get-tuple-element.32), channel_id=1, source_target_pairs={{0,1},{1,2},{2,3},{3,4},{4,5},{5,6},{6,7},{7,8},{8,9},{9,10},{10,1... | collective-permute-start | bytes 589832 | tf_op jit(solution)/shard_map/ppermute | solution.py:425
  123.4 5.2 %copy-start.2 = (bf16[64,1536]{1,0:T(8,128)(2,1)}, bf16[64,1536]{1,0:T(8,128)(2,1)S(1)}, u32[]{:S(2)}) copy-start(bf16[64,1536]{1,0:T(8,128)(2,1)S(1)} %collective-permute-done.1.kr_ref.vr_ref) | copy-start | bytes 589828
  128.6 0.7 copy-start.3
  168.3 27.7 %all-to-all-start.1 = ((f32[16,24,128]{2,1,0:T(8,128)}), f32[16,24,128]{2,1,0:T(8,128)S(1)}, u32[]{:S(2)}, u32[]{:S(2)}) async-start(f32[16,24,128]{2,1,0:T(8,128)} %bitcast.17), calls=%async_computation.1 | async-start | bytes 393216 | tf_op jit(solution)/shard_map/all_to_all | solution.py:475
  189.1 13.7 %collective-permute-start.5 = (f32[64,1536]{1,0:T(8,128)S(1)}, f32[64,1536]{1,0:T(8,128)S(1)}, u32[]{:S(2)}, u32[]{:S(2)}) collective-permute-start(f32[64,1536]{1,0:T(8,128)S(1)} %pad_maximum_fusion.2), channel_id=1, source_target_pairs={{0,15},{1,0},{2,1},{3,2},{4,3},{5,4},{6,5},{7,6},{8,7},{9,8},{10,9... | collective-permute-start | bytes 1179656 | tf_op jit(solution)/shard_map/ppermute | solution.py:425
  193.4 17.5 %collective-permute-start.4 = (f32[64,1536]{1,0:T(8,128)S(1)}, f32[64,1536]{1,0:T(8,128)S(1)}, u32[]{:S(2)}, u32[]{:S(2)}) collective-permute-start(f32[64,1536]{1,0:T(8,128)S(1)} %pad_maximum_fusion.1), channel_id=1, source_target_pairs={{0,1},{1,2},{2,3},{3,4},{4,5},{5,6},{6,7},{7,8},{8,9},{9,10},{10,1... | collective-permute-start | bytes 1179656 | tf_op jit(solution)/shard_map/ppermute | solution.py:425
  196.7 25.7 %all-to-all-start.2 = ((f32[16,24,128]{2,1,0:T(8,128)}), f32[16,24,128]{2,1,0:T(8,128)S(1)}, u32[]{:S(2)}, u32[]{:S(2)}) async-start(f32[16,24,128]{2,1,0:T(8,128)} %broadcast_in_dim.78), calls=%async_computation.2 | async-start | bytes 393216 | tf_op jit(solution)/shard_map/all_to_all | solution.py:478
  202.8 8.1 %copy-start.4 = (f32[64,1536]{1,0:T(8,128)}, f32[64,1536]{1,0:T(8,128)S(1)}, u32[]{:S(2)}) copy-start(f32[64,1536]{1,0:T(8,128)S(1)} %collective-permute-done.5.kr_ref.vr_ref) | copy-start | bytes 1179652
  211.0 0.8 copy-start.5
Sparse Core Ops, SparseCore 0:
  10.1 86.5 all-gather.1

commit v3 on v2

v3 whole, which is shorter than its diff:
```python
import functools
import jax
import jax.numpy as jnp
from jax import lax
from jax.experimental import pallas as pl
from jax.experimental.pallas import tpu as pltpu
from jax.sharding import Mesh
from jax.sharding import PartitionSpec as P

D = 1536
HEADS = 8
HEAD_DIM = 96
VARS = 20
MARGIN = 8
LAT = 8
LON_DEV = 32
INNER = 768
HEAD_OUT = 320
ROWS = 256
EDGE = 64
GROUP = 384
PAIR = 2 * INNER
ZS = 8
CORES = 2
YS = 4
XS = 4
TILES = 16
FSDP = ("z", "c")
TILE = ("y", "x")
HALF_QKV = 1152
HALF_OUT = 768
PIECE = 64
WIDE = ZS * 80
PHASES = 4
CHANNELS = 80
LANES = 128
PADDED = PHASES * LANES
EPSILON = 1e-05
SCALE = HEAD_DIM ** (-0.5)
F32 = jnp.float32
BF16 = jnp.bfloat16
WHOLE = pl.BlockSpec(memory_space=pltpu.VMEM)


def dot(left, right):
    return lax.dot_general(left, right, (((1,), (0,)), ((), ())), preferred_element_type=F32)


def dot_last(left, right):
    return lax.dot_general(left, right, (((1,), (1,)), ((), ())), preferred_element_type=F32)


def dot_first(left, right):
    return lax.dot_general(left, right, (((0,), (0,)), ((), ())), preferred_element_type=F32)


def spread_matrix():
    row = lax.broadcasted_iota(jnp.int32, (LANES, LANES), 0)
    lane = lax.broadcasted_iota(jnp.int32, (LANES, LANES), 1)
    target = (row % LON_DEV) * PHASES + row // LON_DEV
    return jnp.where(lane == target, 1.0, 0.0).astype(BF16)


def prepare_kernel(tokens_ref, gain_ref, fine_ref, normed_ref, rows_ref):
    values = tokens_ref[...].astype(F32)
    average = jnp.mean(values, axis=-1, keepdims=True)
    centred = values - average
    variance = jnp.mean(centred * centred, axis=-1, keepdims=True)
    standard = centred * lax.rsqrt(variance + EPSILON)
    normed_ref[...] = (standard * gain_ref[...]).astype(BF16)
    select = spread_matrix()
    empty = jnp.zeros((LANES - CHANNELS, LANES), BF16)
    for lat in range(LAT):
        block = fine_ref[:, PHASES * lat : PHASES * (lat + 1), :].reshape(CHANNELS, LANES)
        block = jnp.concatenate([block.astype(BF16), empty], axis=0)
        picked = dot_last(select, block).astype(BF16)
        for phase in range(PHASES):
            rows_ref[lat * LON_DEV : (lat + 1) * LON_DEV, phase * LANES : (phase + 1) * LANES] = picked[
                phase * LON_DEV : (phase + 1) * LON_DEV
            ]


def prepare(tokens, gain, grad_fine):
    return pl.pallas_call(
        prepare_kernel,
        out_shape=(
            jax.ShapeDtypeStruct((ROWS, D), BF16),
            jax.ShapeDtypeStruct((ROWS, PADDED), BF16),
        ),
        in_specs=[WHOLE, WHOLE, WHOLE],
        out_specs=(WHOLE, WHOLE),
        name="prepare",
    )(tokens, gain, grad_fine)


def project_kernel(normed_ref, weight_ref, out_ref):
    out_ref[...] = dot(normed_ref[...], weight_ref[0]).astype(BF16)


def project_pairs_kernel(normed_ref, weight_ref, out_ref, leading_ref, last_ref):
    values = dot(normed_ref[...], weight_ref[0])
    out_ref[...] = values.astype(BF16)
    grid = values.reshape(LAT, LON_DEV, GROUP)
    leading_ref[...] = grid[:, :MARGIN].reshape(EDGE, GROUP).astype(BF16)
    last_ref[...] = grid[:, LON_DEV - MARGIN :].reshape(EDGE, GROUP).astype(BF16)


def project_specs(first):
    return [
        pl.BlockSpec((ROWS, D), lambda n: (0, 0)),
        pl.BlockSpec((1, D, GROUP), lambda n: ((n + first) // 3, 0, (n + first) % 3)),
    ]


def project(normed, full):
    return pl.pallas_call(
        project_kernel,
        out_shape=jax.ShapeDtypeStruct((ROWS, INNER), BF16),
        grid=(2,),
        in_specs=project_specs(0),
        out_specs=pl.BlockSpec((ROWS, GROUP), lambda n: (0, n)),
        name="project",
    )(normed, full)


def project_pairs(normed, full):
    edge = jax.ShapeDtypeStruct((EDGE, PAIR), BF16)
    return pl.pallas_call(
        project_pairs_kernel,
        out_shape=(jax.ShapeDtypeStruct((ROWS, PAIR), BF16), edge, edge),
        grid=(4,),
        in_specs=project_specs(2),
        out_specs=(
            pl.BlockSpec((ROWS, GROUP), lambda n: (0, n)),
            pl.BlockSpec((EDGE, GROUP), lambda n: (0, n)),
            pl.BlockSpec((EDGE, GROUP), lambda n: (0, n)),
        ),
        name="project_pairs",
    )(normed, full)


def unpack_kernel(pieces_ref, out_ref, head_ref):
    for core in range(CORES):
        for z in range(ZS):
            shard = z * CORES + core
            for tile in range(60):
                block = pieces_ref[core, tile // 4, z, tile % 4 * 16 : (tile % 4 + 1) * 16, :]
                if tile < 36:
                    top = shard * 48 + tile % 3 * 16
                    out_ref[top : top + 16, tile // 3 * LANES : (tile // 3 + 1) * LANES] = block
                else:
                    top = shard * 96 + tile % 6 * 16
                    phase = (tile - 36) // 6
                    head_ref[top : top + 16, phase * LANES : (phase + 1) * LANES] = block


def unpack(pieces):
    return pl.pallas_call(
        unpack_kernel,
        out_shape=(
            jax.ShapeDtypeStruct((INNER, D), BF16),
            jax.ShapeDtypeStruct((D, PADDED), BF16),
        ),
        in_specs=[WHOLE],
        out_specs=(WHOLE, WHOLE),
        name="unpack",
    )(pieces)


def hidden_grad_kernel(rows_ref, head_ref, out_ref, hidden_ref, attended_ref):
    grad_hidden = dot_last(rows_ref[...], head_ref[...])
    hidden_ref[...] = grad_hidden
    attended_ref[...] = dot_last(grad_hidden.astype(BF16), out_ref[...]).astype(BF16)


def hidden_grad(rows, head, out_weight):
    return pl.pallas_call(
        hidden_grad_kernel,
        out_shape=(
            jax.ShapeDtypeStruct((ROWS, D), F32),
            jax.ShapeDtypeStruct((ROWS, INNER), BF16),
        ),
        in_specs=[WHOLE, WHOLE, WHOLE],
        out_specs=(WHOLE, WHOLE),
        name="hidden_grad",
    )(rows, head, out_weight)


def whole_block(shape):
    return pl.BlockSpec(shape, lambda n: (0,) * len(shape))


def head_window(head):
    first = head * HEAD_DIM // LANES * LANES
    last = -(-(head + 1) * HEAD_DIM // LANES) * LANES
    lane = lax.broadcasted_iota(jnp.int32, (1, last - first), 1) + first
    inside = (lane >= head * HEAD_DIM) & (lane < (head + 1) * HEAD_DIM)
    return first, last, inside


def masked(values, inside):
    return jnp.where(inside, values, jnp.zeros_like(values))


def softmax_of(query, key):
    scores = dot_last(query, key) * SCALE
    biggest = jnp.max(scores, axis=-1, keepdims=True)
    exponent = jnp.exp(scores - biggest)
    return exponent / jnp.sum(exponent, axis=-1, keepdims=True)


def joined(own_ref, left_ref, right_ref):
    return jnp.concatenate([own_ref[...], left_ref[...], right_ref[...]], axis=0)


def forward_group(q_ref, k_ref, v_ref, kl_ref, vl_ref, kr_ref, vr_ref):
    queries = q_ref[...]
    keys = joined(k_ref, kl_ref, kr_ref)
    values = joined(v_ref, vl_ref, vr_ref)
    parts = [None, None, None]
    for head in range(4):
        first, last, inside = head_window(head)
        softmax = softmax_of(masked(queries[:, first:last], inside), keys[:, first:last])
        result = dot(softmax.astype(BF16), masked(values[:, first:last], inside))
        for tile in range(first // LANES, last // LANES):
            piece = result[:, tile * LANES - first : (tile + 1) * LANES - first]
            parts[tile] = piece if parts[tile] is None else parts[tile] + piece
    return jnp.concatenate([part.astype(BF16) for part in parts], axis=1)


def forward_kernel(
    q_ref, k_ref, v_ref, kl_ref, vl_ref, kr_ref, vr_ref,
    tokens_hbm, out_hbm, head_hbm, rows_hbm, residual_hbm,
    fine_ref, pieces_ref,
    attended, tokens_ref, out_ref, head_ref, rows_ref, residual_ref, products, sems,
):
    step = pl.program_id(0)
    copies = [
        pltpu.make_async_copy(source, target, sems.at[place])
        for place, (source, target) in enumerate(
            (
                (tokens_hbm, tokens_ref),
                (out_hbm, out_ref),
                (head_hbm, head_ref),
                (rows_hbm, rows_ref),
                (residual_hbm, residual_ref),
            )
        )
    ]

    @pl.when(step == 0)
    def _():
        for copy in copies:
            copy.start()

    attended[step] = forward_group(q_ref, k_ref, v_ref, kl_ref, vl_ref, kr_ref, vr_ref)

    @pl.when(step == 1)
    def _():
        for copy in copies:
            copy.wait()
        mixed = dot(attended[0], out_ref[:GROUP]) + dot(attended[1], out_ref[GROUP:])
        hidden = (tokens_ref[...].astype(F32) + mixed).astype(BF16)
        head_out = dot(hidden, head_ref[...])
        products[...] = dot_first(hidden, rows_ref[...])
        for core in range(CORES):
            for quad in range(4):
                for phase in range(PHASES):
                    row = [
                        products[
                            (z * CORES + core) * 96 + quad * 24 : (z * CORES + core) * 96 + quad * 24 + 24,
                            phase * LANES : phase * LANES + CHANNELS,
                        ]
                        for z in range(ZS)
                    ]
                    pieces_ref[core * TILES + quad * 4 + phase] = jnp.concatenate(row, axis=1).astype(BF16)
        select = spread_matrix()
        for lat in range(LAT):
            at = slice(lat * LON_DEV, (lat + 1) * LON_DEV)
            stacked = jnp.concatenate(
                [head_out[at, phase * LANES : (phase + 1) * LANES] for phase in range(PHASES)], axis=0
            )
            high = stacked.astype(BF16)
            low = (stacked - high.astype(F32)).astype(BF16)
            spread = dot_first(high, select) + dot_first(low, select)
            across = slice(PHASES * lat, PHASES * (lat + 1))
            fine_ref[:, across, :] = spread[:CHANNELS].reshape(VARS, PHASES, LANES) + residual_ref[:, across, :]


def attention_specs():
    def spec(rows, offset):
        return pl.BlockSpec((rows, GROUP), lambda n: (0, n + offset))

    return [spec(ROWS, 0), spec(ROWS, 0), spec(ROWS, 2), spec(EDGE, 0), spec(EDGE, 2), spec(EDGE, 0), spec(EDGE, 2)]


def forward(queries, pairs, left, right, tokens, out_weight, head, rows, residual):
    fine = (VARS, 4 * LAT, LANES)
    pieces = (CORES * TILES, 24, WIDE)
    return pl.pallas_call(
        forward_kernel,
        out_shape=(jax.ShapeDtypeStruct(fine, F32), jax.ShapeDtypeStruct(pieces, BF16)),
        grid=(2,),
        in_specs=attention_specs() + [pl.BlockSpec(memory_space=pl.ANY)] * 5,
        out_specs=(whole_block(fine), whole_block(pieces)),
        scratch_shapes=[
            pltpu.VMEM((2, ROWS, GROUP), BF16),
            pltpu.VMEM((ROWS, D), BF16),
            pltpu.VMEM((INNER, D), BF16),
            pltpu.VMEM((D, PADDED), BF16),
            pltpu.VMEM((ROWS, PADDED), BF16),
            pltpu.VMEM(fine, F32),
            pltpu.VMEM((D, PADDED), F32),
            pltpu.SemaphoreType.DMA((5,)),
        ],
        name="forward",
    )(queries, pairs, pairs, left, left, right, right, tokens, out_weight, head, rows, residual)


def backward_kernel(
    q_ref, k_ref, v_ref, kl_ref, vl_ref, kr_ref, vr_ref, grad_ref,
    dq_ref, dk_ref, dv_ref, left_ref, right_ref,
):
    queries = q_ref[...]
    grads = grad_ref[...]
    keys = joined(k_ref, kl_ref, kr_ref)
    values = joined(v_ref, vl_ref, vr_ref)
    sums = [[None, None, None] for _ in range(3)]
    for head in range(4):
        first, last, inside = head_window(head)
        query = masked(queries[:, first:last], inside)
        grad = masked(grads[:, first:last], inside)
        softmax = softmax_of(query, keys[:, first:last])
        grad_weights = dot_last(grad, values[:, first:last])
        weighted = jnp.sum(softmax * grad_weights, axis=-1, keepdims=True)
        grad_scores = (softmax * (grad_weights - weighted)).astype(BF16)
        results = (
            dot(grad_scores, masked(keys[:, first:last], inside)),
            dot_first(grad_scores, query),
            dot_first(softmax.astype(BF16), grad),
        )
        for kept, result in zip(sums, results):
            for tile in range(first // LANES, last // LANES):
                piece = result[:, tile * LANES - first : (tile + 1) * LANES - first]
                kept[tile] = piece if kept[tile] is None else kept[tile] + piece
    for tile in range(3):
        at = slice(tile * LANES, (tile + 1) * LANES)
        dq_ref[:, at] = (sums[0][tile] * SCALE).astype(BF16)
        grad_keys = sums[1][tile] * SCALE
        grad_values = sums[2][tile]
        for kind, (grads_of, own) in enumerate(((grad_keys, dk_ref), (grad_values, dv_ref))):
            own[:, at] = grads_of[:ROWS]
            left_ref[kind, :, at] = grads_of[ROWS : ROWS + EDGE].astype(BF16)
            right_ref[kind, :, at] = grads_of[ROWS + EDGE :].astype(BF16)


def attend_backward(queries, pairs, left, right, grad_attended):
    def block(rows):
        return pl.BlockSpec((rows, GROUP), lambda n: (0, n))

    def shape(rows, kind):
        return jax.ShapeDtypeStruct((rows, INNER), kind)

    edge = jax.ShapeDtypeStruct((2, EDGE, INNER), BF16)
    edge_block = pl.BlockSpec((2, EDGE, GROUP), lambda n: (0, 0, n))
    return pl.pallas_call(
        backward_kernel,
        out_shape=(shape(ROWS, BF16), shape(ROWS, F32), shape(ROWS, F32), edge, edge),
        grid=(2,),
        in_specs=attention_specs() + [block(ROWS)],
        out_specs=(block(ROWS), block(ROWS), block(ROWS), edge_block, edge_block),
        name="attend_backward",
    )(queries, pairs, pairs, left, left, right, right, grad_attended)


def norm_grad_kernel(
    dq_ref, dk_ref, dv_ref, left_ref, right_ref, low_ref, up_ref, gain_ref, tokens_hbm, hidden_hbm,
    out_ref, grads, total, tokens_ref, hidden_ref, sems,
):
    step = pl.program_id(0)
    copies = (
        pltpu.make_async_copy(tokens_hbm, tokens_ref, sems.at[0]),
        pltpu.make_async_copy(hidden_hbm, hidden_ref, sems.at[1]),
    )

    @pl.when(step == 0)
    def _():
        for copy in copies:
            copy.start()
        grads[:, :INNER] = dq_ref[...]
        for kind, own_ref in enumerate((dk_ref, dv_ref)):
            own = own_ref[...].reshape(LAT, LON_DEV, INNER)
            left = left_ref[kind].astype(F32).reshape(LAT, MARGIN, INNER)
            right = right_ref[kind].astype(F32).reshape(LAT, MARGIN, INNER)
            own = jnp.concatenate(
                [own[:, :MARGIN] + left, own[:, MARGIN : LON_DEV - MARGIN], own[:, LON_DEV - MARGIN :] + right],
                axis=1,
            )
            grads[:, (kind + 1) * INNER : (kind + 2) * INNER] = own.reshape(ROWS, INNER).astype(BF16)

    at = pl.ds(pl.multiple_of(step * 256, 256), 256)
    total[:, at] = dot_last(grads[:, :HALF_QKV], low_ref[0]) + dot_last(grads[:, HALF_QKV:], up_ref[0])

    @pl.when(step == 5)
    def _():
        for copy in copies:
            copy.wait()
        values = tokens_ref[...].astype(F32)
        average = jnp.mean(values, axis=-1, keepdims=True)
        centred = values - average
        variance = jnp.mean(centred * centred, axis=-1, keepdims=True)
        inverse_dev = lax.rsqrt(variance + EPSILON)
        standard = centred * inverse_dev
        grad_standard = total[...] * gain_ref[...]
        first_mean = jnp.mean(grad_standard, axis=-1, keepdims=True)
        second_mean = jnp.mean(grad_standard * standard, axis=-1, keepdims=True)
        grad = inverse_dev * (grad_standard - first_mean - standard * second_mean)
        out_ref[...] = (hidden_ref[...] + grad).astype(BF16)


def norm_grad(dq, dk, dv, from_left, from_right, full, tokens, gain, grad_hidden):
    return pl.pallas_call(
        norm_grad_kernel,
        out_shape=jax.ShapeDtypeStruct((ROWS, D), BF16),
        grid=(6,),
        in_specs=[
            whole_block((ROWS, INNER)),
            whole_block((ROWS, INNER)),
            whole_block((ROWS, INNER)),
            whole_block((2, EDGE, INNER)),
            whole_block((2, EDGE, INNER)),
            pl.BlockSpec((1, 256, HALF_QKV), lambda n: (0, n, 0)),
            pl.BlockSpec((1, 256, HALF_QKV), lambda n: (1, n, 0)),
            whole_block((1, D)),
            pl.BlockSpec(memory_space=pl.ANY),
            pl.BlockSpec(memory_space=pl.ANY),
        ],
        out_specs=whole_block((ROWS, D)),
        scratch_shapes=[
            pltpu.VMEM((ROWS, 3 * INNER), BF16),
            pltpu.VMEM((ROWS, D), F32),
            pltpu.VMEM((ROWS, D), BF16),
            pltpu.VMEM((ROWS, D), F32),
            pltpu.SemaphoreType.DMA((2,)),
        ],
        name="norm_grad",
    )(dq, dk, dv, from_left, from_right, full, full, gain, tokens, grad_hidden)


def sum_kernel(pieces_ref, out_ref):
    total = pieces_ref[0].astype(F32)
    for place in range(1, CORES * TILES):
        total = total + pieces_ref[place].astype(F32)
    empty = jnp.zeros((24, LANES - CHANNELS), F32)
    for z in range(ZS):
        part = jnp.concatenate([total[:, z * CHANNELS : (z + 1) * CHANNELS], empty], axis=1)
        out_ref[z] = part
        out_ref[ZS + z] = part


def sum_pieces(pieces):
    return pl.pallas_call(
        sum_kernel,
        out_shape=jax.ShapeDtypeStruct((2 * ZS, 24, LANES), F32),
        in_specs=[WHOLE],
        out_specs=WHOLE,
        name="sum_pieces",
    )(pieces)


def interp_weights(fine_index):
    coarse_cell = fine_index // 4
    phase_index = fine_index % 4
    lower_shift = (phase_index < 2).astype(jnp.int32)
    upper_weight = (2 * phase_index - 3 + 8 * lower_shift).astype(F32) / 8.0
    return (coarse_cell - lower_shift, upper_weight)


def build_matrix(lower_cell, upper_cell, upper_weight, count):
    columns = jnp.arange(count, dtype=jnp.int32)
    lower_part = jnp.where(columns[None, :] == lower_cell[:, None], 1.0 - upper_weight[:, None], 0.0)
    upper_portion = jnp.where(columns[None, :] == upper_cell[:, None], upper_weight[:, None], 0.0)
    return lower_part + upper_portion


def shifted(value, steps):
    return lax.ppermute(value, TILE, [(i, (i + steps) % TILES) for i in range(TILES)])


def residual_of(coarse):
    before = shifted(coarse[:, :, -1:], 1)
    after = shifted(coarse[:, :, :1], -1)
    padded = jnp.concatenate([before, coarse, after], axis=2)
    lat_lower, lat_upper_weight = interp_weights(jnp.arange(4 * LAT, dtype=jnp.int32))
    latitude_matrix = build_matrix(
        jnp.clip(lat_lower, 0, LAT - 1), jnp.clip(lat_lower + 1, 0, LAT - 1), lat_upper_weight, LAT
    )
    lon_lower, lon_upper_weight = interp_weights(jnp.arange(4 * LON_DEV, dtype=jnp.int32))
    lon_matrix = build_matrix(lon_lower + 1, lon_lower + 2, lon_upper_weight, LON_DEV + 2)
    incomplete_grid = jnp.einsum("lj,kji->kli", latitude_matrix, padded, precision=lax.Precision.HIGHEST)
    return jnp.einsum("vrb,cb->vrc", incomplete_grid, lon_matrix, precision=lax.Precision.HIGHEST)


def head_columns():
    target = jnp.arange(PADDED, dtype=jnp.int32)
    phase, channel = target // LANES, target % LANES
    source = jnp.where(channel < CHANNELS, channel * PHASES + phase, -1)
    return (jnp.arange(HEAD_OUT, dtype=jnp.int32)[:, None] == source[None, :]).astype(F32)


def gather_qkv(qkv):
    half = lax.axis_index("dp")
    qkv_half = lax.dynamic_slice_in_dim(qkv, half * HALF_QKV, HALF_QKV, 1)
    full = lax.all_gather(qkv_half, ("dp",) + FSDP, axis=0, tiled=True)
    return full.reshape(2, D, HALF_QKV)


def to_all(value, axes, count):
    copies = jnp.broadcast_to(value[None], (count,) + value.shape)
    return lax.all_to_all(copies, axes, 0, 0, tiled=True)


def gather_rest(out_w, head_w):
    out_rows = out_w.reshape(48, 12, LANES).transpose(1, 0, 2).reshape(576, LANES)
    head_pad = dot(head_w, head_columns().astype(BF16)).astype(BF16)
    head_rows = head_pad.reshape(96, PHASES, LANES).transpose(1, 0, 2).reshape(384, LANES)
    rows = jnp.concatenate([out_rows, head_rows, jnp.zeros((PIECE, LANES), BF16)], axis=0)
    own = lax.dynamic_slice_in_dim(rows, lax.axis_index(TILE) * PIECE, PIECE, 0)
    over_z = to_all(own, ("z",), ZS)
    over_tile = to_all(over_z, TILE, TILES)
    return unpack(to_all(over_tile, ("c",), CORES))


def reduce_head(pieces):
    pieces = lax.all_to_all(pieces, ("c",) + TILE, 0, 0, tiled=True)
    both = lax.all_to_all(sum_pieces(pieces), ("dp", "z"), 0, 0, tiled=True)
    spread = to_all(jnp.sum(both, axis=0), TILE, TILES)
    padded = spread.reshape(4, PHASES, 24, LANES).transpose(0, 2, 1, 3).reshape(96, PADDED)
    return lax.dot_general(
        padded, head_columns(), (((1,), (1,)), ((), ())), precision=lax.Precision.HIGHEST, preferred_element_type=F32
    )


def shards(tokens, norm_gain, query_key_value_weight, out_weight, head_weight, coarse, grad_fine):
    tokens = tokens[0].reshape(ROWS, D)
    gain = norm_gain.reshape(1, D)
    full = gather_qkv(query_key_value_weight)
    residual = residual_of(coarse[0])
    normed, rows = prepare(tokens, gain, grad_fine[0])
    out_full, head = gather_rest(out_weight, head_weight)
    grad_hidden, grad_attended = hidden_grad(rows, head, out_full)
    pairs, leading, last = project_pairs(normed, full)
    left = shifted(last, 1)
    right = shifted(leading, -1)
    queries = project(lax.optimization_barrier((normed, pairs))[0], full)
    fine_grid, pieces = forward(queries, pairs, left, right, tokens, out_full, head, rows, residual)
    grad_head = reduce_head(pieces)
    dq, dk, dv, to_left, to_right = attend_backward(queries, pairs, left, right, grad_attended)
    from_right = shifted(to_left, -1)
    from_left = shifted(to_right, 1)
    grad_tokens = norm_grad(dq, dk, dv, from_left, from_right, full, tokens, gain, grad_hidden)
    return (fine_grid[None], grad_tokens.reshape(1, LAT, LON_DEV, D), grad_head)


def solution(mesh):
    fine_mesh = Mesh(mesh.devices.reshape(2, ZS, CORES, YS, XS), ("dp", "z", "c", "y", "x"))
    samples = ("dp", "z", "c")
    placed = (
        P(samples, None, TILE, None),
        P(),
        P(FSDP, None),
        P(FSDP, None),
        P(FSDP, None),
        P(samples, None, None, TILE),
        P(samples, None, None, TILE),
    )
    return jax.shard_map(
        shards,
        mesh=fine_mesh,
        in_specs=placed,
        out_specs=(P(samples, None, None, TILE), P(samples, None, TILE, None), P(FSDP, None)),
        check_vma=False,
    )
```

time: 232 us -> 210 us (0.905)
  the two profiles are of different devices: /device:TPU:32 before, /device:TPU:2 now
where the time goes in v3:
time: 210 us; the launch traced here: 209 us
  blocking collectives  55.5 us (26%)
  Pallas kernels  46.4 us (22%)
  starting transfers between devices  42.5 us (20%)
  waiting for transfers between devices  37.3 us (18%)
  between operations  14.3 us (7%)
  local copies, waits for them, and re-layouts  8.76 us (4%)
  matrix products  3.9 us (2%)
    all_to_all x2, blocking collectives, to_all(): return lax.all_to_all(copies, axes, 0, 0, tiled=True)  32.6 us
    all_to_all x1, blocking collectives, reduce_head(): pieces = lax.all_to_all(pieces, ('c',) + TILE, 0, 0, tiled=True)  22.9 us
    all_gather x1, waiting for transfers between devices, gather_qkv(): full = lax.all_gather(qkv_half, ('dp',) + FSDP, axis=0, tiled=True)  21 us
    ppermute x6, starting transfers between devices, shifted(): lax.ppermute(value, TILE, [(i, (i + steps) % TILES) for i in range(TILES)])  18.2 us
    ppermute x6, waiting for transfers between devices, shifted(): lax.ppermute(value, TILE, [(i, (i + steps) % TILES) for i in range(TILES)])  16.3 us
    all_to_all x2, starting transfers between devices, to_all(): return lax.all_to_all(copies, axes, 0, 0, tiled=True)  16.2 us
    pallas_call x1, Pallas kernels, norm_grad(): pl.pallas_call(norm_grad_kernel, out_shape=jax.ShapeDtypeStruct((ROWS, D)...  8.8 us
    all_to_all x1, starting transfers between devices, reduce_head(): both = lax.all_to_all(sum_pieces(pieces), ('dp', 'z'), 0, 0, tiled=True)  8.05 us
  transfers between devices with their start and end apart: 10, of which 2 were waited for; matrix products, arithmetic and copies ran while one was open for 4% of the time, Pallas kernels for 18%

profile of v3, /device:TPU:2, one launch (start us, length us, event | category | flops | bytes accessed | tf_op | source)
XLA Modules:
  0.0 208.8 jit_solution(11112465464461764769)
XLA Ops:
  11.4 24.4 %all_to_all.30 = bf16[8,64,128]{2,1,0:T(8,128)(2,1)S(1)} all-to-all(bf16[8,64,128]{2,1,0:T(8,128)(2,1)S(1)} %broadcast_in_dim.86), channel_id=1, replica_groups=mesh['dp'=2,'z'=8,'c'=2,'y'=4,'x'=4] {'z'}, dimensions={0} | all-to-all | bytes 262144 | tf_op jit(solution)/shard_map/all_to_all | solution.py:520
  35.7 1.9 broadcast_in_dim.87
  37.7 7.6 %all-to-all-start.1 = ((bf16[16,8,64,128]{3,2,1,0:T(8,128)(2,1)}), bf16[16,8,64,128]{3,2,1,0:T(8,128)(2,1)S(1)}, u32[]{:S(2)}, u32[]{:S(2)}) async-start(bf16[16,8,64,128]{3,2,1,0:T(8,128)(2,1)} %broadcast_in_dim.87), calls=%async_computation.1 | async-start | bytes 4194304 | tf_op jit(solution)/shard_map/all_to_all | solution.py:520
  45.4 2.0 collective-permute-start.3
  47.4 3.8 %collective-permute-start.2 = (f32[20,8,1]{2,1,0:T(8,128)S(1)}, f32[20,8,1]{2,1,0:T(8,128)S(1)}, u32[]{:S(2)}, u32[]{:S(2)}) collective-permute-start(f32[20,8,1]{2,1,0:T(8,128)S(1)} %get-tuple-element.37), channel_id=1, source_target_pairs={{0,1},{1,2},{2,3},{3,4},{4,5},{5,6},{6,7},{7,8},{8,9},{9,10},{10,1... | collective-permute-start | bytes 1928 | tf_op jit(solution)/shard_map/ppermute | solution.py:487
  51.9 2.8 %prepare.1 = (bf16[256,1536]{1,0:T(8,128)(2,1)}, bf16[256,512]{1,0:T(8,128)(2,1)}) custom-call(bf16[256,1536]{1,0:T(8,128)(2,1)} %bitcast.39, f32[1,1536]{1,0:T(1,128)} %reshape.140.gain_ref, f32[20,32,128]{2,1,0:T(8,128)} %bitcast.50), custom_call_target="tpu_custom_call" | custom-call | tf_op jit(solution)/shard_map/prepare/pallas_call | solution.py:84
  54.6 16.3 %collective-permute-done.3 = f32[20,8,1]{2,1,0:T(8,128)S(1)} collective-permute-done((f32[20,8,1]{2,1,0:T(8,128)S(1)}, f32[20,8,1]{2,1,0:T(8,128)S(1)}, u32[]{:S(2)}, u32[]{:S(2)}) %collective-permute-start.3) | collective-permute-done | bytes 672 | tf_op jit(solution)/shard_map/ppermute | solution.py:487
  71.5 21.0 %all-gather.2.cloned.1.call-done = bf16[3072,1152]{1,0:T(8,128)(2,1)} async-done(((bf16[96,1152]{1,0:T(8,128)(2,1)}), bf16[3072,1152]{1,0:T(8,128)(2,1)}) %all-gather.2.cloned.1.call-update) | async-done | bytes 7077904 | tf_op jit(solution)/shard_map/all_gather | solution.py:514
  92.4 5.5 %project_pairs.1 = (bf16[256,1536]{1,0:T(8,128)(2,1)}, bf16[64,1536]{1,0:T(8,128)(2,1)}, bf16[64,1536]{1,0:T(8,128)(2,1)}) custom-call(bf16[256,1536]{1,0:T(8,128)(2,1)} %get-tuple-element.22.normed_ref, bf16[2,1536,1152]{2,1,0:T(8,128)(2,1)} %bitcast.35), custom_call_target="tpu_custom_call" | custom-call | tf_op jit(solution)/shard_map/project_pairs/pallas_call | solution.py:128
  97.9 3.4 %collective-permute-start = (bf16[64,1536]{1,0:T(8,128)(2,1)}, bf16[64,1536]{1,0:T(8,128)(2,1)S(1)}, u32[]{:S(2)}, u32[]{:S(2)}) collective-permute-start(bf16[64,1536]{1,0:T(8,128)(2,1)} %get-tuple-element.23), channel_id=1, source_target_pairs={{0,1},{1,2},{2,3},{3,4},{4,5},{5,6},{6,7},{7,8},{8,9},{9,10},{10,1... | collective-permute-start | bytes 589832 | tf_op jit(solution)/shard_map/ppermute | solution.py:487
  101.3 2.5 %collective-permute-start.1 = (bf16[64,1536]{1,0:T(8,128)(2,1)}, bf16[64,1536]{1,0:T(8,128)(2,1)S(1)}, u32[]{:S(2)}, u32[]{:S(2)}) collective-permute-start(bf16[64,1536]{1,0:T(8,128)(2,1)} %get-tuple-element.24), channel_id=1, source_target_pairs={{0,15},{1,0},{2,1},{3,2},{4,3},{5,4},{6,5},{7,6},{8,7},{9,8},{10,9... | collective-permute-start | bytes 589832 | tf_op jit(solution)/shard_map/ppermute | solution.py:487
  106.0 8.2 %all_to_all.31.pieces_ref = bf16[2,16,8,64,128]{4,3,2,1,0:T(8,128)(2,1)} all-to-all(bf16[2,16,8,64,128]{4,3,2,1,0:T(8,128)(2,1)S(1)} %broadcast_in_dim.88), channel_id=1, replica_groups=mesh['dp'=2,'z'=8,'c'=2,'y'=4,'x'=4] {'c'}, dimensions={0} | all-to-all | bytes 8388608 | tf_op jit(solution)/shard_map/all_to_all | solution.py:520
  114.2 4.8 %unpack.1 = (bf16[768,1536]{1,0:T(8,128)(2,1)}, bf16[1536,512]{1,0:T(8,128)(2,1)}) custom-call(bf16[2,16,8,64,128]{4,3,2,1,0:T(8,128)(2,1)} %all_to_all.31.pieces_ref), custom_call_target="tpu_custom_call" | custom-call | tf_op jit(solution)/shard_map/unpack/pallas_call | solution.py:158
  119.1 3.4 %project.1.q_ref = bf16[256,768]{1,0:T(8,128)(2,1)} custom-call(bf16[256,1536]{1,0:T(8,128)(2,1)} %get-tuple-element.22.normed_ref, bf16[2,1536,1152]{2,1,0:T(8,128)(2,1)} %bitcast.36), custom_call_target="tpu_custom_call" | custom-call | tf_op jit(solution)/shard_map/project/pallas_call | solution.py:116
  123.2 7.6 %forward.1 = (f32[20,32,128]{2,1,0:T(8,128)}, bf16[32,24,640]{2,1,0:T(8,128)(2,1)}) custom-call(bf16[256,768]{1,0:T(8,128)(2,1)} %project.1.q_ref, bf16[256,1536]{1,0:T(8,128)(2,1)} %get-tuple-element.21.k_ref.v_ref, bf16[256,1536]{1,0:T(8,128)(2,1)} %get-tuple-element.21.k_ref.v_ref, bf16[64,1536]{1,0:T(8,128)(2,1)} %copy-done.1, ...), custom_call_target="tpu_custom_call" | custom-call | tf_op jit(solution)/shard_map/forward/pallas_call | solution.py:300
  130.8 22.9 %all_to_all.32.pieces_ref = bf16[32,24,640]{2,1,0:T(8,128)(2,1)} all-to-all(bf16[32,24,640]{2,1,0:T(8,128)(2,1)} %get-tuple-element.36), channel_id=1, replica_groups=mesh['dp'=2,'z'=8,'c'=2,'y'=4,'x'=4] {'c','y','x'}, dimensions={0} | all-to-all | bytes 1966080 | tf_op jit(solution)/shard_map/all_to_all | solution.py:535
  153.7 2.1 %sum_pieces.1 = f32[16,24,128]{2,1,0:T(8,128)} custom-call(bf16[32,24,640]{2,1,0:T(8,128)(2,1)} %all_to_all.32.pieces_ref), custom_call_target="tpu_custom_call" | custom-call | tf_op jit(solution)/shard_map/sum_pieces/pallas_call | solution.py:462
  155.8 8.0 %all-to-all-start.4 = ((f32[16,24,128]{2,1,0:T(8,128)}), f32[16,24,128]{2,1,0:T(8,128)S(1)}, u32[]{:S(2)}, u32[]{:S(2)}) async-start(f32[16,24,128]{2,1,0:T(8,128)} %sum_pieces.1), calls=%async_computation.4 | async-start | bytes 393216 | tf_op jit(solution)/shard_map/all_to_all | solution.py:536
  163.9 4.3 %hidden_grad.1 = (f32[256,1536]{1,0:T(8,128)}, bf16[256,768]{1,0:T(8,128)(2,1)}) custom-call(bf16[256,512]{1,0:T(8,128)(2,1)} %get-tuple-element.27.rows_hbm.rows_ref, bf16[1536,512]{1,0:T(8,128)(2,1)} %get-tuple-element.26.head_hbm.head_ref, bf16[768,1536]{1,0:T(8,128)(2,1)} %get-tuple-element.25.out_hbm.out_ref), custom_call_target="tpu_custom_call" | custom-call | tf_op jit(solution)/shard_map/hidden_grad/pallas_call | solution.py:177
  168.2 7.1 %attend_backward.1 = (bf16[256,768]{1,0:T(8,128)(2,1)}, f32[256,768]{1,0:T(8,128)}, f32[256,768]{1,0:T(8,128)}, bf16[2,64,768]{2,1,0:T(8,128)(2,1)}, bf16[2,64,768]{2,1,0:T(8,128)(2,1)}) custom-call(bf16[256,768]{1,0:T(8,128)(2,1)} %project.1.q_ref, bf16[256,1536]{1,0:T(8,128)(2,1)} %get-tuple-element.21.k_ref.v_ref, ...), custom_call_target="tpu_custom_call" | custom-call | tf_op jit(solution)/shard_map/attend_backward/pallas_call | solution.py:366
  175.3 3.5 %collective-permute-start.4 = (bf16[2,64,768]{2,1,0:T(8,128)(2,1)}, bf16[2,64,768]{2,1,0:T(8,128)(2,1)S(1)}, u32[]{:S(2)}, u32[]{:S(2)}) collective-permute-start(bf16[2,64,768]{2,1,0:T(8,128)(2,1)} %get-tuple-element.33), channel_id=1, source_target_pairs={{0,1},{1,2},{2,3},{3,4},{4,5},{5,6},{6,7},{7,8},{8,9},{9,10},{10,1... | collective-permute-start | bytes 589832 | tf_op jit(solution)/shard_map/ppermute | solution.py:487
  178.8 3.0 %collective-permute-start.5 = (bf16[2,64,768]{2,1,0:T(8,128)(2,1)}, bf16[2,64,768]{2,1,0:T(8,128)(2,1)S(1)}, u32[]{:S(2)}, u32[]{:S(2)}) collective-permute-start(bf16[2,64,768]{2,1,0:T(8,128)(2,1)} %get-tuple-element.34), channel_id=1, source_target_pairs={{0,15},{1,0},{2,1},{3,2},{4,3},{5,4},{6,5},{7,6},{8,7},{9,8},{10,9... | collective-permute-start | bytes 589832 | tf_op jit(solution)/shard_map/ppermute | solution.py:487
  182.5 8.6 %all-to-all-start.5 = ((f32[16,24,128]{2,1,0:T(8,128)}), f32[16,24,128]{2,1,0:T(8,128)S(1)}, u32[]{:S(2)}, u32[]{:S(2)}) async-start(f32[16,24,128]{2,1,0:T(8,128)} %broadcast_in_dim.96), calls=%async_computation.5 | async-start | bytes 393216 | tf_op jit(solution)/shard_map/all_to_all | solution.py:520
  192.0 8.8 %norm_grad.1 = bf16[256,1536]{1,0:T(8,128)(2,1)} custom-call(bf16[256,768]{1,0:T(8,128)(2,1)} %get-tuple-element.30.dq_ref, f32[256,768]{1,0:T(8,128)} %get-tuple-element.31.dk_ref, f32[256,768]{1,0:T(8,128)} %get-tuple-element.32.dv_ref, bf16[2,64,768]{2,1,0:T(8,128)(2,1)} %copy-done.4, bf16[2,64,768]{2,1,0:T(8,128)(2,1)} %copy-done.5, ...), custom_call_target="tpu_custom_call" | custom-call | tf_op jit(solution)/shard_map/norm_grad/pallas_call | solution.py:422
  (47 shorter events, 11.0 us)
Async XLA Ops:
  7.2 1.0 copy-start
  7.2 85.3 %all-gather.2.cloned.1.call-start = ((), (), s32[]{:S(2)}) async-start(), calls=%async_computation.6 | async-start | bytes 7299072 | tf_op jit(solution)/shard_map/all_gather | solution.py:514
  37.7 7.6 %copy-start.3 = (f32[1,20,8,32]{3,2,1,0:T(8,128)S(1)}, f32[1,20,8,32]{3,2,1,0:T(8,128)}, u32[]{:S(2)}) copy-start(f32[1,20,8,32]{3,2,1,0:T(8,128)} %param.12) | copy-start | bytes 61444
  37.7 13.6 %copy-start.6 = (f32[1536]{0:T(1024)S(1)}, f32[1536]{0:T(1024)}, u32[]{:S(2)}) copy-start(f32[1536]{0:T(1024)} %param.8) | copy-start | bytes 18436
  37.7 67.3 %all-to-all-start.1 = ((bf16[16,8,64,128]{3,2,1,0:T(8,128)(2,1)}), bf16[16,8,64,128]{3,2,1,0:T(8,128)(2,1)S(1)}, u32[]{:S(2)}, u32[]{:S(2)}) async-start(bf16[16,8,64,128]{3,2,1,0:T(8,128)(2,1)} %broadcast_in_dim.87), calls=%async_computation.1 | async-start | bytes 4194304 | tf_op jit(solution)/shard_map/all_to_all | solution.py:520
  45.4 25.6 %collective-permute-start.3 = (f32[20,8,1]{2,1,0:T(8,128)S(1)}, f32[20,8,1]{2,1,0:T(8,128)S(1)}, u32[]{:S(2)}, u32[]{:S(2)}) collective-permute-start(f32[20,8,1]{2,1,0:T(8,128)S(1)} %get-tuple-element.38), channel_id=1, source_target_pairs={{0,15},{1,0},{2,1},{3,2},{4,3},{5,4},{6,5},{7,6},{8,7},{9,8},{10,9... | collective-permute-start | bytes 1928 | tf_op jit(solution)/shard_map/ppermute | solution.py:487
  47.4 23.6 %collective-permute-start.2 = (f32[20,8,1]{2,1,0:T(8,128)S(1)}, f32[20,8,1]{2,1,0:T(8,128)S(1)}, u32[]{:S(2)}, u32[]{:S(2)}) collective-permute-start(f32[20,8,1]{2,1,0:T(8,128)S(1)} %get-tuple-element.37), channel_id=1, source_target_pairs={{0,1},{1,2},{2,3},{3,4},{4,5},{5,6},{6,7},{7,8},{8,9},{9,10},{10,1... | collective-permute-start | bytes 1928 | tf_op jit(solution)/shard_map/ppermute | solution.py:487
  97.9 24.5 %collective-permute-start = (bf16[64,1536]{1,0:T(8,128)(2,1)}, bf16[64,1536]{1,0:T(8,128)(2,1)S(1)}, u32[]{:S(2)}, u32[]{:S(2)}) collective-permute-start(bf16[64,1536]{1,0:T(8,128)(2,1)} %get-tuple-element.23), channel_id=1, source_target_pairs={{0,1},{1,2},{2,3},{3,4},{4,5},{5,6},{6,7},{7,8},{8,9},{9,10},{10,1... | collective-permute-start | bytes 589832 | tf_op jit(solution)/shard_map/ppermute | solution.py:487
  101.3 21.2 %collective-permute-start.1 = (bf16[64,1536]{1,0:T(8,128)(2,1)}, bf16[64,1536]{1,0:T(8,128)(2,1)S(1)}, u32[]{:S(2)}, u32[]{:S(2)}) collective-permute-start(bf16[64,1536]{1,0:T(8,128)(2,1)} %get-tuple-element.24), channel_id=1, source_target_pairs={{0,15},{1,0},{2,1},{3,2},{4,3},{5,4},{6,5},{7,6},{8,7},{9,8},{10,9... | collective-permute-start | bytes 589832 | tf_op jit(solution)/shard_map/ppermute | solution.py:487
  122.4 0.7 copy-start.1
  122.5 0.7 copy-start.2
  155.8 26.0 %all-to-all-start.4 = ((f32[16,24,128]{2,1,0:T(8,128)}), f32[16,24,128]{2,1,0:T(8,128)S(1)}, u32[]{:S(2)}, u32[]{:S(2)}) async-start(f32[16,24,128]{2,1,0:T(8,128)} %sum_pieces.1), calls=%async_computation.4 | async-start | bytes 393216 | tf_op jit(solution)/shard_map/all_to_all | solution.py:536
  175.3 15.9 %collective-permute-start.4 = (bf16[2,64,768]{2,1,0:T(8,128)(2,1)}, bf16[2,64,768]{2,1,0:T(8,128)(2,1)S(1)}, u32[]{:S(2)}, u32[]{:S(2)}) collective-permute-start(bf16[2,64,768]{2,1,0:T(8,128)(2,1)} %get-tuple-element.33), channel_id=1, source_target_pairs={{0,1},{1,2},{2,3},{3,4},{4,5},{5,6},{6,7},{7,8},{8,9},{9,10},{10,1... | collective-permute-start | bytes 589832 | tf_op jit(solution)/shard_map/ppermute | solution.py:487
  178.8 12.4 %collective-permute-start.5 = (bf16[2,64,768]{2,1,0:T(8,128)(2,1)}, bf16[2,64,768]{2,1,0:T(8,128)(2,1)S(1)}, u32[]{:S(2)}, u32[]{:S(2)}) collective-permute-start(bf16[2,64,768]{2,1,0:T(8,128)(2,1)} %get-tuple-element.34), channel_id=1, source_target_pairs={{0,15},{1,0},{2,1},{3,2},{4,3},{5,4},{6,5},{7,6},{8,7},{9,8},{10,9... | collective-permute-start | bytes 589832 | tf_op jit(solution)/shard_map/ppermute | solution.py:487
  182.5 18.2 %all-to-all-start.5 = ((f32[16,24,128]{2,1,0:T(8,128)}), f32[16,24,128]{2,1,0:T(8,128)S(1)}, u32[]{:S(2)}, u32[]{:S(2)}) async-start(f32[16,24,128]{2,1,0:T(8,128)} %broadcast_in_dim.96), calls=%async_computation.5 | async-start | bytes 393216 | tf_op jit(solution)/shard_map/all_to_all | solution.py:520
  191.2 0.7 copy-start.4
  191.2 0.7 copy-start.5
Sparse Core Ops, SparseCore 0:
  10.7 81.7 all-gather.1

commit v4 on v3

--- a/solution.py
+++ b/solution.py
@@ -18,6 +18,7 @@
 HEAD_OUT = 320
 ROWS = 256
 EDGE = 64
+KEYS = ROWS + 2 * EDGE
 GROUP = 384
 PAIR = 2 * INNER
 ZS = 8
@@ -30,6 +31,7 @@
 HALF_QKV = 1152
 HALF_OUT = 768
 PIECE = 64
+UNPACK = 4
 WIDE = ZS * 80
 PHASES = 4
 CHANNELS = 80
@@ -61,13 +63,18 @@
     return jnp.where(lane == target, 1.0, 0.0).astype(BF16)
 
 
-def prepare_kernel(tokens_ref, gain_ref, fine_ref, normed_ref, rows_ref):
-    values = tokens_ref[...].astype(F32)
+def standardized(values):
     average = jnp.mean(values, axis=-1, keepdims=True)
     centred = values - average
     variance = jnp.mean(centred * centred, axis=-1, keepdims=True)
-    standard = centred * lax.rsqrt(variance + EPSILON)
-    normed_ref[...] = (standard * gain_ref[...]).astype(BF16)
+    inverse_dev = lax.rsqrt(variance + EPSILON)
+    return centred * inverse_dev, inverse_dev
+
+
+def prepare_kernel(tokens_ref, left_ref, right_ref, gain_ref, fine_ref, normed_ref, rows_ref):
+    for source, first in ((tokens_ref, 0), (left_ref, ROWS), (right_ref, ROWS + EDGE)):
+        standard, _ = standardized(source[...].astype(F32))
+        normed_ref[first : first + source.shape[0]] = (standard * gain_ref[...]).astype(BF16)
     select = spread_matrix()
     empty = jnp.zeros((LANES - CHANNELS, LANES), BF16)
     for lat in range(LAT):
@@ -80,91 +87,50 @@
             ]
 
 
-def prepare(tokens, gain, grad_fine):
+def prepare(tokens, left, right, gain, grad_fine):
     return pl.pallas_call(
         prepare_kernel,
         out_shape=(
-            jax.ShapeDtypeStruct((ROWS, D), BF16),
+            jax.ShapeDtypeStruct((KEYS, D), BF16),
             jax.ShapeDtypeStruct((ROWS, PADDED), BF16),
         ),
-        in_specs=[WHOLE, WHOLE, WHOLE],
+        in_specs=[WHOLE] * 5,
         out_specs=(WHOLE, WHOLE),
         name="prepare",
-    )(tokens, gain, grad_fine)
-
-
-def project_kernel(normed_ref, weight_ref, out_ref):
-    out_ref[...] = dot(normed_ref[...], weight_ref[0]).astype(BF16)
-
-
-def project_pairs_kernel(normed_ref, weight_ref, out_ref, leading_ref, last_ref):
-    values = dot(normed_ref[...], weight_ref[0])
-    out_ref[...] = values.astype(BF16)
-    grid = values.reshape(LAT, LON_DEV, GROUP)
-    leading_ref[...] = grid[:, :MARGIN].reshape(EDGE, GROUP).astype(BF16)
-    last_ref[...] = grid[:, LON_DEV - MARGIN :].reshape(EDGE, GROUP).astype(BF16)
-
-
-def project_specs(first):
-    return [
-        pl.BlockSpec((ROWS, D), lambda n: (0, 0)),
-        pl.BlockSpec((1, D, GROUP), lambda n: ((n + first) // 3, 0, (n + first) % 3)),
-    ]
-
-
-def project(normed, full):
-    return pl.pallas_call(
-        project_kernel,
-        out_shape=jax.ShapeDtypeStruct((ROWS, INNER), BF16),
-        grid=(2,),
-        in_specs=project_specs(0),
-        out_specs=pl.BlockSpec((ROWS, GROUP), lambda n: (0, n)),
-        name="project",
-    )(normed, full)
-
-
-def project_pairs(normed, full):
-    edge = jax.ShapeDtypeStruct((EDGE, PAIR), BF16)
-    return pl.pallas_call(
-        project_pairs_kernel,
-        out_shape=(jax.ShapeDtypeStruct((ROWS, PAIR), BF16), edge, edge),
-        grid=(4,),
-        in_specs=project_specs(2),
-        out_specs=(
-            pl.BlockSpec((ROWS, GROUP), lambda n: (0, n)),
-            pl.BlockSpec((EDGE, GROUP), lambda n: (0, n)),
-            pl.BlockSpec((EDGE, GROUP), lambda n: (0, n)),
-        ),
-        name="project_pairs",
-    )(normed, full)
-
-
-def unpack_kernel(pieces_ref, out_ref, head_ref):
-    for core in range(CORES):
-        for z in range(ZS):
-            shard = z * CORES + core
-            for tile in range(60):
-                block = pieces_ref[core, tile // 4, z, tile % 4 * 16 : (tile % 4 + 1) * 16, :]
+    )(tokens, left, right, gain, grad_fine)
+
+
+def unpack_kernel(core_ref, own_ref, other_ref, out_ref, head_ref):
+    core = core_ref[0]
+    for source, place in ((own_ref, core), (other_ref, 1 - core)):
+        for tile in range(60):
+            for z in range(UNPACK):
+                block = source[tile // 4, z, tile % 4 * 16 : (tile % 4 + 1) * 16, :]
                 if tile < 36:
-                    top = shard * 48 + tile % 3 * 16
-                    out_ref[top : top + 16, tile // 3 * LANES : (tile // 3 + 1) * LANES] = block
+                    top = pl.multiple_of(z * 96 + place * 48 + tile % 3 * 16, 16)
+                    out_ref[pl.ds(top, 16), tile // 3 * LANES : (tile // 3 + 1) * LANES] = block
                 else:
-                    top = shard * 96 + tile % 6 * 16
+                    top = pl.multiple_of(z * 192 + place * 96 + tile % 6 * 16, 16)
                     phase = (tile - 36) // 6
-                    head_ref[top : top + 16, phase * LANES : (phase + 1) * LANES] = block
-
-
-def unpack(pieces):
+                    head_ref[pl.ds(top, 16), phase * LANES : (phase + 1) * LANES] = block
+
+
+def unpack(core, own, other):
+    block = pl.BlockSpec((TILES, UNPACK, PIECE, LANES), lambda z: (0, z, 0, 0))
     return pl.pallas_call(
         unpack_kernel,
         out_shape=(
             jax.ShapeDtypeStruct((INNER, D), BF16),
             jax.ShapeDtypeStruct((D, PADDED), BF16),
         ),
-        in_specs=[WHOLE],
-        out_specs=(WHOLE, WHOLE),
+        grid=(ZS // UNPACK,),
+        in_specs=[pl.BlockSpec(memory_space=pltpu.SMEM), block, block],
+        out_specs=(
+            pl.BlockSpec((UNPACK * 96, D), lambda z: (z, 0)),
+            pl.BlockSpec((UNPACK * 192, PADDED), lambda z: (z, 0)),
+        ),
         name="unpack",
-    )(pieces)
+    )(core, own, other)
 
 
 def hidden_grad_kernel(rows_ref, head_ref, out_ref, hidden_ref, attended_ref):
@@ -209,14 +175,7 @@
     return exponent / jnp.sum(exponent, axis=-1, keepdims=True)
 
 
-def joined(own_ref, left_ref, right_ref):
-    return jnp.concatenate([own_ref[...], left_ref[...], right_ref[...]], axis=0)
-
-
-def forward_group(q_ref, k_ref, v_ref, kl_ref, vl_ref, kr_ref, vr_ref):
-    queries = q_ref[...]
-    keys = joined(k_ref, kl_ref, kr_ref)
-    values = joined(v_ref, vl_ref, vr_ref)
+def forward_group(queries, keys, values):
     parts = [None, None, None]
     for head in range(4):
         first, last, inside = head_window(head)
@@ -229,10 +188,10 @@
 
 
 def forward_kernel(
-    q_ref, k_ref, v_ref, kl_ref, vl_ref, kr_ref, vr_ref,
+    normed_ref, weight_ref,
     tokens_hbm, out_hbm, head_hbm, rows_hbm, residual_hbm,
-    fine_ref, pieces_ref,
-    attended, tokens_ref, out_ref, head_ref, rows_ref, residual_ref, products, sems,
+    projected_ref, fine_ref, pieces_ref,
+    tokens_ref, out_ref, head_ref, rows_ref, residual_ref, products, sems,
 ):
     step = pl.program_id(0)
     copies = [
@@ -248,15 +207,25 @@
         )
     ]
 
-    @pl.when(step == 0)
+    @pl.when(step == 3)
     def _():
         for copy in copies:
             copy.start()
 
-    attended[step] = forward_group(q_ref, k_ref, v_ref, kl_ref, vl_ref, kr_ref, vr_ref)
-
-    @pl.when(step == 1)
+    @pl.when(step < 2)
     def _():
+        projected_ref[step, :ROWS] = dot(normed_ref[:ROWS], weight_ref[0]).astype(BF16)
+
+    @pl.when(step >= 2)
+    def _():
+        projected_ref[step] = dot(normed_ref[...], weight_ref[0]).astype(BF16)
+
+    @pl.when(step == 5)
+    def _():
+        attended = [
+            forward_group(projected_ref[group, :ROWS], projected_ref[2 + group], projected_ref[4 + group])
+            for group in range(2)
+        ]
         for copy in copies:
             copy.wait()
         mixed = dot(attended[0], out_ref[:GROUP]) + dot(attended[1], out_ref[GROUP:])
@@ -287,24 +256,25 @@
             fine_ref[:, across, :] = spread[:CHANNELS].reshape(VARS, PHASES, LANES) + residual_ref[:, across, :]
 
 
-def attention_specs():
-    def spec(rows, offset):
-        return pl.BlockSpec((rows, GROUP), lambda n: (0, n + offset))
-
-    return [spec(ROWS, 0), spec(ROWS, 0), spec(ROWS, 2), spec(EDGE, 0), spec(EDGE, 2), spec(EDGE, 0), spec(EDGE, 2)]
-
-
-def forward(queries, pairs, left, right, tokens, out_weight, head, rows, residual):
+def forward(normed, full, tokens, out_weight, head, rows, residual):
     fine = (VARS, 4 * LAT, LANES)
     pieces = (CORES * TILES, 24, WIDE)
+    projected = (6, KEYS, GROUP)
     return pl.pallas_call(
         forward_kernel,
-        out_shape=(jax.ShapeDtypeStruct(fine, F32), jax.ShapeDtypeStruct(pieces, BF16)),
-        grid=(2,),
-        in_specs=attention_specs() + [pl.BlockSpec(memory_space=pl.ANY)] * 5,
-        out_specs=(whole_block(fine), whole_block(pieces)),
+        out_shape=(
+            jax.ShapeDtypeStruct(projected, BF16),
+            jax.ShapeDtypeStruct(fine, F32),
+            jax.ShapeDtypeStruct(pieces, BF16),
+        ),
+        grid=(6,),
+        in_specs=[
+            whole_block((KEYS, D)),
+            pl.BlockSpec((1, D, GROUP), lambda n: (n // 3, 0, n % 3)),
+        ]
+        + [pl.BlockSpec(memory_space=pl.ANY)] * 5,
+        out_specs=(whole_block(projected), whole_block(fine), whole_block(pieces)),
         scratch_shapes=[
-            pltpu.VMEM((2, ROWS, GROUP), BF16),
             pltpu.VMEM((ROWS, D), BF16),
             pltpu.VMEM((INNER, D), BF16),
             pltpu.VMEM((D, PADDED), BF16),
@@ -314,17 +284,17 @@
             pltpu.SemaphoreType.DMA((5,)),
         ],
         name="forward",
-    )(queries, pairs, pairs, left, left, right, right, tokens, out_weight, head, rows, residual)
+    )(normed, full, tokens, out_weight, head, rows, residual)
 
 
 def backward_kernel(
-    q_ref, k_ref, v_ref, kl_ref, vl_ref, kr_ref, vr_ref, grad_ref,
+    q_ref, k_ref, v_ref, grad_ref,
     dq_ref, dk_ref, dv_ref, left_ref, right_ref,
 ):
-    queries = q_ref[...]
+    queries = q_ref[0, :ROWS]
     grads = grad_ref[...]
-    keys = joined(k_ref, kl_ref, kr_ref)
-    values = joined(v_ref, vl_ref, vr_ref)
+    keys = k_ref[0]
+    values = v_ref[0]
     sums = [[None, None, None] for _ in range(3)]
     for head in range(4):
         first, last, inside = head_window(head)
@@ -354,7 +324,7 @@
             right_ref[kind, :, at] = grads_of[ROWS + EDGE :].astype(BF16)
 
 
-def attend_backward(queries, pairs, left, right, grad_attended):
+def attend_backward(projected, grad_attended):
     def block(rows):
         return pl.BlockSpec((rows, GROUP), lambda n: (0, n))
 
@@ -367,10 +337,11 @@
         backward_kernel,
         out_shape=(shape(ROWS, BF16), shape(ROWS, F32), shape(ROWS, F32), edge, edge),
         grid=(2,),
-        in_specs=attention_specs() + [block(ROWS)],
+        in_specs=[pl.BlockSpec((1, KEYS, GROUP), lambda n, first=first: (first + n, 0, 0)) for first in (0, 2, 4)]
+        + [block(ROWS)],
         out_specs=(block(ROWS), block(ROWS), block(ROWS), edge_block, edge_block),
         name="attend_backward",
-    )(queries, pairs, pairs, left, left, right, right, grad_attended)
+    )(projected, projected, projected, grad_attended)
 
 
 def norm_grad_kernel(
@@ -406,11 +377,7 @@
         for copy in copies:
             copy.wait()
         values = tokens_ref[...].astype(F32)
-        average = jnp.mean(values, axis=-1, keepdims=True)
-        centred = values - average
-        variance = jnp.mean(centred * centred, axis=-1, keepdims=True)
-        inverse_dev = lax.rsqrt(variance + EPSILON)
-        standard = centred * inverse_dev
+        standard, inverse_dev = standardized(values)
         grad_standard = total[...] * gain_ref[...]
         first_mean = jnp.mean(grad_standard, axis=-1, keepdims=True)
         second_mean = jnp.mean(grad_standard * standard, axis=-1, keepdims=True)
@@ -520,7 +487,7 @@
     return lax.all_to_all(copies, axes, 0, 0, tiled=True)
 
 
-def gather_rest(out_w, head_w):
+def gather_rest(out_w, head_w, ready):
     out_rows = out_w.reshape(48, 12, LANES).transpose(1, 0, 2).reshape(576, LANES)
     head_pad = dot(head_w, head_columns().astype(BF16)).astype(BF16)
     head_rows = head_pad.reshape(96, PHASES, LANES).transpose(1, 0, 2).reshape(384, LANES)
@@ -528,7 +495,9 @@
     own = lax.dynamic_slice_in_dim(rows, lax.axis_index(TILE) * PIECE, PIECE, 0)
     over_z = to_all(own, ("z",), ZS)
     over_tile = to_all(over_z, TILE, TILES)
-    return unpack(to_all(over_tile, ("c",), CORES))
+    over_tile = lax.optimization_barrier((over_tile, ready))[0]
+    other = lax.ppermute(over_tile, "c", [(0, 1), (1, 0)])
+    return unpack(lax.axis_index("c").reshape(1).astype(jnp.int32), over_tile, other)
 
 
 def reduce_head(pieces):
@@ -545,17 +514,19 @@
     tokens = tokens[0].reshape(ROWS, D)
     gain = norm_gain.reshape(1, D)
     full = gather_qkv(query_key_value_weight)
+    grid = tokens.reshape(LAT, LON_DEV, D)
+    left = shifted(grid[:, LON_DEV - MARGIN :].reshape(EDGE, D), 1)
+    right = shifted(grid[:, :MARGIN].reshape(EDGE, D), -1)
     residual = residual_of(coarse[0])
-    normed, rows = prepare(tokens, gain, grad_fine[0])
-    out_full, head = gather_rest(out_weight, head_weight)
+    normed, rows = prepare(tokens, left, right, gain, grad_fine[0])
+    out_full, head = gather_rest(out_weight, head_weight, (normed, residual))
     grad_hidden, grad_attended = hidden_grad(rows, head, out_full)
-    pairs, leading, last = project_pairs(normed, full)
-    left = shifted(last, 1)
-    right = shifted(leading, -1)
-    queries = project(lax.optimization_barrier((normed, pairs))[0], full)
-    fine_grid, pieces = forward(queries, pairs, left, right, tokens, out_full, head, rows, residual)
+    full, grad_hidden, grad_attended, residual = lax.optimization_barrier(
+        (full, grad_hidden, grad_attended, residual)
+    )
+    projected, fine_grid, pieces = forward(normed, full, tokens, out_full, head, rows, residual)
     grad_head = reduce_head(pieces)
-    dq, dk, dv, to_left, to_right = attend_backward(queries, pairs, left, right, grad_attended)
+    dq, dk, dv, to_left, to_right = attend_backward(projected, grad_attended)
     from_right = shifted(to_left, -1)
     from_left = shifted(to_right, 1)
     grad_tokens = norm_grad(dq, dk, dv, from_left, from_right, full, tokens, gain, grad_hidden)

time: 210 us -> 182 us (0.87)
  waiting for transfers between devices: 37.3 us -> 20.8 us
  blocking collectives: 55.5 us -> 46.5 us
    all_gather x1, waiting for transfers between devices: 21 us -> 0.01 us  [gather_qkv(): full = lax.all_gather(qkv_half, ('dp',) + FSDP, axis=0, tiled=True)]
    all_to_all x2 -> x1, blocking collectives: 32.6 us -> 24.4 us  [to_all(): return lax.all_to_all(copies, axes, 0, 0, tiled=True)]
    ppermute x0 -> x1, waiting for transfers between devices: none -> 4.33 us  [gather_rest(): other = lax.ppermute(over_tile, 'c', [(0, 1), (1, 0)])]
    pallas_call x4 -> x2, Pallas kernels: 19.2 us -> 18.1 us  [the longest x1 14.7 us: forward(): pl.pallas_call(forward_kernel, out_shape=(jax.ShapeDtypeStruct(projected,...]
  transfers between devices with their start and end apart: 10 -> 11, of which waited for: 2 -> 5; matrix products, arithmetic and copies ran while one was open for 4% -> 4% of each run, Pallas kernels for 18% -> 15%
where the time goes in v4:
time: 182 us; the launch traced here: 181 us
  blocking collectives  46.5 us (26%)
  Pallas kernels  44.4 us (24%)
  starting transfers between devices  43.5 us (24%)
  waiting for transfers between devices  20.8 us (11%)
  between operations  14.3 us (8%)
  local copies, waits for them, and re-layouts  7.7 us (4%)
  matrix products  3.88 us (2%)
    all_to_all x1, blocking collectives, to_all(): return lax.all_to_all(copies, axes, 0, 0, tiled=True)  24.4 us
    all_to_all x1, blocking collectives, reduce_head(): pieces = lax.all_to_all(pieces, ('c',) + TILE, 0, 0, tiled=True)  22.1 us
    ppermute x6, starting transfers between devices, shifted(): lax.ppermute(value, TILE, [(i, (i + steps) % TILES) for i in range(TILES)])  19.6 us
    pallas_call x1, Pallas kernels, forward(): pl.pallas_call(forward_kernel, out_shape=(jax.ShapeDtypeStruct(projected,...  14.7 us
    ppermute x6, waiting for transfers between devices, shifted(): lax.ppermute(value, TILE, [(i, (i + steps) % TILES) for i in range(TILES)])  14.3 us
    all_to_all x2, starting transfers between devices, to_all(): return lax.all_to_all(copies, axes, 0, 0, tiled=True)  14.2 us
    pallas_call x1, Pallas kernels, norm_grad(): pl.pallas_call(norm_grad_kernel, out_shape=jax.ShapeDtypeStruct((ROWS, D)...  8.8 us
    all_to_all x1, starting transfers between devices, reduce_head(): both = lax.all_to_all(sum_pieces(pieces), ('dp', 'z'), 0, 0, tiled=True)  7.74 us
  transfers between devices with their start and end apart: 11, of which 5 were waited for; matrix products, arithmetic and copies ran while one was open for 4% of the time, Pallas kernels for 15%

profile of v4, /device:TPU:2, one launch (start us, length us, event | category | flops | bytes accessed | tf_op | source)
XLA Modules:
  0.0 181.1 jit_solution(11622924837762487692)
XLA Ops:
  11.4 24.4 %all_to_all.25 = bf16[8,64,128]{2,1,0:T(8,128)(2,1)S(1)} all-to-all(bf16[8,64,128]{2,1,0:T(8,128)(2,1)S(1)} %broadcast_in_dim.80), channel_id=1, replica_groups=mesh['dp'=2,'z'=8,'c'=2,'y'=4,'x'=4] {'z'}, dimensions={0} | all-to-all | bytes 262144 | tf_op jit(solution)/shard_map/all_to_all | solution.py:487
  35.7 1.9 %broadcast_in_dim.81 = bf16[16,8,64,128]{3,2,1,0:T(8,128)(2,1)} broadcast(bf16[8,64,128]{2,1,0:T(8,128)(2,1)S(1)} %all_to_all.25), dimensions={1,2,3} | broadcast | bytes 2228224 | tf_op jit(solution)/shard_map/broadcast_in_dim | solution.py:486
  37.6 7.6 %all-to-all-start.1 = ((bf16[16,8,64,128]{3,2,1,0:T(8,128)(2,1)}), bf16[16,8,64,128]{3,2,1,0:T(8,128)(2,1)S(1)}, u32[]{:S(2)}, u32[]{:S(2)}) async-start(bf16[16,8,64,128]{3,2,1,0:T(8,128)(2,1)} %broadcast_in_dim.81), calls=%async_computation.1 | async-start | bytes 4194304 | tf_op jit(solution)/shard_map/all_to_all | solution.py:487
  45.3 3.4 %collective-permute-start.2 = (f32[20,8,1]{2,1,0:T(8,128)S(1)}, f32[20,8,1]{2,1,0:T(8,128)S(1)}, u32[]{:S(2)}, u32[]{:S(2)}) collective-permute-start(f32[20,8,1]{2,1,0:T(8,128)S(1)} %get-tuple-element.43), channel_id=1, source_target_pairs={{0,1},{1,2},{2,3},{3,4},{4,5},{5,6},{6,7},{7,8},{8,9},{9,10},{10,1... | collective-permute-start | bytes 1928 | tf_op jit(solution)/shard_map/ppermute | solution.py:454
  48.7 2.5 %collective-permute-start.3 = (f32[20,8,1]{2,1,0:T(8,128)S(1)}, f32[20,8,1]{2,1,0:T(8,128)S(1)}, u32[]{:S(2)}, u32[]{:S(2)}) collective-permute-start(f32[20,8,1]{2,1,0:T(8,128)S(1)} %get-tuple-element.44), channel_id=1, source_target_pairs={{0,15},{1,0},{2,1},{3,2},{4,3},{5,4},{6,5},{7,6},{8,7},{9,8},{10,9... | collective-permute-start | bytes 1928 | tf_op jit(solution)/shard_map/ppermute | solution.py:454
  51.2 5.3 %collective-permute-start.1 = (bf16[64,1536]{1,0:T(8,128)(2,1)S(1)}, bf16[64,1536]{1,0:T(8,128)(2,1)S(1)}, u32[]{:S(2)}, u32[]{:S(2)}) collective-permute-start(bf16[64,1536]{1,0:T(8,128)(2,1)S(1)} %get-tuple-element.41), channel_id=1, source_target_pairs={{0,15},{1,0},{2,1},{3,2},{4,3},{5,4},{6,5},{7,6},{8,7},{9,8},{10,9... | collective-permute-start | bytes 589832 | tf_op jit(solution)/shard_map/ppermute | solution.py:454
  56.6 1.9 %collective-permute-start = (bf16[64,1536]{1,0:T(8,128)(2,1)S(1)}, bf16[64,1536]{1,0:T(8,128)(2,1)S(1)}, u32[]{:S(2)}, u32[]{:S(2)}) collective-permute-start(bf16[64,1536]{1,0:T(8,128)(2,1)S(1)} %get-tuple-element.42), channel_id=1, source_target_pairs={{0,1},{1,2},{2,3},{3,4},{4,5},{5,6},{6,7},{7,8},{8,9},{9,10},{10,1... | collective-permute-start | bytes 589832 | tf_op jit(solution)/shard_map/ppermute | solution.py:454
  59.2 11.1 %collective-permute-done.2 = f32[20,8,1]{2,1,0:T(8,128)S(1)} collective-permute-done((f32[20,8,1]{2,1,0:T(8,128)S(1)}, f32[20,8,1]{2,1,0:T(8,128)S(1)}, u32[]{:S(2)}, u32[]{:S(2)}) %collective-permute-start.2) | collective-permute-done | bytes 672 | tf_op jit(solution)/shard_map/ppermute | solution.py:454
  73.4 1.7 collective-permute-done.1.right_ref
  75.9 3.3 %prepare.1 = (bf16[384,1536]{1,0:T(8,128)(2,1)}, bf16[256,512]{1,0:T(8,128)(2,1)}) custom-call(bf16[256,1536]{1,0:T(8,128)(2,1)} %bitcast.44, bf16[64,1536]{1,0:T(8,128)(2,1)} %copy-done.7, bf16[64,1536]{1,0:T(8,128)(2,1)} %copy-done.6, f32[1,1536]{1,0:T(1,128)} %reshape.150.gain_ref, f32[20,32,128]{2,1,0:T(8,128)} %bitcast.56), custom_call_target="tpu_custom_call" | custom-call | tf_op jit(solution)/shard_map/prepare/pallas_call | solution.py:91
  79.2 1.9 %collective-permute-start.4 = (bf16[16,8,64,128]{3,2,1,0:T(8,128)(2,1)S(1)}, bf16[16,8,64,128]{3,2,1,0:T(8,128)(2,1)}, u32[]{:S(2)}, u32[]{:S(2)}) collective-permute-start(bf16[16,8,64,128]{3,2,1,0:T(8,128)(2,1)S(1)} %all-to-all-done.1.own_ref), channel_id=1, source_target_pairs={{0,16},{16,0},{1,17},{17,1},{2,18},{18,2},{3,19},{19,3},{4,20},{20... | collective-permute-start | bytes 6291464 | tf_op jit(solution)/shard_map/ppermute | solution.py:499
  81.2 4.3 %collective-permute-done.4.other_ref = bf16[16,8,64,128]{3,2,1,0:T(8,128)(2,1)} collective-permute-done((bf16[16,8,64,128]{3,2,1,0:T(8,128)(2,1)S(1)}, bf16[16,8,64,128]{3,2,1,0:T(8,128)(2,1)}, u32[]{:S(2)}, u32[]{:S(2)}) %collective-permute-start.4) | collective-permute-done | bytes 2097184 | tf_op jit(solution)/shard_map/ppermute | solution.py:499
  85.5 4.0 %unpack.1 = (bf16[768,1536]{1,0:T(8,128)(2,1)}, bf16[1536,512]{1,0:T(8,128)(2,1)}) custom-call(s32[1]{0:T(128)} %bitcast.6.core_ref, bf16[16,8,64,128]{3,2,1,0:T(8,128)(2,1)} %copy-done.2, bf16[16,8,64,128]{3,2,1,0:T(8,128)(2,1)} %collective-permute-done.4.other_ref), custom_call_target="tpu_custom_call" | custom-call | tf_op jit(solution)/shard_map/unpack/pallas_call | solution.py:120
  89.5 4.3 %hidden_grad.1 = (f32[256,1536]{1,0:T(8,128)}, bf16[256,768]{1,0:T(8,128)(2,1)}) custom-call(bf16[256,512]{1,0:T(8,128)(2,1)} %get-tuple-element.23.rows_ref.rows_hbm, bf16[1536,512]{1,0:T(8,128)(2,1)} %get-tuple-element.25.head_ref.head_hbm, bf16[768,1536]{1,0:T(8,128)(2,1)} %get-tuple-element.26.out_ref.out_hbm), custom_call_target="tpu_custom_call" | custom-call | tf_op jit(solution)/shard_map/hidden_grad/pallas_call | solution.py:143
  93.8 14.7 %forward.1 = (bf16[6,384,384]{2,1,0:T(8,128)(2,1)}, f32[20,32,128]{2,1,0:T(8,128)}, bf16[32,24,640]{2,1,0:T(8,128)(2,1)}) custom-call(bf16[384,1536]{1,0:T(8,128)(2,1)} %get-tuple-element.22.normed_ref, bf16[2,1536,1152]{2,1,0:T(8,128)(2,1)} %bitcast.41, bf16[256,1536]{1,0:T(8,128)(2,1)} %bitcast.45, bf16[768,1536]{1,0:T(8,128)(2,1)} %get-tuple-element.26.out_ref.out_hbm, ...), custom_call_target="tpu_custom_call" | custom-call | tf_op jit(solution)/shard_map/forward/pallas_call | solution.py:263
  108.6 22.1 %all_to_all.26.pieces_ref = bf16[32,24,640]{2,1,0:T(8,128)(2,1)} all-to-all(bf16[32,24,640]{2,1,0:T(8,128)(2,1)} %get-tuple-element.40), channel_id=1, replica_groups=mesh['dp'=2,'z'=8,'c'=2,'y'=4,'x'=4] {'c','y','x'}, dimensions={0} | all-to-all | bytes 1966080 | tf_op jit(solution)/shard_map/all_to_all | solution.py:504
  130.7 2.1 %sum_pieces.1 = f32[16,24,128]{2,1,0:T(8,128)} custom-call(bf16[32,24,640]{2,1,0:T(8,128)(2,1)} %all_to_all.26.pieces_ref), custom_call_target="tpu_custom_call" | custom-call | tf_op jit(solution)/shard_map/sum_pieces/pallas_call | solution.py:429
  132.8 7.7 %all-to-all-start.3 = ((f32[16,24,128]{2,1,0:T(8,128)}), f32[16,24,128]{2,1,0:T(8,128)S(1)}, u32[]{:S(2)}, u32[]{:S(2)}) async-start(f32[16,24,128]{2,1,0:T(8,128)} %sum_pieces.1), calls=%async_computation.3 | async-start | bytes 393216 | tf_op jit(solution)/shard_map/all_to_all | solution.py:505
  140.5 7.1 %attend_backward.1 = (bf16[256,768]{1,0:T(8,128)(2,1)}, f32[256,768]{1,0:T(8,128)}, f32[256,768]{1,0:T(8,128)}, bf16[2,64,768]{2,1,0:T(8,128)(2,1)}, bf16[2,64,768]{2,1,0:T(8,128)(2,1)}) custom-call(bf16[6,384,384]{2,1,0:T(8,128)(2,1)} %get-tuple-element.32.q_ref.k_ref.v_ref, bf16[6,384,384]{2,1,0:T(8,128)(2,1)} %get-tuple-element.32.q_ref.k_ref.v_ref, ...), custom_call_target="tpu_custom_call" | custom-call | tf_op jit(solution)/shard_map/attend_backward/pallas_call | solution.py:336
  147.6 3.5 %collective-permute-start.5 = (bf16[2,64,768]{2,1,0:T(8,128)(2,1)}, bf16[2,64,768]{2,1,0:T(8,128)(2,1)S(1)}, u32[]{:S(2)}, u32[]{:S(2)}) collective-permute-start(bf16[2,64,768]{2,1,0:T(8,128)(2,1)} %get-tuple-element.37), channel_id=1, source_target_pairs={{0,1},{1,2},{2,3},{3,4},{4,5},{5,6},{6,7},{7,8},{8,9},{9,10},{10,1... | collective-permute-start | bytes 589832 | tf_op jit(solution)/shard_map/ppermute | solution.py:454
  151.1 2.9 %collective-permute-start.6 = (bf16[2,64,768]{2,1,0:T(8,128)(2,1)}, bf16[2,64,768]{2,1,0:T(8,128)(2,1)S(1)}, u32[]{:S(2)}, u32[]{:S(2)}) collective-permute-start(bf16[2,64,768]{2,1,0:T(8,128)(2,1)} %get-tuple-element.38), channel_id=1, source_target_pairs={{0,15},{1,0},{2,1},{3,2},{4,3},{5,4},{6,5},{7,6},{8,7},{9,8},{10,9... | collective-permute-start | bytes 589832 | tf_op jit(solution)/shard_map/ppermute | solution.py:454
  154.1 2.1 %all-to-all-done.3 = f32[16,24,128]{2,1,0:T(8,128)S(1)} async-done(((f32[16,24,128]{2,1,0:T(8,128)}), f32[16,24,128]{2,1,0:T(8,128)S(1)}, u32[]{:S(2)}, u32[]{:S(2)}) %all-to-all-start.3) | async-done | bytes 196640 | tf_op jit(solution)/shard_map/all_to_all | solution.py:505
  156.9 6.6 %all-to-all-start.4 = ((f32[16,24,128]{2,1,0:T(8,128)}), f32[16,24,128]{2,1,0:T(8,128)S(1)}, u32[]{:S(2)}, u32[]{:S(2)}) async-start(f32[16,24,128]{2,1,0:T(8,128)} %broadcast_in_dim.89), calls=%async_computation.4 | async-start | bytes 393216 | tf_op jit(solution)/shard_map/all_to_all | solution.py:487
  164.2 8.8 %norm_grad.1 = bf16[256,1536]{1,0:T(8,128)(2,1)} custom-call(bf16[256,768]{1,0:T(8,128)(2,1)} %get-tuple-element.34.dq_ref, f32[256,768]{1,0:T(8,128)} %get-tuple-element.35.dk_ref, f32[256,768]{1,0:T(8,128)} %get-tuple-element.36.dv_ref, bf16[2,64,768]{2,1,0:T(8,128)(2,1)} %copy-done.4, bf16[2,64,768]{2,1,0:T(8,128)(2,1)} %copy-done.5, ...), custom_call_target="tpu_custom_call" | custom-call | tf_op jit(solution)/shard_map/norm_grad/pallas_call | solution.py:389
  (50 shorter events, 11.3 us)
Async XLA Ops:
  7.2 1.0 copy-start
  7.2 86.7 %all-gather.2.cloned.1.call-start = ((), (), s32[]{:S(2)}) async-start(), calls=%async_computation.5 | async-start | bytes 7299072 | tf_op jit(solution)/shard_map/all_gather | solution.py:481
  37.6 7.6 %copy-start.3 = (f32[1,20,8,32]{3,2,1,0:T(8,128)S(1)}, f32[1,20,8,32]{3,2,1,0:T(8,128)}, u32[]{:S(2)}) copy-start(f32[1,20,8,32]{3,2,1,0:T(8,128)} %param.12) | copy-start | bytes 61444
  37.6 13.6 %copy-start.1 = (bf16[1,8,32,1536]{3,2,1,0:T(8,128)(2,1)S(1)}, bf16[1,8,32,1536]{3,2,1,0:T(8,128)(2,1)}, u32[]{:S(2)}) copy-start(bf16[1,8,32,1536]{3,2,1,0:T(8,128)(2,1)} %param.7) | copy-start | bytes 2359300
  37.6 20.9 %copy-start.8 = (f32[1536]{0:T(1024)S(1)}, f32[1536]{0:T(1024)}, u32[]{:S(2)}) copy-start(f32[1536]{0:T(1024)} %param.8) | copy-start | bytes 18436
  37.6 41.6 %all-to-all-start.1 = ((bf16[16,8,64,128]{3,2,1,0:T(8,128)(2,1)}), bf16[16,8,64,128]{3,2,1,0:T(8,128)(2,1)S(1)}, u32[]{:S(2)}, u32[]{:S(2)}) async-start(bf16[16,8,64,128]{3,2,1,0:T(8,128)(2,1)} %broadcast_in_dim.81), calls=%async_computation.1 | async-start | bytes 4194304 | tf_op jit(solution)/shard_map/all_to_all | solution.py:487
  45.3 25.0 %collective-permute-start.2 = (f32[20,8,1]{2,1,0:T(8,128)S(1)}, f32[20,8,1]{2,1,0:T(8,128)S(1)}, u32[]{:S(2)}, u32[]{:S(2)}) collective-permute-start(f32[20,8,1]{2,1,0:T(8,128)S(1)} %get-tuple-element.43), channel_id=1, source_target_pairs={{0,1},{1,2},{2,3},{3,4},{4,5},{5,6},{6,7},{7,8},{8,9},{9,10},{10,1... | collective-permute-start | bytes 1928 | tf_op jit(solution)/shard_map/ppermute | solution.py:454
  48.7 23.1 %collective-permute-start.3 = (f32[20,8,1]{2,1,0:T(8,128)S(1)}, f32[20,8,1]{2,1,0:T(8,128)S(1)}, u32[]{:S(2)}, u32[]{:S(2)}) collective-permute-start(f32[20,8,1]{2,1,0:T(8,128)S(1)} %get-tuple-element.44), channel_id=1, source_target_pairs={{0,15},{1,0},{2,1},{3,2},{4,3},{5,4},{6,5},{7,6},{8,7},{9,8},{10,9... | collective-permute-start | bytes 1928 | tf_op jit(solution)/shard_map/ppermute | solution.py:454
  51.2 23.9 %collective-permute-start.1 = (bf16[64,1536]{1,0:T(8,128)(2,1)S(1)}, bf16[64,1536]{1,0:T(8,128)(2,1)S(1)}, u32[]{:S(2)}, u32[]{:S(2)}) collective-permute-start(bf16[64,1536]{1,0:T(8,128)(2,1)S(1)} %get-tuple-element.41), channel_id=1, source_target_pairs={{0,15},{1,0},{2,1},{3,2},{4,3},{5,4},{6,5},{7,6},{8,7},{9,8},{10,9... | collective-permute-start | bytes 589832 | tf_op jit(solution)/shard_map/ppermute | solution.py:454
  56.6 18.6 %collective-permute-start = (bf16[64,1536]{1,0:T(8,128)(2,1)S(1)}, bf16[64,1536]{1,0:T(8,128)(2,1)S(1)}, u32[]{:S(2)}, u32[]{:S(2)}) collective-permute-start(bf16[64,1536]{1,0:T(8,128)(2,1)S(1)} %get-tuple-element.42), channel_id=1, source_target_pairs={{0,1},{1,2},{2,3},{3,4},{4,5},{5,6},{6,7},{7,8},{8,9},{9,10},{10,1... | collective-permute-start | bytes 589832 | tf_op jit(solution)/shard_map/ppermute | solution.py:454
  75.2 0.7 copy-start.6
  75.2 0.7 copy-start.7
  79.2 6.3 %copy-start.2 = (bf16[16,8,64,128]{3,2,1,0:T(8,128)(2,1)}, bf16[16,8,64,128]{3,2,1,0:T(8,128)(2,1)S(1)}, u32[]{:S(2)}) copy-start(bf16[16,8,64,128]{3,2,1,0:T(8,128)(2,1)S(1)} %all-to-all-done.1.own_ref) | copy-start | bytes 6291460
  79.2 6.3 %collective-permute-start.4 = (bf16[16,8,64,128]{3,2,1,0:T(8,128)(2,1)S(1)}, bf16[16,8,64,128]{3,2,1,0:T(8,128)(2,1)}, u32[]{:S(2)}, u32[]{:S(2)}) collective-permute-start(bf16[16,8,64,128]{3,2,1,0:T(8,128)(2,1)S(1)} %all-to-all-done.1.own_ref), channel_id=1, source_target_pairs={{0,16},{16,0},{1,17},{17,1},{2,18},{18,2},{3,19},{19,3},{4,20},{20... | collective-permute-start | bytes 6291464 | tf_op jit(solution)/shard_map/ppermute | solution.py:499
  132.8 23.4 %all-to-all-start.3 = ((f32[16,24,128]{2,1,0:T(8,128)}), f32[16,24,128]{2,1,0:T(8,128)S(1)}, u32[]{:S(2)}, u32[]{:S(2)}) async-start(f32[16,24,128]{2,1,0:T(8,128)} %sum_pieces.1), calls=%async_computation.3 | async-start | bytes 393216 | tf_op jit(solution)/shard_map/all_to_all | solution.py:505
  147.6 15.9 %collective-permute-start.5 = (bf16[2,64,768]{2,1,0:T(8,128)(2,1)}, bf16[2,64,768]{2,1,0:T(8,128)(2,1)S(1)}, u32[]{:S(2)}, u32[]{:S(2)}) collective-permute-start(bf16[2,64,768]{2,1,0:T(8,128)(2,1)} %get-tuple-element.37), channel_id=1, source_target_pairs={{0,1},{1,2},{2,3},{3,4},{4,5},{5,6},{6,7},{7,8},{8,9},{9,10},{10,1... | collective-permute-start | bytes 589832 | tf_op jit(solution)/shard_map/ppermute | solution.py:454
  151.1 12.3 %collective-permute-start.6 = (bf16[2,64,768]{2,1,0:T(8,128)(2,1)}, bf16[2,64,768]{2,1,0:T(8,128)(2,1)S(1)}, u32[]{:S(2)}, u32[]{:S(2)}) collective-permute-start(bf16[2,64,768]{2,1,0:T(8,128)(2,1)} %get-tuple-element.38), channel_id=1, source_target_pairs={{0,15},{1,0},{2,1},{3,2},{4,3},{5,4},{6,5},{7,6},{8,7},{9,8},{10,9... | collective-permute-start | bytes 589832 | tf_op jit(solution)/shard_map/ppermute | solution.py:454
  156.9 16.2 %all-to-all-start.4 = ((f32[16,24,128]{2,1,0:T(8,128)}), f32[16,24,128]{2,1,0:T(8,128)S(1)}, u32[]{:S(2)}, u32[]{:S(2)}) async-start(f32[16,24,128]{2,1,0:T(8,128)} %broadcast_in_dim.89), calls=%async_computation.4 | async-start | bytes 393216 | tf_op jit(solution)/shard_map/all_to_all | solution.py:487
  163.5 0.7 copy-start.4
  163.5 0.7 copy-start.5
Sparse Core Ops, SparseCore 0:
  10.7 81.7 all-gather.1

commit v5 on v4

--- a/solution.py
+++ b/solution.py
@@ -188,9 +188,9 @@
 
 
 def forward_kernel(
-    normed_ref, weight_ref,
+    core_ref, normed_ref, weight_ref,
     tokens_hbm, out_hbm, head_hbm, rows_hbm, residual_hbm,
-    projected_ref, fine_ref, pieces_ref,
+    projected_ref, fine_ref, own_ref, send_ref,
     tokens_ref, out_ref, head_ref, rows_ref, residual_ref, products, sems,
 ):
     step = pl.program_id(0)
@@ -232,17 +232,15 @@
         hidden = (tokens_ref[...].astype(F32) + mixed).astype(BF16)
         head_out = dot(hidden, head_ref[...])
         products[...] = dot_first(hidden, rows_ref[...])
-        for core in range(CORES):
+        core = core_ref[0]
+        for target, place in ((own_ref, core), (send_ref, 1 - core)):
             for quad in range(4):
                 for phase in range(PHASES):
-                    row = [
-                        products[
-                            (z * CORES + core) * 96 + quad * 24 : (z * CORES + core) * 96 + quad * 24 + 24,
-                            phase * LANES : phase * LANES + CHANNELS,
-                        ]
-                        for z in range(ZS)
-                    ]
-                    pieces_ref[core * TILES + quad * 4 + phase] = jnp.concatenate(row, axis=1).astype(BF16)
+                    row = []
+                    for z in range(ZS):
+                        top = pl.multiple_of(place * 96 + z * 192 + quad * 24, 8)
+                        row.append(products[pl.ds(top, 24), phase * LANES : phase * LANES + CHANNELS])
+                    target[quad * 4 + phase] = jnp.concatenate(row, axis=1).astype(target.dtype)
         select = spread_matrix()
         for lat in range(LAT):
             at = slice(lat * LON_DEV, (lat + 1) * LON_DEV)
@@ -256,24 +254,26 @@
             fine_ref[:, across, :] = spread[:CHANNELS].reshape(VARS, PHASES, LANES) + residual_ref[:, across, :]
 
 
-def forward(normed, full, tokens, out_weight, head, rows, residual):
+def forward(core, normed, full, tokens, out_weight, head, rows, residual):
     fine = (VARS, 4 * LAT, LANES)
-    pieces = (CORES * TILES, 24, WIDE)
+    pieces = (TILES, 24, WIDE)
     projected = (6, KEYS, GROUP)
     return pl.pallas_call(
         forward_kernel,
         out_shape=(
             jax.ShapeDtypeStruct(projected, BF16),
             jax.ShapeDtypeStruct(fine, F32),
+            jax.ShapeDtypeStruct(pieces, F32),
             jax.ShapeDtypeStruct(pieces, BF16),
         ),
         grid=(6,),
         in_specs=[
+            pl.BlockSpec(memory_space=pltpu.SMEM),
             whole_block((KEYS, D)),
             pl.BlockSpec((1, D, GROUP), lambda n: (n // 3, 0, n % 3)),
         ]
         + [pl.BlockSpec(memory_space=pl.ANY)] * 5,
-        out_specs=(whole_block(projected), whole_block(fine), whole_block(pieces)),
+        out_specs=(whole_block(projected), whole_block(fine), whole_block(pieces), whole_block(pieces)),
         scratch_shapes=[
             pltpu.VMEM((ROWS, D), BF16),
             pltpu.VMEM((INNER, D), BF16),
@@ -284,7 +284,7 @@
             pltpu.SemaphoreType.DMA((5,)),
         ],
         name="forward",
-    )(normed, full, tokens, out_weight, head, rows, residual)
+    )(core, normed, full, tokens, out_weight, head, rows, residual)
 
 
 def backward_kernel(
@@ -416,7 +416,7 @@
 
 def sum_kernel(pieces_ref, out_ref):
     total = pieces_ref[0].astype(F32)
-    for place in range(1, CORES * TILES):
+    for place in range(1, TILES):
         total = total + pieces_ref[place].astype(F32)
     empty = jnp.zeros((24, LANES - CHANNELS), F32)
     for z in range(ZS):
@@ -487,7 +487,7 @@
     return lax.all_to_all(copies, axes, 0, 0, tiled=True)
 
 
-def gather_rest(out_w, head_w, ready):
+def gather_rest(core, out_w, head_w, ready):
     out_rows = out_w.reshape(48, 12, LANES).transpose(1, 0, 2).reshape(576, LANES)
     head_pad = dot(head_w, head_columns().astype(BF16)).astype(BF16)
     head_rows = head_pad.reshape(96, PHASES, LANES).transpose(1, 0, 2).reshape(384, LANES)
@@ -497,12 +497,16 @@
     over_tile = to_all(over_z, TILE, TILES)
     over_tile = lax.optimization_barrier((over_tile, ready))[0]
     other = lax.ppermute(over_tile, "c", [(0, 1), (1, 0)])
-    return unpack(lax.axis_index("c").reshape(1).astype(jnp.int32), over_tile, other)
-
-
-def reduce_head(pieces):
-    pieces = lax.all_to_all(pieces, ("c",) + TILE, 0, 0, tiled=True)
-    both = lax.all_to_all(sum_pieces(pieces), ("dp", "z"), 0, 0, tiled=True)
+    return unpack(core, over_tile, other)
+
+
+def over_tiles(own, send):
+    pair = own + lax.ppermute(send, "c", [(0, 1), (1, 0)]).astype(F32)
+    return lax.all_to_all(pair.astype(BF16), TILE, 0, 0, tiled=True)
+
+
+def over_samples(summed):
+    both = lax.all_to_all(summed, ("dp", "z"), 0, 0, tiled=True)
     spread = to_all(jnp.sum(both, axis=0), TILE, TILES)
     padded = spread.reshape(4, PHASES, 24, LANES).transpose(0, 2, 1, 3).reshape(96, PADDED)
     return lax.dot_general(
@@ -519,14 +523,17 @@
     right = shifted(grid[:, :MARGIN].reshape(EDGE, D), -1)
     residual = residual_of(coarse[0])
     normed, rows = prepare(tokens, left, right, gain, grad_fine[0])
-    out_full, head = gather_rest(out_weight, head_weight, (normed, residual))
+    core = lax.axis_index("c").reshape(1).astype(jnp.int32)
+    out_full, head = gather_rest(core, out_weight, head_weight, (normed, residual))
+    full, out_full, head, residual = lax.optimization_barrier((full, out_full, head, residual))
+    projected, fine_grid, own, send = forward(core, normed, full, tokens, out_full, head, rows, residual)
+    pieces = over_tiles(own, send)
     grad_hidden, grad_attended = hidden_grad(rows, head, out_full)
-    full, grad_hidden, grad_attended, residual = lax.optimization_barrier(
-        (full, grad_hidden, grad_attended, residual)
-    )
-    projected, fine_grid, pieces = forward(normed, full, tokens, out_full, head, rows, residual)
-    grad_head = reduce_head(pieces)
     dq, dk, dv, to_left, to_right = attend_backward(projected, grad_attended)
+    pieces, to_left, to_right = lax.optimization_barrier((pieces, to_left, to_right))
+    summed = sum_pieces(pieces)
+    grad_head = over_samples(summed)
+    to_left, to_right = lax.optimization_barrier((to_left, to_right, summed))[:2]
     from_right = shifted(to_left, -1)
     from_left = shifted(to_right, 1)
     grad_tokens = norm_grad(dq, dk, dv, from_left, from_right, full, tokens, gain, grad_hidden)

time: 182 us -> 186 us (1.022)
  blocking collectives: 46.5 us -> 24.4 us
  waiting for transfers between devices: 20.8 us -> 33.8 us
  starting transfers between devices: 43.5 us -> 53.2 us
  other arithmetic: 0.15 us -> 2.22 us
    all_to_all x1 -> x0, blocking collectives: 22.1 us -> none  [reduce_head(): pieces = lax.all_to_all(pieces, ('c',) + TILE, 0, 0, tiled=True)]
    all_to_all x1 -> x2, waiting for transfers between devices: 2.08 us -> 10.3 us  [the longest x1 10.3 us: over_samples(): both = lax.all_to_all(summed, ('dp', 'z'), 0, 0, tiled=True)]
    all_to_all x1 -> x2, starting transfers between devices: 7.74 us -> 15.3 us  [the longest x1 7.9 us: over_samples(): both = lax.all_to_all(summed, ('dp', 'z'), 0, 0, tiled=True)]
    all_gather x1, waiting for transfers between devices: 0.01 us -> 2.96 us  [gather_qkv(): full = lax.all_gather(qkv_half, ('dp',) + FSDP, axis=0, tiled=True)]
    ppermute x0 -> x1, starting transfers between devices: none -> 2.13 us  [over_tiles(): pair = own + lax.ppermute(send, 'c', [(0, 1), (1, 0)]).astype(F32)]
    convert_element_type x0 -> x1, other arithmetic: none -> 2.07 us  [over_tiles(): return lax.all_to_all(pair.astype(BF16), TILE, 0, 0, tiled=True)]
  transfers between devices with their start and end apart: 11 -> 13, of which waited for: 5 -> 8; matrix products, arithmetic and copies ran while one was open for 4% -> 4% of each run, Pallas kernels for 15% -> 15%
where the time goes in v5:
time: 186 us; the launch traced here: 185 us
  starting transfers between devices  53.2 us (29%)
  Pallas kernels  44.7 us (24%)
  waiting for transfers between devices  33.8 us (18%)
  blocking collectives  24.4 us (13%)
  between operations  14.3 us (8%)
  local copies, waits for them, and re-layouts  8.45 us (5%)
  matrix products  3.86 us (2%)
  other arithmetic  2.22 us (1%)
    all_to_all x1, blocking collectives, to_all(): return lax.all_to_all(copies, axes, 0, 0, tiled=True)  24.4 us
    ppermute x6, starting transfers between devices, shifted(): lax.ppermute(value, TILE, [(i, (i + steps) % TILES) for i in range(TILES)])  18.9 us
    pallas_call x1, Pallas kernels, forward(): pl.pallas_call(forward_kernel, out_shape=(jax.ShapeDtypeStruct(projected,...  15.3 us
    all_to_all x2, starting transfers between devices, to_all(): return lax.all_to_all(copies, axes, 0, 0, tiled=True)  14.8 us
    ppermute x6, waiting for transfers between devices, shifted(): lax.ppermute(value, TILE, [(i, (i + steps) % TILES) for i in range(TILES)])  14.4 us
    all_to_all x1, waiting for transfers between devices, over_samples(): both = lax.all_to_all(summed, ('dp', 'z'), 0, 0, tiled=True)  10.3 us
    pallas_call x1, Pallas kernels, norm_grad(): pl.pallas_call(norm_grad_kernel, out_shape=jax.ShapeDtypeStruct((ROWS, D)...  8.81 us
    all_to_all x1, starting transfers between devices, over_samples(): both = lax.all_to_all(summed, ('dp', 'z'), 0, 0, tiled=True)  7.9 us
  transfers between devices with their start and end apart: 13, of which 8 were waited for; matrix products, arithmetic and copies ran while one was open for 4% of the time, Pallas kernels for 15%

profile of v5, /device:TPU:2, one launch (start us, length us, event | category | flops | bytes accessed | tf_op | source)
XLA Modules:
  0.0 184.9 jit_solution(12796598945246211233)
XLA Ops:
  11.4 24.4 %all_to_all.25 = bf16[8,64,128]{2,1,0:T(8,128)(2,1)S(1)} all-to-all(bf16[8,64,128]{2,1,0:T(8,128)(2,1)S(1)} %broadcast_in_dim.80), channel_id=1, replica_groups=mesh['dp'=2,'z'=8,'c'=2,'y'=4,'x'=4] {'z'}, dimensions={0} | all-to-all | bytes 262144 | tf_op jit(solution)/shard_map/all_to_all | solution.py:487
  35.7 1.9 %broadcast_in_dim.81 = bf16[16,8,64,128]{3,2,1,0:T(8,128)(2,1)} broadcast(bf16[8,64,128]{2,1,0:T(8,128)(2,1)S(1)} %all_to_all.25), dimensions={1,2,3} | broadcast | bytes 2228224 | tf_op jit(solution)/shard_map/broadcast_in_dim | solution.py:486
  37.7 7.6 %all-to-all-start.1 = ((bf16[16,8,64,128]{3,2,1,0:T(8,128)(2,1)}), bf16[16,8,64,128]{3,2,1,0:T(8,128)(2,1)S(1)}, u32[]{:S(2)}, u32[]{:S(2)}) async-start(bf16[16,8,64,128]{3,2,1,0:T(8,128)(2,1)} %broadcast_in_dim.81), calls=%async_computation.1 | async-start | bytes 4194304 | tf_op jit(solution)/shard_map/all_to_all | solution.py:487
  45.4 3.4 %collective-permute-start.2 = (f32[20,8,1]{2,1,0:T(8,128)S(1)}, f32[20,8,1]{2,1,0:T(8,128)S(1)}, u32[]{:S(2)}, u32[]{:S(2)}) collective-permute-start(f32[20,8,1]{2,1,0:T(8,128)S(1)} %get-tuple-element.55), channel_id=1, source_target_pairs={{0,1},{1,2},{2,3},{3,4},{4,5},{5,6},{6,7},{7,8},{8,9},{9,10},{10,1... | collective-permute-start | bytes 1928 | tf_op jit(solution)/shard_map/ppermute | solution.py:454
  48.7 2.5 %collective-permute-start.3 = (f32[20,8,1]{2,1,0:T(8,128)S(1)}, f32[20,8,1]{2,1,0:T(8,128)S(1)}, u32[]{:S(2)}, u32[]{:S(2)}) collective-permute-start(f32[20,8,1]{2,1,0:T(8,128)S(1)} %get-tuple-element.56), channel_id=1, source_target_pairs={{0,15},{1,0},{2,1},{3,2},{4,3},{5,4},{6,5},{7,6},{8,7},{9,8},{10,9... | collective-permute-start | bytes 1928 | tf_op jit(solution)/shard_map/ppermute | solution.py:454
  51.3 3.4 %collective-permute-start = (bf16[64,1536]{1,0:T(8,128)(2,1)S(1)}, bf16[64,1536]{1,0:T(8,128)(2,1)S(1)}, u32[]{:S(2)}, u32[]{:S(2)}) collective-permute-start(bf16[64,1536]{1,0:T(8,128)(2,1)S(1)} %get-tuple-element.54), channel_id=1, source_target_pairs={{0,1},{1,2},{2,3},{3,4},{4,5},{5,6},{6,7},{7,8},{8,9},{9,10},{10,1... | collective-permute-start | bytes 589832 | tf_op jit(solution)/shard_map/ppermute | solution.py:454
  54.6 3.9 %collective-permute-start.1 = (bf16[64,1536]{1,0:T(8,128)(2,1)S(1)}, bf16[64,1536]{1,0:T(8,128)(2,1)S(1)}, u32[]{:S(2)}, u32[]{:S(2)}) collective-permute-start(bf16[64,1536]{1,0:T(8,128)(2,1)S(1)} %get-tuple-element.53), channel_id=1, source_target_pairs={{0,15},{1,0},{2,1},{3,2},{4,3},{5,4},{6,5},{7,6},{8,7},{9,8},{10,9... | collective-permute-start | bytes 589832 | tf_op jit(solution)/shard_map/ppermute | solution.py:454
  59.2 11.1 %collective-permute-done.2 = f32[20,8,1]{2,1,0:T(8,128)S(1)} collective-permute-done((f32[20,8,1]{2,1,0:T(8,128)S(1)}, f32[20,8,1]{2,1,0:T(8,128)S(1)}, u32[]{:S(2)}, u32[]{:S(2)}) %collective-permute-start.2) | collective-permute-done | bytes 672 | tf_op jit(solution)/shard_map/ppermute | solution.py:454
  75.9 3.3 %prepare.1 = (bf16[384,1536]{1,0:T(8,128)(2,1)}, bf16[256,512]{1,0:T(8,128)(2,1)}) custom-call(bf16[256,1536]{1,0:T(8,128)(2,1)} %bitcast.44, bf16[64,1536]{1,0:T(8,128)(2,1)} %copy-done.7, bf16[64,1536]{1,0:T(8,128)(2,1)} %copy-done.8, f32[1,1536]{1,0:T(1,128)} %reshape.151.gain_ref, f32[20,32,128]{2,1,0:T(8,128)} %bitcast.56), custom_call_target="tpu_custom_call" | custom-call | tf_op jit(solution)/shard_map/prepare/pallas_call | solution.py:91
  81.1 4.3 %collective-permute-done.4.other_ref = bf16[16,8,64,128]{3,2,1,0:T(8,128)(2,1)} collective-permute-done((bf16[16,8,64,128]{3,2,1,0:T(8,128)(2,1)S(1)}, bf16[16,8,64,128]{3,2,1,0:T(8,128)(2,1)}, u32[]{:S(2)}, u32[]{:S(2)}) %collective-permute-start.4) | collective-permute-done | bytes 2097184 | tf_op jit(solution)/shard_map/ppermute | solution.py:499
  85.5 4.0 %unpack.1 = (bf16[768,1536]{1,0:T(8,128)(2,1)}, bf16[1536,512]{1,0:T(8,128)(2,1)}) custom-call(s32[1]{0:T(128)} %bitcast.core_ref, bf16[16,8,64,128]{3,2,1,0:T(8,128)(2,1)} %copy-done.2, bf16[16,8,64,128]{3,2,1,0:T(8,128)(2,1)} %collective-permute-done.4.other_ref), custom_call_target="tpu_custom_call" | custom-call | tf_op jit(solution)/shard_map/unpack/pallas_call | solution.py:120
  89.5 3.0 %all-gather.2.cloned.1.call-done = bf16[3072,1152]{1,0:T(8,128)(2,1)} async-done(((bf16[96,1152]{1,0:T(8,128)(2,1)}), bf16[3072,1152]{1,0:T(8,128)(2,1)}) %all-gather.2.cloned.1.call-update) | async-done | bytes 7077904 | tf_op jit(solution)/shard_map/all_gather | solution.py:481
  92.4 15.3 %forward.1 = (bf16[6,384,384]{2,1,0:T(8,128)(2,1)}, f32[20,32,128]{2,1,0:T(8,128)}, f32[16,24,640]{2,1,0:T(8,128)}, bf16[16,24,640]{2,1,0:T(8,128)(2,1)}) custom-call(s32[1]{0:T(128)} %bitcast.core_ref, bf16[384,1536]{1,0:T(8,128)(2,1)} %get-tuple-element.28.normed_ref, bf16[2,1536,1152]{2,1,0:T(8,128)(2,1)} %bitcast.41, bf16[256,1536]{1,0:T(8,128)(2,1)} %bitcast.45, ...), custom_call_target="tpu_custom_call" | custom-call | tf_op jit(solution)/shard_map/forward/pallas_call | solution.py:261
  107.7 2.1 %collective-permute-start.5 = (bf16[16,24,640]{2,1,0:T(8,128)(2,1)}, bf16[16,24,640]{2,1,0:T(8,128)(2,1)S(1)}, u32[]{:S(2)}, u32[]{:S(2)}) collective-permute-start(bf16[16,24,640]{2,1,0:T(8,128)(2,1)} %get-tuple-element.44), channel_id=1, source_target_pairs={{0,16},{16,0},{1,17},{17,1},{2,18},{18,2},{3,19},{19,3},{4,20},{20... | collective-permute-start | bytes 1474568 | tf_op jit(solution)/shard_map/ppermute | solution.py:504
  111.7 2.1 %add_convert_fusion = bf16[16,24,640]{2,1,0:T(8,128)(2,1)} fusion(f32[16,24,640]{2,1,0:T(8,128)} %get-tuple-element.43, bf16[16,24,640]{2,1,0:T(8,128)(2,1)S(1)} %collective-permute-done.5), kind=kLoop, calls=%fused_computation.3 | loop fusion | flops 737280 | bytes 1966080 | tf_op jit(solution)/shard_map/convert_element_type | solution.py:505
  113.7 7.4 %all-to-all-start.2 = ((bf16[16,24,640]{2,1,0:T(8,128)(2,1)}), bf16[16,24,640]{2,1,0:T(8,128)(2,1)S(1)}, u32[]{:S(2)}, u32[]{:S(2)}) async-start(bf16[16,24,640]{2,1,0:T(8,128)(2,1)} %add_convert_fusion), calls=%async_computation.2 | async-start | bytes 983040 | tf_op jit(solution)/shard_map/all_to_all | solution.py:505
  121.1 4.4 %hidden_grad.1 = (f32[256,1536]{1,0:T(8,128)}, bf16[256,768]{1,0:T(8,128)(2,1)}) custom-call(bf16[256,512]{1,0:T(8,128)(2,1)} %get-tuple-element.35.rows_hbm.rows_ref, bf16[1536,512]{1,0:T(8,128)(2,1)} %get-tuple-element.34.head_hbm.head_ref, bf16[768,1536]{1,0:T(8,128)(2,1)} %get-tuple-element.33.out_hbm.out_ref), custom_call_target="tpu_custom_call" | custom-call | tf_op jit(solution)/shard_map/hidden_grad/pallas_call | solution.py:143
  125.6 7.0 %attend_backward.1 = (bf16[256,768]{1,0:T(8,128)(2,1)}, f32[256,768]{1,0:T(8,128)}, f32[256,768]{1,0:T(8,128)}, bf16[2,64,768]{2,1,0:T(8,128)(2,1)}, bf16[2,64,768]{2,1,0:T(8,128)(2,1)}) custom-call(bf16[6,384,384]{2,1,0:T(8,128)(2,1)} %get-tuple-element.38.q_ref.k_ref.v_ref, bf16[6,384,384]{2,1,0:T(8,128)(2,1)} %get-tuple-element.38.q_ref.k_ref.v_ref, ...), custom_call_target="tpu_custom_call" | custom-call | tf_op jit(solution)/shard_map/attend_backward/pallas_call | solution.py:336
  135.2 7.9 %all-to-all-start.3 = ((f32[16,24,128]{2,1,0:T(8,128)}), f32[16,24,128]{2,1,0:T(8,128)S(1)}, u32[]{:S(2)}, u32[]{:S(2)}) async-start(f32[16,24,128]{2,1,0:T(8,128)} %sum_pieces.1), calls=%async_computation.3 | async-start | bytes 393216 | tf_op jit(solution)/shard_map/all_to_all | solution.py:509
  143.1 3.4 %collective-permute-start.6 = (bf16[2,64,768]{2,1,0:T(8,128)(2,1)}, bf16[2,64,768]{2,1,0:T(8,128)(2,1)S(1)}, u32[]{:S(2)}, u32[]{:S(2)}) collective-permute-start(bf16[2,64,768]{2,1,0:T(8,128)(2,1)} %get-tuple-element.50), channel_id=1, source_target_pairs={{0,1},{1,2},{2,3},{3,4},{4,5},{5,6},{6,7},{7,8},{8,9},{9,10},{10,1... | collective-permute-start | bytes 589832 | tf_op jit(solution)/shard_map/ppermute | solution.py:454
  146.5 2.5 %collective-permute-start.7 = (bf16[2,64,768]{2,1,0:T(8,128)(2,1)}, bf16[2,64,768]{2,1,0:T(8,128)(2,1)S(1)}, u32[]{:S(2)}, u32[]{:S(2)}) collective-permute-start(bf16[2,64,768]{2,1,0:T(8,128)(2,1)} %get-tuple-element.51), channel_id=1, source_target_pairs={{0,15},{1,0},{2,1},{3,2},{4,3},{5,4},{6,5},{7,6},{8,7},{9,8},{10,9... | collective-permute-start | bytes 589832 | tf_op jit(solution)/shard_map/ppermute | solution.py:454
  149.0 10.3 %all-to-all-done.3 = f32[16,24,128]{2,1,0:T(8,128)S(1)} async-done(((f32[16,24,128]{2,1,0:T(8,128)}), f32[16,24,128]{2,1,0:T(8,128)S(1)}, u32[]{:S(2)}, u32[]{:S(2)}) %all-to-all-start.3) | async-done | bytes 196640 | tf_op jit(solution)/shard_map/all_to_all | solution.py:509
  160.0 7.2 %all-to-all-start.4 = ((f32[16,24,128]{2,1,0:T(8,128)}), f32[16,24,128]{2,1,0:T(8,128)S(1)}, u32[]{:S(2)}, u32[]{:S(2)}) async-start(f32[16,24,128]{2,1,0:T(8,128)} %broadcast_in_dim.89), calls=%async_computation.4 | async-start | bytes 393216 | tf_op jit(solution)/shard_map/all_to_all | solution.py:487
  168.0 8.8 %norm_grad.1 = bf16[256,1536]{1,0:T(8,128)(2,1)} custom-call(bf16[256,768]{1,0:T(8,128)(2,1)} %get-tuple-element.40.dq_ref, f32[256,768]{1,0:T(8,128)} %get-tuple-element.41.dk_ref, f32[256,768]{1,0:T(8,128)} %get-tuple-element.42.dv_ref, bf16[2,64,768]{2,1,0:T(8,128)(2,1)} %copy-done.5, bf16[2,64,768]{2,1,0:T(8,128)(2,1)} %copy-done.6, ...), custom_call_target="tpu_custom_call" | custom-call | tf_op jit(solution)/shard_map/norm_grad/pallas_call | solution.py:389
  (56 shorter events, 19.4 us)
Async XLA Ops:
  7.2 1.0 copy-start
  7.2 85.2 %all-gather.2.cloned.1.call-start = ((), (), s32[]{:S(2)}) async-start(), calls=%async_computation.5 | async-start | bytes 7299072 | tf_op jit(solution)/shard_map/all_gather | solution.py:481
  37.7 7.6 %copy-start.4 = (f32[1,20,8,32]{3,2,1,0:T(8,128)S(1)}, f32[1,20,8,32]{3,2,1,0:T(8,128)}, u32[]{:S(2)}) copy-start(f32[1,20,8,32]{3,2,1,0:T(8,128)} %param.12) | copy-start | bytes 61444
  37.7 13.6 %copy-start.1 = (bf16[1,8,32,1536]{3,2,1,0:T(8,128)(2,1)S(1)}, bf16[1,8,32,1536]{3,2,1,0:T(8,128)(2,1)}, u32[]{:S(2)}) copy-start(bf16[1,8,32,1536]{3,2,1,0:T(8,128)(2,1)} %param.7) | copy-start | bytes 2359300
  37.7 20.9 %copy-start.9 = (f32[1536]{0:T(1024)S(1)}, f32[1536]{0:T(1024)}, u32[]{:S(2)}) copy-start(f32[1536]{0:T(1024)} %param.8) | copy-start | bytes 18436
  37.7 41.5 %all-to-all-start.1 = ((bf16[16,8,64,128]{3,2,1,0:T(8,128)(2,1)}), bf16[16,8,64,128]{3,2,1,0:T(8,128)(2,1)S(1)}, u32[]{:S(2)}, u32[]{:S(2)}) async-start(bf16[16,8,64,128]{3,2,1,0:T(8,128)(2,1)} %broadcast_in_dim.81), calls=%async_computation.1 | async-start | bytes 4194304 | tf_op jit(solution)/shard_map/all_to_all | solution.py:487
  45.4 25.0 %collective-permute-start.2 = (f32[20,8,1]{2,1,0:T(8,128)S(1)}, f32[20,8,1]{2,1,0:T(8,128)S(1)}, u32[]{:S(2)}, u32[]{:S(2)}) collective-permute-start(f32[20,8,1]{2,1,0:T(8,128)S(1)} %get-tuple-element.55), channel_id=1, source_target_pairs={{0,1},{1,2},{2,3},{3,4},{4,5},{5,6},{6,7},{7,8},{8,9},{9,10},{10,1... | collective-permute-start | bytes 1928 | tf_op jit(solution)/shard_map/ppermute | solution.py:454
  48.7 23.1 %collective-permute-start.3 = (f32[20,8,1]{2,1,0:T(8,128)S(1)}, f32[20,8,1]{2,1,0:T(8,128)S(1)}, u32[]{:S(2)}, u32[]{:S(2)}) collective-permute-start(f32[20,8,1]{2,1,0:T(8,128)S(1)} %get-tuple-element.56), channel_id=1, source_target_pairs={{0,15},{1,0},{2,1},{3,2},{4,3},{5,4},{6,5},{7,6},{8,7},{9,8},{10,9... | collective-permute-start | bytes 1928 | tf_op jit(solution)/shard_map/ppermute | solution.py:454
  51.3 22.8 %collective-permute-start = (bf16[64,1536]{1,0:T(8,128)(2,1)S(1)}, bf16[64,1536]{1,0:T(8,128)(2,1)S(1)}, u32[]{:S(2)}, u32[]{:S(2)}) collective-permute-start(bf16[64,1536]{1,0:T(8,128)(2,1)S(1)} %get-tuple-element.54), channel_id=1, source_target_pairs={{0,1},{1,2},{2,3},{3,4},{4,5},{5,6},{6,7},{7,8},{8,9},{9,10},{10,1... | collective-permute-start | bytes 589832 | tf_op jit(solution)/shard_map/ppermute | solution.py:454
  54.6 20.5 %collective-permute-start.1 = (bf16[64,1536]{1,0:T(8,128)(2,1)S(1)}, bf16[64,1536]{1,0:T(8,128)(2,1)S(1)}, u32[]{:S(2)}, u32[]{:S(2)}) collective-permute-start(bf16[64,1536]{1,0:T(8,128)(2,1)S(1)} %get-tuple-element.53), channel_id=1, source_target_pairs={{0,15},{1,0},{2,1},{3,2},{4,3},{5,4},{6,5},{7,6},{8,7},{9,8},{10,9... | collective-permute-start | bytes 589832 | tf_op jit(solution)/shard_map/ppermute | solution.py:454
  74.0 1.1 copy-start.7
  75.2 0.7 copy-start.8
  79.2 6.3 %copy-start.2 = (bf16[16,8,64,128]{3,2,1,0:T(8,128)(2,1)}, bf16[16,8,64,128]{3,2,1,0:T(8,128)(2,1)S(1)}, u32[]{:S(2)}) copy-start(bf16[16,8,64,128]{3,2,1,0:T(8,128)(2,1)S(1)} %all-to-all-done.1.own_ref) | copy-start | bytes 6291460
  79.2 6.3 %collective-permute-start.4 = (bf16[16,8,64,128]{3,2,1,0:T(8,128)(2,1)S(1)}, bf16[16,8,64,128]{3,2,1,0:T(8,128)(2,1)}, u32[]{:S(2)}, u32[]{:S(2)}) collective-permute-start(bf16[16,8,64,128]{3,2,1,0:T(8,128)(2,1)S(1)} %all-to-all-done.1.own_ref), channel_id=1, source_target_pairs={{0,16},{16,0},{1,17},{17,1},{2,18},{18,2},{3,19},{19,3},{4,20},{20... | collective-permute-start | bytes 6291464 | tf_op jit(solution)/shard_map/ppermute | solution.py:499
  107.7 4.0 %collective-permute-start.5 = (bf16[16,24,640]{2,1,0:T(8,128)(2,1)}, bf16[16,24,640]{2,1,0:T(8,128)(2,1)S(1)}, u32[]{:S(2)}, u32[]{:S(2)}) collective-permute-start(bf16[16,24,640]{2,1,0:T(8,128)(2,1)} %get-tuple-element.44), channel_id=1, source_target_pairs={{0,16},{16,0},{1,17},{17,1},{2,18},{18,2},{3,19},{19,3},{4,20},{20... | collective-permute-start | bytes 1474568 | tf_op jit(solution)/shard_map/ppermute | solution.py:504
  113.7 18.9 %all-to-all-start.2 = ((bf16[16,24,640]{2,1,0:T(8,128)(2,1)}), bf16[16,24,640]{2,1,0:T(8,128)(2,1)S(1)}, u32[]{:S(2)}, u32[]{:S(2)}) async-start(bf16[16,24,640]{2,1,0:T(8,128)(2,1)} %add_convert_fusion), calls=%async_computation.2 | async-start | bytes 983040 | tf_op jit(solution)/shard_map/all_to_all | solution.py:505
  132.6 0.8 copy-start.3
  135.2 24.1 %all-to-all-start.3 = ((f32[16,24,128]{2,1,0:T(8,128)}), f32[16,24,128]{2,1,0:T(8,128)S(1)}, u32[]{:S(2)}, u32[]{:S(2)}) async-start(f32[16,24,128]{2,1,0:T(8,128)} %sum_pieces.1), calls=%async_computation.3 | async-start | bytes 393216 | tf_op jit(solution)/shard_map/all_to_all | solution.py:509
  143.1 24.1 %collective-permute-start.6 = (bf16[2,64,768]{2,1,0:T(8,128)(2,1)}, bf16[2,64,768]{2,1,0:T(8,128)(2,1)S(1)}, u32[]{:S(2)}, u32[]{:S(2)}) collective-permute-start(bf16[2,64,768]{2,1,0:T(8,128)(2,1)} %get-tuple-element.50), channel_id=1, source_target_pairs={{0,1},{1,2},{2,3},{3,4},{4,5},{5,6},{6,7},{7,8},{8,9},{9,10},{10,1... | collective-permute-start | bytes 589832 | tf_op jit(solution)/shard_map/ppermute | solution.py:454
  146.5 20.8 %collective-permute-start.7 = (bf16[2,64,768]{2,1,0:T(8,128)(2,1)}, bf16[2,64,768]{2,1,0:T(8,128)(2,1)S(1)}, u32[]{:S(2)}, u32[]{:S(2)}) collective-permute-start(bf16[2,64,768]{2,1,0:T(8,128)(2,1)} %get-tuple-element.51), channel_id=1, source_target_pairs={{0,15},{1,0},{2,1},{3,2},{4,3},{5,4},{6,5},{7,6},{8,7},{9,8},{10,9... | collective-permute-start | bytes 589832 | tf_op jit(solution)/shard_map/ppermute | solution.py:454
  160.0 16.8 %all-to-all-start.4 = ((f32[16,24,128]{2,1,0:T(8,128)}), f32[16,24,128]{2,1,0:T(8,128)S(1)}, u32[]{:S(2)}, u32[]{:S(2)}) async-start(f32[16,24,128]{2,1,0:T(8,128)} %broadcast_in_dim.89), calls=%async_computation.4 | async-start | bytes 393216 | tf_op jit(solution)/shard_map/all_to_all | solution.py:487
  167.3 0.7 copy-start.5
  167.3 0.7 copy-start.6
Sparse Core Ops, SparseCore 0:
  10.7 81.6 all-gather.1

commit v6 on v5

--- a/solution.py
+++ b/solution.py
@@ -39,6 +39,7 @@
 PADDED = PHASES * LANES
 EPSILON = 1e-05
 SCALE = HEAD_DIM ** (-0.5)
+LOG2_E = 1.4426950408889634
 F32 = jnp.float32
 BF16 = jnp.bfloat16
 WHOLE = pl.BlockSpec(memory_space=pltpu.VMEM)
@@ -169,10 +170,10 @@
 
 
 def softmax_of(query, key):
-    scores = dot_last(query, key) * SCALE
+    scores = dot_last(query, key)
     biggest = jnp.max(scores, axis=-1, keepdims=True)
-    exponent = jnp.exp(scores - biggest)
-    return exponent / jnp.sum(exponent, axis=-1, keepdims=True)
+    exponent = jnp.exp2((scores - biggest) * (SCALE * LOG2_E))
+    return exponent * (1.0 / jnp.sum(exponent, axis=-1, keepdims=True))
 
 
 def forward_group(queries, keys, values):
@@ -529,11 +530,11 @@
     projected, fine_grid, own, send = forward(core, normed, full, tokens, out_full, head, rows, residual)
     pieces = over_tiles(own, send)
     grad_hidden, grad_attended = hidden_grad(rows, head, out_full)
+    pieces, grad_attended = lax.optimization_barrier((pieces, grad_attended))
+    summed = sum_pieces(pieces)
+    grad_attended = lax.optimization_barrier((grad_attended, summed))[0]
     dq, dk, dv, to_left, to_right = attend_backward(projected, grad_attended)
-    pieces, to_left, to_right = lax.optimization_barrier((pieces, to_left, to_right))
-    summed = sum_pieces(pieces)
     grad_head = over_samples(summed)
-    to_left, to_right = lax.optimization_barrier((to_left, to_right, summed))[:2]
     from_right = shifted(to_left, -1)
     from_left = shifted(to_right, 1)
     grad_tokens = norm_grad(dq, dk, dv, from_left, from_right, full, tokens, gain, grad_hidden)

time: 186 us -> 183 us (0.984)
  the two profiles are of different devices: /device:TPU:2 before, /device:TPU:62 now
where the time goes in v6:
time: 183 us; the launch traced here: 181 us
  starting transfers between devices  57.3 us (31%)
  Pallas kernels  44.6 us (24%)
  waiting for transfers between devices  27.1 us (15%)
  blocking collectives  23.7 us (13%)
  between operations  14.3 us (8%)
  local copies, waits for them, and re-layouts  8.46 us (5%)
  matrix products  3.87 us (2%)
  other arithmetic  2.22 us (1%)
    all_to_all x1, blocking collectives, to_all(): return lax.all_to_all(copies, axes, 0, 0, tiled=True)  23.7 us
    ppermute x6, starting transfers between devices, shifted(): lax.ppermute(value, TILE, [(i, (i + steps) % TILES) for i in range(TILES)])  23 us
    pallas_call x1, Pallas kernels, forward(): pl.pallas_call(forward_kernel, out_shape=(jax.ShapeDtypeStruct(projected,...  15.2 us
    all_to_all x2, starting transfers between devices, to_all(): return lax.all_to_all(copies, axes, 0, 0, tiled=True)  14.8 us
    ppermute x6, waiting for transfers between devices, shifted(): lax.ppermute(value, TILE, [(i, (i + steps) % TILES) for i in range(TILES)])  13 us
    pallas_call x1, Pallas kernels, norm_grad(): pl.pallas_call(norm_grad_kernel, out_shape=jax.ShapeDtypeStruct((ROWS, D)...  8.8 us
    all_to_all x1, starting transfers between devices, over_samples(): both = lax.all_to_all(summed, ('dp', 'z'), 0, 0, tiled=True)  8.18 us
    all_to_all x1, starting transfers between devices, over_tiles(): return lax.all_to_all(pair.astype(BF16), TILE, 0, 0, tiled=True)  7.22 us
  transfers between devices with their start and end apart: 13, of which 7 were waited for; matrix products, arithmetic and copies ran while one was open for 4% of the time, Pallas kernels for 15%

profile of v6, /device:TPU:62, one launch (start us, length us, event | category | flops | bytes accessed | tf_op | source)
XLA Modules:
  0.0 181.5 jit_solution(3326104709325049826)
XLA Ops:
  11.4 23.7 %all_to_all.25 = bf16[8,64,128]{2,1,0:T(8,128)(2,1)S(1)} all-to-all(bf16[8,64,128]{2,1,0:T(8,128)(2,1)S(1)} %broadcast_in_dim.80), channel_id=1, replica_groups=mesh['dp'=2,'z'=8,'c'=2,'y'=4,'x'=4] {'z'}, dimensions={0} | all-to-all | bytes 262144 | tf_op jit(solution)/shard_map/all_to_all | solution.py:488
  35.0 1.9 %broadcast_in_dim.81 = bf16[16,8,64,128]{3,2,1,0:T(8,128)(2,1)} broadcast(bf16[8,64,128]{2,1,0:T(8,128)(2,1)S(1)} %all_to_all.25), dimensions={1,2,3} | broadcast | bytes 2228224 | tf_op jit(solution)/shard_map/broadcast_in_dim | solution.py:487
  37.0 7.1 %all-to-all-start.1 = ((bf16[16,8,64,128]{3,2,1,0:T(8,128)(2,1)}), bf16[16,8,64,128]{3,2,1,0:T(8,128)(2,1)S(1)}, u32[]{:S(2)}, u32[]{:S(2)}) async-start(bf16[16,8,64,128]{3,2,1,0:T(8,128)(2,1)} %broadcast_in_dim.81), calls=%async_computation.1 | async-start | bytes 4194304 | tf_op jit(solution)/shard_map/all_to_all | solution.py:488
  44.1 2.0 %collective-permute-start = (bf16[64,1536]{1,0:T(8,128)(2,1)S(1)}, bf16[64,1536]{1,0:T(8,128)(2,1)S(1)}, u32[]{:S(2)}, u32[]{:S(2)}) collective-permute-start(bf16[64,1536]{1,0:T(8,128)(2,1)S(1)} %get-tuple-element.50), channel_id=1, source_target_pairs={{0,1},{1,2},{2,3},{3,4},{4,5},{5,6},{6,7},{7,8},{8,9},{9,10},{10,1... | collective-permute-start | bytes 589832 | tf_op jit(solution)/shard_map/ppermute | solution.py:455
  46.2 3.8 %collective-permute-start.1 = (bf16[64,1536]{1,0:T(8,128)(2,1)S(1)}, bf16[64,1536]{1,0:T(8,128)(2,1)S(1)}, u32[]{:S(2)}, u32[]{:S(2)}) collective-permute-start(bf16[64,1536]{1,0:T(8,128)(2,1)S(1)} %get-tuple-element.49), channel_id=1, source_target_pairs={{0,15},{1,0},{2,1},{3,2},{4,3},{5,4},{6,5},{7,6},{8,7},{9,8},{10,9... | collective-permute-start | bytes 589832 | tf_op jit(solution)/shard_map/ppermute | solution.py:455
  50.1 2.8 %collective-permute-start.3 = (f32[20,8,1]{2,1,0:T(8,128)S(1)}, f32[20,8,1]{2,1,0:T(8,128)S(1)}, u32[]{:S(2)}, u32[]{:S(2)}) collective-permute-start(f32[20,8,1]{2,1,0:T(8,128)S(1)} %get-tuple-element.52), channel_id=1, source_target_pairs={{0,15},{1,0},{2,1},{3,2},{4,3},{5,4},{6,5},{7,6},{8,7},{9,8},{10,9... | collective-permute-start | bytes 1928 | tf_op jit(solution)/shard_map/ppermute | solution.py:455
  52.9 6.4 %collective-permute-start.2 = (f32[20,8,1]{2,1,0:T(8,128)S(1)}, f32[20,8,1]{2,1,0:T(8,128)S(1)}, u32[]{:S(2)}, u32[]{:S(2)}) collective-permute-start(f32[20,8,1]{2,1,0:T(8,128)S(1)} %get-tuple-element.51), channel_id=1, source_target_pairs={{0,1},{1,2},{2,3},{3,4},{4,5},{5,6},{6,7},{7,8},{8,9},{9,10},{10,1... | collective-permute-start | bytes 1928 | tf_op jit(solution)/shard_map/ppermute | solution.py:455
  59.9 12.2 %collective-permute-done.3 = f32[20,8,1]{2,1,0:T(8,128)S(1)} collective-permute-done((f32[20,8,1]{2,1,0:T(8,128)S(1)}, f32[20,8,1]{2,1,0:T(8,128)S(1)}, u32[]{:S(2)}, u32[]{:S(2)}) %collective-permute-start.3) | collective-permute-done | bytes 672 | tf_op jit(solution)/shard_map/ppermute | solution.py:455
  74.6 3.3 %prepare.1 = (bf16[384,1536]{1,0:T(8,128)(2,1)}, bf16[256,512]{1,0:T(8,128)(2,1)}) custom-call(bf16[256,1536]{1,0:T(8,128)(2,1)} %bitcast.44, bf16[64,1536]{1,0:T(8,128)(2,1)} %copy-done.7, bf16[64,1536]{1,0:T(8,128)(2,1)} %copy-done.8, f32[1,1536]{1,0:T(1,128)} %reshape.151.gain_ref, f32[20,32,128]{2,1,0:T(8,128)} %bitcast.56), custom_call_target="tpu_custom_call" | custom-call | tf_op jit(solution)/shard_map/prepare/pallas_call | solution.py:92
  77.9 1.9 %collective-permute-start.4 = (bf16[16,8,64,128]{3,2,1,0:T(8,128)(2,1)S(1)}, bf16[16,8,64,128]{3,2,1,0:T(8,128)(2,1)}, u32[]{:S(2)}, u32[]{:S(2)}) collective-permute-start(bf16[16,8,64,128]{3,2,1,0:T(8,128)(2,1)S(1)} %all-to-all-done.1.own_ref), channel_id=1, source_target_pairs={{0,16},{16,0},{1,17},{17,1},{2,18},{18,2},{3,19},{19,3},{4,20},{20... | collective-permute-start | bytes 6291464 | tf_op jit(solution)/shard_map/ppermute | solution.py:500
  79.9 4.3 %collective-permute-done.4.other_ref = bf16[16,8,64,128]{3,2,1,0:T(8,128)(2,1)} collective-permute-done((bf16[16,8,64,128]{3,2,1,0:T(8,128)(2,1)S(1)}, bf16[16,8,64,128]{3,2,1,0:T(8,128)(2,1)}, u32[]{:S(2)}, u32[]{:S(2)}) %collective-permute-start.4) | collective-permute-done | bytes 2097184 | tf_op jit(solution)/shard_map/ppermute | solution.py:500
  84.2 4.0 %unpack.1 = (bf16[768,1536]{1,0:T(8,128)(2,1)}, bf16[1536,512]{1,0:T(8,128)(2,1)}) custom-call(s32[1]{0:T(128)} %bitcast.core_ref, bf16[16,8,64,128]{3,2,1,0:T(8,128)(2,1)} %copy-done.2, bf16[16,8,64,128]{3,2,1,0:T(8,128)(2,1)} %collective-permute-done.4.other_ref), custom_call_target="tpu_custom_call" | custom-call | tf_op jit(solution)/shard_map/unpack/pallas_call | solution.py:121
  88.2 3.7 %all-gather.2.cloned.1.call-done = bf16[3072,1152]{1,0:T(8,128)(2,1)} async-done(((bf16[96,1152]{1,0:T(8,128)(2,1)}), bf16[3072,1152]{1,0:T(8,128)(2,1)}) %all-gather.2.cloned.1.call-update) | async-done | bytes 7077904 | tf_op jit(solution)/shard_map/all_gather | solution.py:482
  92.0 15.2 %forward.1 = (bf16[6,384,384]{2,1,0:T(8,128)(2,1)}, f32[20,32,128]{2,1,0:T(8,128)}, f32[16,24,640]{2,1,0:T(8,128)}, bf16[16,24,640]{2,1,0:T(8,128)(2,1)}) custom-call(s32[1]{0:T(128)} %bitcast.core_ref, bf16[384,1536]{1,0:T(8,128)(2,1)} %get-tuple-element.26.normed_ref, bf16[2,1536,1152]{2,1,0:T(8,128)(2,1)} %bitcast.41, bf16[256,1536]{1,0:T(8,128)(2,1)} %bitcast.45, ...), custom_call_target="tpu_custom_call" | custom-call | tf_op jit(solution)/shard_map/forward/pallas_call | solution.py:262
  107.2 2.1 %collective-permute-start.5 = (bf16[16,24,640]{2,1,0:T(8,128)(2,1)}, bf16[16,24,640]{2,1,0:T(8,128)(2,1)S(1)}, u32[]{:S(2)}, u32[]{:S(2)}) collective-permute-start(bf16[16,24,640]{2,1,0:T(8,128)(2,1)} %get-tuple-element.38), channel_id=1, source_target_pairs={{0,16},{16,0},{1,17},{17,1},{2,18},{18,2},{3,19},{19,3},{4,20},{20... | collective-permute-start | bytes 1474568 | tf_op jit(solution)/shard_map/ppermute | solution.py:505
  111.1 2.1 %add_convert_fusion = bf16[16,24,640]{2,1,0:T(8,128)(2,1)} fusion(f32[16,24,640]{2,1,0:T(8,128)} %get-tuple-element.37, bf16[16,24,640]{2,1,0:T(8,128)(2,1)S(1)} %collective-permute-done.5), kind=kLoop, calls=%fused_computation.3 | loop fusion | flops 737280 | bytes 1966080 | tf_op jit(solution)/shard_map/convert_element_type | solution.py:506
  113.2 7.2 %all-to-all-start.2 = ((bf16[16,24,640]{2,1,0:T(8,128)(2,1)}), bf16[16,24,640]{2,1,0:T(8,128)(2,1)S(1)}, u32[]{:S(2)}, u32[]{:S(2)}) async-start(bf16[16,24,640]{2,1,0:T(8,128)(2,1)} %add_convert_fusion), calls=%async_computation.2 | async-start | bytes 983040 | tf_op jit(solution)/shard_map/all_to_all | solution.py:506
  120.4 4.4 %hidden_grad.1 = (f32[256,1536]{1,0:T(8,128)}, bf16[256,768]{1,0:T(8,128)(2,1)}) custom-call(bf16[256,512]{1,0:T(8,128)(2,1)} %get-tuple-element.33.rows_hbm.rows_ref, bf16[1536,512]{1,0:T(8,128)(2,1)} %get-tuple-element.32.head_hbm.head_ref, bf16[768,1536]{1,0:T(8,128)(2,1)} %get-tuple-element.31.out_hbm.out_ref), custom_call_target="tpu_custom_call" | custom-call | tf_op jit(solution)/shard_map/hidden_grad/pallas_call | solution.py:144
  124.9 3.1 %all-to-all-done.2.pieces_ref = bf16[16,24,640]{2,1,0:T(8,128)(2,1)S(1)} async-done(((bf16[16,24,640]{2,1,0:T(8,128)(2,1)}), bf16[16,24,640]{2,1,0:T(8,128)(2,1)S(1)}, u32[]{:S(2)}, u32[]{:S(2)}) %all-to-all-start.2) | async-done | bytes 491552 | tf_op jit(solution)/shard_map/all_to_all | solution.py:506
  130.6 8.2 %all-to-all-start.3 = ((f32[16,24,128]{2,1,0:T(8,128)}), f32[16,24,128]{2,1,0:T(8,128)S(1)}, u32[]{:S(2)}, u32[]{:S(2)}) async-start(f32[16,24,128]{2,1,0:T(8,128)} %sum_pieces.1), calls=%async_computation.3 | async-start | bytes 393216 | tf_op jit(solution)/shard_map/all_to_all | solution.py:510
  138.8 6.9 %attend_backward.1 = (bf16[256,768]{1,0:T(8,128)(2,1)}, f32[256,768]{1,0:T(8,128)}, f32[256,768]{1,0:T(8,128)}, bf16[2,64,768]{2,1,0:T(8,128)(2,1)}, bf16[2,64,768]{2,1,0:T(8,128)(2,1)}) custom-call(bf16[6,384,384]{2,1,0:T(8,128)(2,1)} %get-tuple-element.36.q_ref.k_ref.v_ref, bf16[6,384,384]{2,1,0:T(8,128)(2,1)} %get-tuple-element.36.q_ref.k_ref.v_ref, ...), custom_call_target="tpu_custom_call" | custom-call | tf_op jit(solution)/shard_map/attend_backward/pallas_call | solution.py:337
  145.7 6.1 %collective-permute-start.6 = (bf16[2,64,768]{2,1,0:T(8,128)(2,1)}, bf16[2,64,768]{2,1,0:T(8,128)(2,1)S(1)}, u32[]{:S(2)}, u32[]{:S(2)}) collective-permute-start(bf16[2,64,768]{2,1,0:T(8,128)(2,1)} %get-tuple-element.46), channel_id=1, source_target_pairs={{0,1},{1,2},{2,3},{3,4},{4,5},{5,6},{6,7},{7,8},{8,9},{9,10},{10,1... | collective-permute-start | bytes 589832 | tf_op jit(solution)/shard_map/ppermute | solution.py:455
  155.5 7.7 %all-to-all-start.4 = ((f32[16,24,128]{2,1,0:T(8,128)}), f32[16,24,128]{2,1,0:T(8,128)S(1)}, u32[]{:S(2)}, u32[]{:S(2)}) async-start(f32[16,24,128]{2,1,0:T(8,128)} %broadcast_in_dim.89), calls=%async_computation.4 | async-start | bytes 393216 | tf_op jit(solution)/shard_map/all_to_all | solution.py:488
  164.6 8.8 %norm_grad.1 = bf16[256,1536]{1,0:T(8,128)(2,1)} custom-call(bf16[256,768]{1,0:T(8,128)(2,1)} %get-tuple-element.43.dq_ref, f32[256,768]{1,0:T(8,128)} %get-tuple-element.44.dk_ref, f32[256,768]{1,0:T(8,128)} %get-tuple-element.45.dv_ref, bf16[2,64,768]{2,1,0:T(8,128)(2,1)} %copy-done.5, bf16[2,64,768]{2,1,0:T(8,128)(2,1)} %copy-done.6, ...), custom_call_target="tpu_custom_call" | custom-call | tf_op jit(solution)/shard_map/norm_grad/pallas_call | solution.py:390
  (56 shorter events, 18.1 us)
Async XLA Ops:
  7.2 1.0 copy-start
  7.2 84.8 %all-gather.2.cloned.1.call-start = ((), (), s32[]{:S(2)}) async-start(), calls=%async_computation.5 | async-start | bytes 7299072 | tf_op jit(solution)/shard_map/all_gather | solution.py:482
  37.0 7.1 %copy-start.1 = (bf16[1,8,32,1536]{3,2,1,0:T(8,128)(2,1)S(1)}, bf16[1,8,32,1536]{3,2,1,0:T(8,128)(2,1)}, u32[]{:S(2)}) copy-start(bf16[1,8,32,1536]{3,2,1,0:T(8,128)(2,1)} %param.7) | copy-start | bytes 2359300
  37.0 13.0 %copy-start.4 = (f32[1,20,8,32]{3,2,1,0:T(8,128)S(1)}, f32[1,20,8,32]{3,2,1,0:T(8,128)}, u32[]{:S(2)}) copy-start(f32[1,20,8,32]{3,2,1,0:T(8,128)} %param.12) | copy-start | bytes 61444
  37.0 22.4 %copy-start.9 = (f32[1536]{0:T(1024)S(1)}, f32[1536]{0:T(1024)}, u32[]{:S(2)}) copy-start(f32[1536]{0:T(1024)} %param.8) | copy-start | bytes 18436
  37.0 40.9 %all-to-all-start.1 = ((bf16[16,8,64,128]{3,2,1,0:T(8,128)(2,1)}), bf16[16,8,64,128]{3,2,1,0:T(8,128)(2,1)S(1)}, u32[]{:S(2)}, u32[]{:S(2)}) async-start(bf16[16,8,64,128]{3,2,1,0:T(8,128)(2,1)} %broadcast_in_dim.81), calls=%async_computation.1 | async-start | bytes 4194304 | tf_op jit(solution)/shard_map/all_to_all | solution.py:488
  44.1 29.7 %collective-permute-start = (bf16[64,1536]{1,0:T(8,128)(2,1)S(1)}, bf16[64,1536]{1,0:T(8,128)(2,1)S(1)}, u32[]{:S(2)}, u32[]{:S(2)}) collective-permute-start(bf16[64,1536]{1,0:T(8,128)(2,1)S(1)} %get-tuple-element.50), channel_id=1, source_target_pairs={{0,1},{1,2},{2,3},{3,4},{4,5},{5,6},{6,7},{7,8},{8,9},{9,10},{10,1... | collective-permute-start | bytes 589832 | tf_op jit(solution)/shard_map/ppermute | solution.py:455
  46.2 27.7 %collective-permute-start.1 = (bf16[64,1536]{1,0:T(8,128)(2,1)S(1)}, bf16[64,1536]{1,0:T(8,128)(2,1)S(1)}, u32[]{:S(2)}, u32[]{:S(2)}) collective-permute-start(bf16[64,1536]{1,0:T(8,128)(2,1)S(1)} %get-tuple-element.49), channel_id=1, source_target_pairs={{0,15},{1,0},{2,1},{3,2},{4,3},{5,4},{6,5},{7,6},{8,7},{9,8},{10,9... | collective-permute-start | bytes 589832 | tf_op jit(solution)/shard_map/ppermute | solution.py:455
  50.1 22.1 %collective-permute-start.3 = (f32[20,8,1]{2,1,0:T(8,128)S(1)}, f32[20,8,1]{2,1,0:T(8,128)S(1)}, u32[]{:S(2)}, u32[]{:S(2)}) collective-permute-start(f32[20,8,1]{2,1,0:T(8,128)S(1)} %get-tuple-element.52), channel_id=1, source_target_pairs={{0,15},{1,0},{2,1},{3,2},{4,3},{5,4},{6,5},{7,6},{8,7},{9,8},{10,9... | collective-permute-start | bytes 1928 | tf_op jit(solution)/shard_map/ppermute | solution.py:455
  52.9 19.3 %collective-permute-start.2 = (f32[20,8,1]{2,1,0:T(8,128)S(1)}, f32[20,8,1]{2,1,0:T(8,128)S(1)}, u32[]{:S(2)}, u32[]{:S(2)}) collective-permute-start(f32[20,8,1]{2,1,0:T(8,128)S(1)} %get-tuple-element.51), channel_id=1, source_target_pairs={{0,1},{1,2},{2,3},{3,4},{4,5},{5,6},{6,7},{7,8},{8,9},{9,10},{10,1... | collective-permute-start | bytes 1928 | tf_op jit(solution)/shard_map/ppermute | solution.py:455
  73.8 0.7 copy-start.7
  73.8 0.7 copy-start.8
  77.9 6.3 %copy-start.2 = (bf16[16,8,64,128]{3,2,1,0:T(8,128)(2,1)}, bf16[16,8,64,128]{3,2,1,0:T(8,128)(2,1)S(1)}, u32[]{:S(2)}) copy-start(bf16[16,8,64,128]{3,2,1,0:T(8,128)(2,1)S(1)} %all-to-all-done.1.own_ref) | copy-start | bytes 6291460
  77.9 6.3 %collective-permute-start.4 = (bf16[16,8,64,128]{3,2,1,0:T(8,128)(2,1)S(1)}, bf16[16,8,64,128]{3,2,1,0:T(8,128)(2,1)}, u32[]{:S(2)}, u32[]{:S(2)}) collective-permute-start(bf16[16,8,64,128]{3,2,1,0:T(8,128)(2,1)S(1)} %all-to-all-done.1.own_ref), channel_id=1, source_target_pairs={{0,16},{16,0},{1,17},{17,1},{2,18},{18,2},{3,19},{19,3},{4,20},{20... | collective-permute-start | bytes 6291464 | tf_op jit(solution)/shard_map/ppermute | solution.py:500
  107.2 4.0 %collective-permute-start.5 = (bf16[16,24,640]{2,1,0:T(8,128)(2,1)}, bf16[16,24,640]{2,1,0:T(8,128)(2,1)S(1)}, u32[]{:S(2)}, u32[]{:S(2)}) collective-permute-start(bf16[16,24,640]{2,1,0:T(8,128)(2,1)} %get-tuple-element.38), channel_id=1, source_target_pairs={{0,16},{16,0},{1,17},{17,1},{2,18},{18,2},{3,19},{19,3},{4,20},{20... | collective-permute-start | bytes 1474568 | tf_op jit(solution)/shard_map/ppermute | solution.py:505
  113.2 14.7 %all-to-all-start.2 = ((bf16[16,24,640]{2,1,0:T(8,128)(2,1)}), bf16[16,24,640]{2,1,0:T(8,128)(2,1)S(1)}, u32[]{:S(2)}, u32[]{:S(2)}) async-start(bf16[16,24,640]{2,1,0:T(8,128)(2,1)} %add_convert_fusion), calls=%async_computation.2 | async-start | bytes 983040 | tf_op jit(solution)/shard_map/all_to_all | solution.py:506
  127.9 0.8 copy-start.3
  130.6 24.2 %all-to-all-start.3 = ((f32[16,24,128]{2,1,0:T(8,128)}), f32[16,24,128]{2,1,0:T(8,128)S(1)}, u32[]{:S(2)}, u32[]{:S(2)}) async-start(f32[16,24,128]{2,1,0:T(8,128)} %sum_pieces.1), calls=%async_computation.3 | async-start | bytes 393216 | tf_op jit(solution)/shard_map/all_to_all | solution.py:510
  145.7 17.5 %collective-permute-start.6 = (bf16[2,64,768]{2,1,0:T(8,128)(2,1)}, bf16[2,64,768]{2,1,0:T(8,128)(2,1)S(1)}, u32[]{:S(2)}, u32[]{:S(2)}) collective-permute-start(bf16[2,64,768]{2,1,0:T(8,128)(2,1)} %get-tuple-element.46), channel_id=1, source_target_pairs={{0,1},{1,2},{2,3},{3,4},{4,5},{5,6},{6,7},{7,8},{8,9},{9,10},{10,1... | collective-permute-start | bytes 589832 | tf_op jit(solution)/shard_map/ppermute | solution.py:455
  151.8 12.2 %collective-permute-start.7 = (bf16[2,64,768]{2,1,0:T(8,128)(2,1)}, bf16[2,64,768]{2,1,0:T(8,128)(2,1)S(1)}, u32[]{:S(2)}, u32[]{:S(2)}) collective-permute-start(bf16[2,64,768]{2,1,0:T(8,128)(2,1)} %get-tuple-element.47), channel_id=1, source_target_pairs={{0,15},{1,0},{2,1},{3,2},{4,3},{5,4},{6,5},{7,6},{8,7},{9,8},{10,9... | collective-permute-start | bytes 589832 | tf_op jit(solution)/shard_map/ppermute | solution.py:455
  155.5 17.9 %all-to-all-start.4 = ((f32[16,24,128]{2,1,0:T(8,128)}), f32[16,24,128]{2,1,0:T(8,128)S(1)}, u32[]{:S(2)}, u32[]{:S(2)}) async-start(f32[16,24,128]{2,1,0:T(8,128)} %broadcast_in_dim.89), calls=%async_computation.4 | async-start | bytes 393216 | tf_op jit(solution)/shard_map/all_to_all | solution.py:488
  163.2 0.8 copy-start.5
  163.9 0.7 copy-start.6
Sparse Core Ops, SparseCore 0:
  10.7 81.2 all-gather.1

commit v7 on v4

--- a/solution.py
+++ b/solution.py
@@ -39,6 +39,7 @@
 PADDED = PHASES * LANES
 EPSILON = 1e-05
 SCALE = HEAD_DIM ** (-0.5)
+LOG2_E = 1.4426950408889634
 F32 = jnp.float32
 BF16 = jnp.bfloat16
 WHOLE = pl.BlockSpec(memory_space=pltpu.VMEM)
@@ -169,10 +170,10 @@
 
 
 def softmax_of(query, key):
-    scores = dot_last(query, key) * SCALE
+    scores = dot_last(query, key)
     biggest = jnp.max(scores, axis=-1, keepdims=True)
-    exponent = jnp.exp(scores - biggest)
-    return exponent / jnp.sum(exponent, axis=-1, keepdims=True)
+    exponent = jnp.exp2((scores - biggest) * (SCALE * LOG2_E))
+    return exponent * (1.0 / jnp.sum(exponent, axis=-1, keepdims=True))
 
 
 def forward_group(queries, keys, values):
@@ -190,8 +191,8 @@
 def forward_kernel(
     normed_ref, weight_ref,
     tokens_hbm, out_hbm, head_hbm, rows_hbm, residual_hbm,
-    projected_ref, fine_ref, pieces_ref,
-    tokens_ref, out_ref, head_ref, rows_ref, residual_ref, products, sems,
+    projected_out, fine_ref, pieces_hbm,
+    projected_ref, pieces_ref, tokens_ref, out_ref, head_ref, rows_ref, residual_ref, products, sems,
 ):
     step = pl.program_id(0)
     copies = [
@@ -214,11 +215,16 @@
 
     @pl.when(step < 2)
     def _():
-        projected_ref[step, :ROWS] = dot(normed_ref[:ROWS], weight_ref[0]).astype(BF16)
+        queries = dot(normed_ref[:ROWS], weight_ref[0]).astype(BF16)
+        projected_ref[step, :ROWS] = queries
+        projected_out[0, :ROWS] = queries
+        projected_out[0, ROWS:] = jnp.zeros((2 * EDGE, GROUP), BF16)
 
     @pl.when(step >= 2)
     def _():
-        projected_ref[step] = dot(normed_ref[...], weight_ref[0]).astype(BF16)
+        pairs = dot(normed_ref[...], weight_ref[0]).astype(BF16)
+        projected_ref[step] = pairs
+        projected_out[0] = pairs
 
     @pl.when(step == 5)
     def _():
@@ -230,7 +236,6 @@
             copy.wait()
         mixed = dot(attended[0], out_ref[:GROUP]) + dot(attended[1], out_ref[GROUP:])
         hidden = (tokens_ref[...].astype(F32) + mixed).astype(BF16)
-        head_out = dot(hidden, head_ref[...])
         products[...] = dot_first(hidden, rows_ref[...])
         for core in range(CORES):
             for quad in range(4):
@@ -243,6 +248,9 @@
                         for z in range(ZS)
                     ]
                     pieces_ref[core * TILES + quad * 4 + phase] = jnp.concatenate(row, axis=1).astype(BF16)
+        send = pltpu.make_async_copy(pieces_ref, pieces_hbm, sems.at[5])
+        send.start()
+        head_out = dot(hidden, head_ref[...])
         select = spread_matrix()
         for lat in range(LAT):
             at = slice(lat * LON_DEV, (lat + 1) * LON_DEV)
@@ -254,6 +262,7 @@
             spread = dot_first(high, select) + dot_first(low, select)
             across = slice(PHASES * lat, PHASES * (lat + 1))
             fine_ref[:, across, :] = spread[:CHANNELS].reshape(VARS, PHASES, LANES) + residual_ref[:, across, :]
+        send.wait()
 
 
 def forward(normed, full, tokens, out_weight, head, rows, residual):
@@ -273,15 +282,21 @@
             pl.BlockSpec((1, D, GROUP), lambda n: (n // 3, 0, n % 3)),
         ]
         + [pl.BlockSpec(memory_space=pl.ANY)] * 5,
-        out_specs=(whole_block(projected), whole_block(fine), whole_block(pieces)),
+        out_specs=(
+            pl.BlockSpec((1, KEYS, GROUP), lambda n: (n, 0, 0)),
+            whole_block(fine),
+            pl.BlockSpec(memory_space=pl.ANY),
+        ),
         scratch_shapes=[
+            pltpu.VMEM(projected, BF16),
+            pltpu.VMEM(pieces, BF16),
             pltpu.VMEM((ROWS, D), BF16),
             pltpu.VMEM((INNER, D), BF16),
             pltpu.VMEM((D, PADDED), BF16),
             pltpu.VMEM((ROWS, PADDED), BF16),
             pltpu.VMEM(fine, F32),
             pltpu.VMEM((D, PADDED), F32),
-            pltpu.SemaphoreType.DMA((5,)),
+            pltpu.SemaphoreType.DMA((6,)),
         ],
         name="forward",
     )(normed, full, tokens, out_weight, head, rows, residual)
@@ -420,7 +435,7 @@
         total = total + pieces_ref[place].astype(F32)
     empty = jnp.zeros((24, LANES - CHANNELS), F32)
     for z in range(ZS):
-        part = jnp.concatenate([total[:, z * CHANNELS : (z + 1) * CHANNELS], empty], axis=1)
+        part = jnp.concatenate([total[:, z * CHANNELS : (z + 1) * CHANNELS], empty], axis=1).astype(BF16)
         out_ref[z] = part
         out_ref[ZS + z] = part
 
@@ -428,7 +443,7 @@
 def sum_pieces(pieces):
     return pl.pallas_call(
         sum_kernel,
-        out_shape=jax.ShapeDtypeStruct((2 * ZS, 24, LANES), F32),
+        out_shape=jax.ShapeDtypeStruct((2 * ZS, 24, LANES), BF16),
         in_specs=[WHOLE],
         out_specs=WHOLE,
         name="sum_pieces",
@@ -487,7 +502,7 @@
     return lax.all_to_all(copies, axes, 0, 0, tiled=True)
 
 
-def gather_rest(out_w, head_w, ready):
+def gather_rest(core, out_w, head_w, ready):
     out_rows = out_w.reshape(48, 12, LANES).transpose(1, 0, 2).reshape(576, LANES)
     head_pad = dot(head_w, head_columns().astype(BF16)).astype(BF16)
     head_rows = head_pad.reshape(96, PHASES, LANES).transpose(1, 0, 2).reshape(384, LANES)
@@ -497,13 +512,12 @@
     over_tile = to_all(over_z, TILE, TILES)
     over_tile = lax.optimization_barrier((over_tile, ready))[0]
     other = lax.ppermute(over_tile, "c", [(0, 1), (1, 0)])
-    return unpack(lax.axis_index("c").reshape(1).astype(jnp.int32), over_tile, other)
-
-
-def reduce_head(pieces):
-    pieces = lax.all_to_all(pieces, ("c",) + TILE, 0, 0, tiled=True)
-    both = lax.all_to_all(sum_pieces(pieces), ("dp", "z"), 0, 0, tiled=True)
-    spread = to_all(jnp.sum(both, axis=0), TILE, TILES)
+    return unpack(core, over_tile, other)
+
+
+def over_samples(summed):
+    both = lax.all_to_all(summed, ("dp", "z"), 0, 0, tiled=True)
+    spread = to_all(jnp.sum(both.astype(F32), axis=0), TILE, TILES)
     padded = spread.reshape(4, PHASES, 24, LANES).transpose(0, 2, 1, 3).reshape(96, PADDED)
     return lax.dot_general(
         padded, head_columns(), (((1,), (1,)), ((), ())), precision=lax.Precision.HIGHEST, preferred_element_type=F32
@@ -519,14 +533,17 @@
     right = shifted(grid[:, :MARGIN].reshape(EDGE, D), -1)
     residual = residual_of(coarse[0])
     normed, rows = prepare(tokens, left, right, gain, grad_fine[0])
-    out_full, head = gather_rest(out_weight, head_weight, (normed, residual))
+    core = lax.axis_index("c").reshape(1).astype(jnp.int32)
+    out_full, head = gather_rest(core, out_weight, head_weight, (normed, residual))
+    full, out_full, head, residual = lax.optimization_barrier((full, out_full, head, residual))
+    projected, fine_grid, pieces = forward(normed, full, tokens, out_full, head, rows, residual)
+    pieces = lax.all_to_all(pieces, ("c",) + TILE, 0, 0, tiled=True)
     grad_hidden, grad_attended = hidden_grad(rows, head, out_full)
-    full, grad_hidden, grad_attended, residual = lax.optimization_barrier(
-        (full, grad_hidden, grad_attended, residual)
-    )
-    projected, fine_grid, pieces = forward(normed, full, tokens, out_full, head, rows, residual)
-    grad_head = reduce_head(pieces)
     dq, dk, dv, to_left, to_right = attend_backward(projected, grad_attended)
+    pieces, to_left, to_right = lax.optimization_barrier((pieces, to_left, to_right))
+    summed = sum_pieces(pieces)
+    grad_head = over_samples(summed)
+    to_left, to_right = lax.optimization_barrier((to_left, to_right, summed))[:2]
     from_right = shifted(to_left, -1)
     from_left = shifted(to_right, 1)
     grad_tokens = norm_grad(dq, dk, dv, from_left, from_right, full, tokens, gain, grad_hidden)

time: 182 us -> 179 us (0.984)
  blocking collectives: 46.5 us -> 24.4 us
  waiting for transfers between devices: 20.8 us -> 32.4 us
  starting transfers between devices: 43.5 us -> 49.9 us
    all_to_all x1 -> x0, blocking collectives: 22.1 us -> none  [reduce_head(): pieces = lax.all_to_all(pieces, ('c',) + TILE, 0, 0, tiled=True)]
    all_to_all x1 -> x2, waiting for transfers between devices: 2.08 us -> 10.8 us  [the longest x1 7.47 us: over_samples(): both = lax.all_to_all(summed, ('dp', 'z'), 0, 0, tiled=True)]
    all_to_all x1 -> x2, starting transfers between devices: 7.74 us -> 15.5 us  [the longest x1 7.9 us: over_samples(): both = lax.all_to_all(summed, ('dp', 'z'), 0, 0, tiled=True)]
    all_gather x1, waiting for transfers between devices: 0.01 us -> 2.89 us  [gather_qkv(): full = lax.all_gather(qkv_half, ('dp',) + FSDP, axis=0, tiled=True)]
  transfers between devices with their start and end apart: 11 -> 12, of which waited for: 5 -> 7; matrix products, arithmetic and copies ran while one was open for 4% -> 4% of each run, Pallas kernels for 15% -> 15%
where the time goes in v7:
time: 179 us
  starting transfers between devices  49.9 us (28%)
  Pallas kernels  44.8 us (25%)
  waiting for transfers between devices  32.4 us (18%)
  blocking collectives  24.4 us (14%)
  between operations  14.3 us (8%)
  local copies, waits for them, and re-layouts  8.74 us (5%)
  matrix products  3.88 us (2%)
    all_to_all x1, blocking collectives, to_all(): return lax.all_to_all(copies, axes, 0, 0, tiled=True)  24.4 us
    ppermute x6, starting transfers between devices, shifted(): lax.ppermute(value, TILE, [(i, (i + steps) % TILES) for i in range(TILES)])  19.6 us
    pallas_call x1, Pallas kernels, forward(): pl.pallas_call(forward_kernel, out_shape=(jax.ShapeDtypeStruct(projected,...  15.3 us
    ppermute x6, waiting for transfers between devices, shifted(): lax.ppermute(value, TILE, [(i, (i + steps) % TILES) for i in range(TILES)])  14.3 us
    all_to_all x2, starting transfers between devices, to_all(): return lax.all_to_all(copies, axes, 0, 0, tiled=True)  12.8 us
    pallas_call x1, Pallas kernels, norm_grad(): pl.pallas_call(norm_grad_kernel, out_shape=jax.ShapeDtypeStruct((ROWS, D)...  8.8 us
    all_to_all x1, starting transfers between devices, over_samples(): both = lax.all_to_all(summed, ('dp', 'z'), 0, 0, tiled=True)  7.9 us
    all_to_all x1, starting transfers between devices, shards(): pieces = lax.all_to_all(pieces, ('c',) + TILE, 0, 0, tiled=True)  7.58 us
  transfers between devices with their start and end apart: 12, of which 7 were waited for; matrix products, arithmetic and copies ran while one was open for 4% of the time, Pallas kernels for 15%

profile of v7, /device:TPU:2, one launch (start us, length us, event | category | flops | bytes accessed | tf_op | source)
XLA Modules:
  0.0 178.5 jit_solution(2429165730676578918)
XLA Ops:
  11.4 24.4 %all_to_all.25 = bf16[8,64,128]{2,1,0:T(8,128)(2,1)S(1)} all-to-all(bf16[8,64,128]{2,1,0:T(8,128)(2,1)S(1)} %broadcast_in_dim.80), channel_id=1, replica_groups=mesh['dp'=2,'z'=8,'c'=2,'y'=4,'x'=4] {'z'}, dimensions={0} | all-to-all | bytes 262144 | tf_op jit(solution)/shard_map/all_to_all | solution.py:502
  35.7 1.9 %broadcast_in_dim.81 = bf16[16,8,64,128]{3,2,1,0:T(8,128)(2,1)} broadcast(bf16[8,64,128]{2,1,0:T(8,128)(2,1)S(1)} %all_to_all.25), dimensions={1,2,3} | broadcast | bytes 2228224 | tf_op jit(solution)/shard_map/broadcast_in_dim | solution.py:501
  37.7 7.6 %all-to-all-start.1 = ((bf16[16,8,64,128]{3,2,1,0:T(8,128)(2,1)}), bf16[16,8,64,128]{3,2,1,0:T(8,128)(2,1)S(1)}, u32[]{:S(2)}, u32[]{:S(2)}) async-start(bf16[16,8,64,128]{3,2,1,0:T(8,128)(2,1)} %broadcast_in_dim.81), calls=%async_computation.1 | async-start | bytes 4194304 | tf_op jit(solution)/shard_map/all_to_all | solution.py:502
  45.4 3.4 %collective-permute-start.2 = (f32[20,8,1]{2,1,0:T(8,128)S(1)}, f32[20,8,1]{2,1,0:T(8,128)S(1)}, u32[]{:S(2)}, u32[]{:S(2)}) collective-permute-start(f32[20,8,1]{2,1,0:T(8,128)S(1)} %get-tuple-element.53), channel_id=1, source_target_pairs={{0,1},{1,2},{2,3},{3,4},{4,5},{5,6},{6,7},{7,8},{8,9},{9,10},{10,1... | collective-permute-start | bytes 1928 | tf_op jit(solution)/shard_map/ppermute | solution.py:469
  48.7 2.5 %collective-permute-start.3 = (f32[20,8,1]{2,1,0:T(8,128)S(1)}, f32[20,8,1]{2,1,0:T(8,128)S(1)}, u32[]{:S(2)}, u32[]{:S(2)}) collective-permute-start(f32[20,8,1]{2,1,0:T(8,128)S(1)} %get-tuple-element.54), channel_id=1, source_target_pairs={{0,15},{1,0},{2,1},{3,2},{4,3},{5,4},{6,5},{7,6},{8,7},{9,8},{10,9... | collective-permute-start | bytes 1928 | tf_op jit(solution)/shard_map/ppermute | solution.py:469
  51.3 5.3 %collective-permute-start.1 = (bf16[64,1536]{1,0:T(8,128)(2,1)S(1)}, bf16[64,1536]{1,0:T(8,128)(2,1)S(1)}, u32[]{:S(2)}, u32[]{:S(2)}) collective-permute-start(bf16[64,1536]{1,0:T(8,128)(2,1)S(1)} %get-tuple-element.51), channel_id=1, source_target_pairs={{0,15},{1,0},{2,1},{3,2},{4,3},{5,4},{6,5},{7,6},{8,7},{9,8},{10,9... | collective-permute-start | bytes 589832 | tf_op jit(solution)/shard_map/ppermute | solution.py:469
  59.2 11.1 %collective-permute-done.2 = f32[20,8,1]{2,1,0:T(8,128)S(1)} collective-permute-done((f32[20,8,1]{2,1,0:T(8,128)S(1)}, f32[20,8,1]{2,1,0:T(8,128)S(1)}, u32[]{:S(2)}, u32[]{:S(2)}) %collective-permute-start.2) | collective-permute-done | bytes 672 | tf_op jit(solution)/shard_map/ppermute | solution.py:469
  75.9 3.3 %prepare.1 = (bf16[384,1536]{1,0:T(8,128)(2,1)}, bf16[256,512]{1,0:T(8,128)(2,1)}) custom-call(bf16[256,1536]{1,0:T(8,128)(2,1)} %bitcast.44, bf16[64,1536]{1,0:T(8,128)(2,1)} %copy-done.8, bf16[64,1536]{1,0:T(8,128)(2,1)} %copy-done.7, f32[1,1536]{1,0:T(1,128)} %reshape.150.gain_ref, f32[20,32,128]{2,1,0:T(8,128)} %bitcast.56), custom_call_target="tpu_custom_call" | custom-call | tf_op jit(solution)/shard_map/prepare/pallas_call | solution.py:92
  79.3 1.9 %collective-permute-start.4 = (bf16[16,8,64,128]{3,2,1,0:T(8,128)(2,1)S(1)}, bf16[16,8,64,128]{3,2,1,0:T(8,128)(2,1)}, u32[]{:S(2)}, u32[]{:S(2)}) collective-permute-start(bf16[16,8,64,128]{3,2,1,0:T(8,128)(2,1)S(1)} %all-to-all-done.1.own_ref), channel_id=1, source_target_pairs={{0,16},{16,0},{1,17},{17,1},{2,18},{18,2},{3,19},{19,3},{4,20},{20... | collective-permute-start | bytes 6291464 | tf_op jit(solution)/shard_map/ppermute | solution.py:514
  81.2 4.3 %collective-permute-done.4.other_ref = bf16[16,8,64,128]{3,2,1,0:T(8,128)(2,1)} collective-permute-done((bf16[16,8,64,128]{3,2,1,0:T(8,128)(2,1)S(1)}, bf16[16,8,64,128]{3,2,1,0:T(8,128)(2,1)}, u32[]{:S(2)}, u32[]{:S(2)}) %collective-permute-start.4) | collective-permute-done | bytes 2097184 | tf_op jit(solution)/shard_map/ppermute | solution.py:514
  85.5 4.0 %unpack.1 = (bf16[768,1536]{1,0:T(8,128)(2,1)}, bf16[1536,512]{1,0:T(8,128)(2,1)}) custom-call(s32[1]{0:T(128)} %bitcast.6.core_ref, bf16[16,8,64,128]{3,2,1,0:T(8,128)(2,1)} %copy-done.2, bf16[16,8,64,128]{3,2,1,0:T(8,128)(2,1)} %collective-permute-done.4.other_ref), custom_call_target="tpu_custom_call" | custom-call | tf_op jit(solution)/shard_map/unpack/pallas_call | solution.py:121
  89.5 2.9 %all-gather.2.cloned.1.call-done = bf16[3072,1152]{1,0:T(8,128)(2,1)} async-done(((bf16[96,1152]{1,0:T(8,128)(2,1)}), bf16[3072,1152]{1,0:T(8,128)(2,1)}) %all-gather.2.cloned.1.call-update) | async-done | bytes 7077904 | tf_op jit(solution)/shard_map/all_gather | solution.py:496
  92.4 15.3 %forward.1 = (bf16[6,384,384]{2,1,0:T(8,128)(2,1)}, f32[20,32,128]{2,1,0:T(8,128)}, bf16[32,24,640]{2,1,0:T(8,128)(2,1)}) custom-call(bf16[384,1536]{1,0:T(8,128)(2,1)} %get-tuple-element.27.normed_ref, bf16[2,1536,1152]{2,1,0:T(8,128)(2,1)} %bitcast.41, bf16[256,1536]{1,0:T(8,128)(2,1)} %bitcast.45, bf16[768,1536]{1,0:T(8,128)(2,1)} %get-tuple-element.32.out_hbm.out_ref, ...), custom_call_target="tpu_custom_call" | custom-call | tf_op jit(solution)/shard_map/forward/pallas_call | solution.py:272
  107.7 7.6 %all-to-all-start.2 = ((bf16[32,24,640]{2,1,0:T(8,128)(2,1)}), bf16[32,24,640]{2,1,0:T(8,128)(2,1)S(1)}, u32[]{:S(2)}, u32[]{:S(2)}) async-start(bf16[32,24,640]{2,1,0:T(8,128)(2,1)} %get-tuple-element.42), calls=%async_computation.2 | async-start | bytes 1966080 | tf_op jit(solution)/shard_map/all_to_all | solution.py:540
  115.3 4.3 %hidden_grad.1 = (f32[256,1536]{1,0:T(8,128)}, bf16[256,768]{1,0:T(8,128)(2,1)}) custom-call(bf16[256,512]{1,0:T(8,128)(2,1)} %get-tuple-element.34.rows_hbm.rows_ref, bf16[1536,512]{1,0:T(8,128)(2,1)} %get-tuple-element.33.head_hbm.head_ref, bf16[768,1536]{1,0:T(8,128)(2,1)} %get-tuple-element.32.out_hbm.out_ref), custom_call_target="tpu_custom_call" | custom-call | tf_op jit(solution)/shard_map/hidden_grad/pallas_call | solution.py:144
  119.7 7.0 %attend_backward.1 = (bf16[256,768]{1,0:T(8,128)(2,1)}, f32[256,768]{1,0:T(8,128)}, f32[256,768]{1,0:T(8,128)}, bf16[2,64,768]{2,1,0:T(8,128)(2,1)}, bf16[2,64,768]{2,1,0:T(8,128)(2,1)}) custom-call(bf16[6,384,384]{2,1,0:T(8,128)(2,1)} %get-tuple-element.37.q_ref.k_ref.v_ref, bf16[6,384,384]{2,1,0:T(8,128)(2,1)} %get-tuple-element.37.q_ref.k_ref.v_ref, ...), custom_call_target="tpu_custom_call" | custom-call | tf_op jit(solution)/shard_map/attend_backward/pallas_call | solution.py:351
  126.6 3.3 %all-to-all-done.2.pieces_ref = bf16[32,24,640]{2,1,0:T(8,128)(2,1)S(1)} async-done(((bf16[32,24,640]{2,1,0:T(8,128)(2,1)}), bf16[32,24,640]{2,1,0:T(8,128)(2,1)S(1)}, u32[]{:S(2)}, u32[]{:S(2)}) %all-to-all-start.2) | async-done | bytes 983072 | tf_op jit(solution)/shard_map/all_to_all | solution.py:540
  131.0 2.1 %sum_pieces.1 = bf16[16,24,128]{2,1,0:T(8,128)(2,1)} custom-call(bf16[32,24,640]{2,1,0:T(8,128)(2,1)} %copy-done.3), custom_call_target="tpu_custom_call" | custom-call | tf_op jit(solution)/shard_map/sum_pieces/pallas_call | solution.py:444
  133.1 7.9 %all-to-all-start.3 = ((bf16[16,24,128]{2,1,0:T(8,128)(2,1)}), bf16[16,24,128]{2,1,0:T(8,128)(2,1)S(1)}, u32[]{:S(2)}, u32[]{:S(2)}) async-start(bf16[16,24,128]{2,1,0:T(8,128)(2,1)} %sum_pieces.1), calls=%async_computation.3 | async-start | bytes 196608 | tf_op jit(solution)/shard_map/all_to_all | solution.py:519
  141.0 3.5 %collective-permute-start.5 = (bf16[2,64,768]{2,1,0:T(8,128)(2,1)}, bf16[2,64,768]{2,1,0:T(8,128)(2,1)S(1)}, u32[]{:S(2)}, u32[]{:S(2)}) collective-permute-start(bf16[2,64,768]{2,1,0:T(8,128)(2,1)} %get-tuple-element.48), channel_id=1, source_target_pairs={{0,1},{1,2},{2,3},{3,4},{4,5},{5,6},{6,7},{7,8},{8,9},{9,10},{10,1... | collective-permute-start | bytes 589832 | tf_op jit(solution)/shard_map/ppermute | solution.py:469
  144.5 2.9 %collective-permute-start.6 = (bf16[2,64,768]{2,1,0:T(8,128)(2,1)}, bf16[2,64,768]{2,1,0:T(8,128)(2,1)S(1)}, u32[]{:S(2)}, u32[]{:S(2)}) collective-permute-start(bf16[2,64,768]{2,1,0:T(8,128)(2,1)} %get-tuple-element.49), channel_id=1, source_target_pairs={{0,15},{1,0},{2,1},{3,2},{4,3},{5,4},{6,5},{7,6},{8,7},{9,8},{10,9... | collective-permute-start | bytes 589832 | tf_op jit(solution)/shard_map/ppermute | solution.py:469
  147.5 7.5 %all-to-all-done.3 = bf16[16,24,128]{2,1,0:T(8,128)(2,1)S(1)} async-done(((bf16[16,24,128]{2,1,0:T(8,128)(2,1)}), bf16[16,24,128]{2,1,0:T(8,128)(2,1)S(1)}, u32[]{:S(2)}, u32[]{:S(2)}) %all-to-all-start.3) | async-done | bytes 98336 | tf_op jit(solution)/shard_map/all_to_all | solution.py:519
  155.6 5.2 %all-to-all-start.4 = ((f32[16,24,128]{2,1,0:T(8,128)}), f32[16,24,128]{2,1,0:T(8,128)S(1)}, u32[]{:S(2)}, u32[]{:S(2)}) async-start(f32[16,24,128]{2,1,0:T(8,128)} %broadcast_in_dim.89), calls=%async_computation.4 | async-start | bytes 393216 | tf_op jit(solution)/shard_map/all_to_all | solution.py:502
  161.6 8.8 %norm_grad.1 = bf16[256,1536]{1,0:T(8,128)(2,1)} custom-call(bf16[256,768]{1,0:T(8,128)(2,1)} %get-tuple-element.39.dq_ref, f32[256,768]{1,0:T(8,128)} %get-tuple-element.40.dk_ref, f32[256,768]{1,0:T(8,128)} %get-tuple-element.41.dv_ref, bf16[2,64,768]{2,1,0:T(8,128)(2,1)} %copy-done.5, bf16[2,64,768]{2,1,0:T(8,128)(2,1)} %copy-done.6, ...), custom_call_target="tpu_custom_call" | custom-call | tf_op jit(solution)/shard_map/norm_grad/pallas_call | solution.py:404
  (53 shorter events, 16.0 us)
Async XLA Ops:
  7.2 1.0 copy-start
  7.2 85.2 %all-gather.2.cloned.1.call-start = ((), (), s32[]{:S(2)}) async-start(), calls=%async_computation.5 | async-start | bytes 7299072 | tf_op jit(solution)/shard_map/all_gather | solution.py:496
  37.7 7.6 %copy-start.4 = (f32[1,20,8,32]{3,2,1,0:T(8,128)S(1)}, f32[1,20,8,32]{3,2,1,0:T(8,128)}, u32[]{:S(2)}) copy-start(f32[1,20,8,32]{3,2,1,0:T(8,128)} %param.12) | copy-start | bytes 61444
  37.7 13.6 %copy-start.1 = (bf16[1,8,32,1536]{3,2,1,0:T(8,128)(2,1)S(1)}, bf16[1,8,32,1536]{3,2,1,0:T(8,128)(2,1)}, u32[]{:S(2)}) copy-start(bf16[1,8,32,1536]{3,2,1,0:T(8,128)(2,1)} %param.7) | copy-start | bytes 2359300
  37.7 20.9 %copy-start.9 = (f32[1536]{0:T(1024)S(1)}, f32[1536]{0:T(1024)}, u32[]{:S(2)}) copy-start(f32[1536]{0:T(1024)} %param.8) | copy-start | bytes 18436
  37.7 41.6 %all-to-all-start.1 = ((bf16[16,8,64,128]{3,2,1,0:T(8,128)(2,1)}), bf16[16,8,64,128]{3,2,1,0:T(8,128)(2,1)S(1)}, u32[]{:S(2)}, u32[]{:S(2)}) async-start(bf16[16,8,64,128]{3,2,1,0:T(8,128)(2,1)} %broadcast_in_dim.81), calls=%async_computation.1 | async-start | bytes 4194304 | tf_op jit(solution)/shard_map/all_to_all | solution.py:502
  45.4 25.0 %collective-permute-start.2 = (f32[20,8,1]{2,1,0:T(8,128)S(1)}, f32[20,8,1]{2,1,0:T(8,128)S(1)}, u32[]{:S(2)}, u32[]{:S(2)}) collective-permute-start(f32[20,8,1]{2,1,0:T(8,128)S(1)} %get-tuple-element.53), channel_id=1, source_target_pairs={{0,1},{1,2},{2,3},{3,4},{4,5},{5,6},{6,7},{7,8},{8,9},{9,10},{10,1... | collective-permute-start | bytes 1928 | tf_op jit(solution)/shard_map/ppermute | solution.py:469
  48.7 23.1 %collective-permute-start.3 = (f32[20,8,1]{2,1,0:T(8,128)S(1)}, f32[20,8,1]{2,1,0:T(8,128)S(1)}, u32[]{:S(2)}, u32[]{:S(2)}) collective-permute-start(f32[20,8,1]{2,1,0:T(8,128)S(1)} %get-tuple-element.54), channel_id=1, source_target_pairs={{0,15},{1,0},{2,1},{3,2},{4,3},{5,4},{6,5},{7,6},{8,7},{9,8},{10,9... | collective-permute-start | bytes 1928 | tf_op jit(solution)/shard_map/ppermute | solution.py:469
  51.3 23.9 %collective-permute-start.1 = (bf16[64,1536]{1,0:T(8,128)(2,1)S(1)}, bf16[64,1536]{1,0:T(8,128)(2,1)S(1)}, u32[]{:S(2)}, u32[]{:S(2)}) collective-permute-start(bf16[64,1536]{1,0:T(8,128)(2,1)S(1)} %get-tuple-element.51), channel_id=1, source_target_pairs={{0,15},{1,0},{2,1},{3,2},{4,3},{5,4},{6,5},{7,6},{8,7},{9,8},{10,9... | collective-permute-start | bytes 589832 | tf_op jit(solution)/shard_map/ppermute | solution.py:469
  56.6 18.6 %collective-permute-start = (bf16[64,1536]{1,0:T(8,128)(2,1)S(1)}, bf16[64,1536]{1,0:T(8,128)(2,1)S(1)}, u32[]{:S(2)}, u32[]{:S(2)}) collective-permute-start(bf16[64,1536]{1,0:T(8,128)(2,1)S(1)} %get-tuple-element.52), channel_id=1, source_target_pairs={{0,1},{1,2},{2,3},{3,4},{4,5},{5,6},{6,7},{7,8},{8,9},{9,10},{10,1... | collective-permute-start | bytes 589832 | tf_op jit(solution)/shard_map/ppermute | solution.py:469
  75.2 0.7 copy-start.7
  75.2 0.7 copy-start.8
  79.3 6.3 %copy-start.2 = (bf16[16,8,64,128]{3,2,1,0:T(8,128)(2,1)}, bf16[16,8,64,128]{3,2,1,0:T(8,128)(2,1)S(1)}, u32[]{:S(2)}) copy-start(bf16[16,8,64,128]{3,2,1,0:T(8,128)(2,1)S(1)} %all-to-all-done.1.own_ref) | copy-start | bytes 6291460
  79.3 6.3 %collective-permute-start.4 = (bf16[16,8,64,128]{3,2,1,0:T(8,128)(2,1)S(1)}, bf16[16,8,64,128]{3,2,1,0:T(8,128)(2,1)}, u32[]{:S(2)}, u32[]{:S(2)}) collective-permute-start(bf16[16,8,64,128]{3,2,1,0:T(8,128)(2,1)S(1)} %all-to-all-done.1.own_ref), channel_id=1, source_target_pairs={{0,16},{16,0},{1,17},{17,1},{2,18},{18,2},{3,19},{19,3},{4,20},{20... | collective-permute-start | bytes 6291464 | tf_op jit(solution)/shard_map/ppermute | solution.py:514
  107.7 22.2 %all-to-all-start.2 = ((bf16[32,24,640]{2,1,0:T(8,128)(2,1)}), bf16[32,24,640]{2,1,0:T(8,128)(2,1)S(1)}, u32[]{:S(2)}, u32[]{:S(2)}) async-start(bf16[32,24,640]{2,1,0:T(8,128)(2,1)} %get-tuple-element.42), calls=%async_computation.2 | async-start | bytes 1966080 | tf_op jit(solution)/shard_map/all_to_all | solution.py:540
  130.0 1.0 copy-start.3
  133.1 21.9 %all-to-all-start.3 = ((bf16[16,24,128]{2,1,0:T(8,128)(2,1)}), bf16[16,24,128]{2,1,0:T(8,128)(2,1)S(1)}, u32[]{:S(2)}, u32[]{:S(2)}) async-start(bf16[16,24,128]{2,1,0:T(8,128)(2,1)} %sum_pieces.1), calls=%async_computation.3 | async-start | bytes 196608 | tf_op jit(solution)/shard_map/all_to_all | solution.py:519
  141.0 19.9 %collective-permute-start.5 = (bf16[2,64,768]{2,1,0:T(8,128)(2,1)}, bf16[2,64,768]{2,1,0:T(8,128)(2,1)S(1)}, u32[]{:S(2)}, u32[]{:S(2)}) collective-permute-start(bf16[2,64,768]{2,1,0:T(8,128)(2,1)} %get-tuple-element.48), channel_id=1, source_target_pairs={{0,1},{1,2},{2,3},{3,4},{4,5},{5,6},{6,7},{7,8},{8,9},{9,10},{10,1... | collective-permute-start | bytes 589832 | tf_op jit(solution)/shard_map/ppermute | solution.py:469
  144.5 16.4 %collective-permute-start.6 = (bf16[2,64,768]{2,1,0:T(8,128)(2,1)}, bf16[2,64,768]{2,1,0:T(8,128)(2,1)S(1)}, u32[]{:S(2)}, u32[]{:S(2)}) collective-permute-start(bf16[2,64,768]{2,1,0:T(8,128)(2,1)} %get-tuple-element.49), channel_id=1, source_target_pairs={{0,15},{1,0},{2,1},{3,2},{4,3},{5,4},{6,5},{7,6},{8,7},{9,8},{10,9... | collective-permute-start | bytes 589832 | tf_op jit(solution)/shard_map/ppermute | solution.py:469
  155.6 14.8 %all-to-all-start.4 = ((f32[16,24,128]{2,1,0:T(8,128)}), f32[16,24,128]{2,1,0:T(8,128)S(1)}, u32[]{:S(2)}, u32[]{:S(2)}) async-start(f32[16,24,128]{2,1,0:T(8,128)} %broadcast_in_dim.89), calls=%async_computation.4 | async-start | bytes 393216 | tf_op jit(solution)/shard_map/all_to_all | solution.py:502
  160.9 0.7 copy-start.5
  160.9 0.7 copy-start.6
Sparse Core Ops, SparseCore 0:
  10.7 81.6 all-gather.1

commit v8 on v7

--- a/solution.py
+++ b/solution.py
@@ -188,16 +188,21 @@
     return jnp.concatenate([part.astype(BF16) for part in parts], axis=1)
 
 
+def column_block(step):
+    return step % 3 * 2 + step // 3
+
+
 def forward_kernel(
     normed_ref, weight_ref,
     tokens_hbm, out_hbm, head_hbm, rows_hbm, residual_hbm,
     projected_out, fine_ref, pieces_hbm,
-    projected_ref, pieces_ref, tokens_ref, out_ref, head_ref, rows_ref, residual_ref, products, sems,
+    projected_ref, attended_ref, pieces_ref, tokens_ref, out_ref, head_ref, rows_ref, residual_ref, products, sems,
 ):
     step = pl.program_id(0)
+    place = column_block(step)
     copies = [
-        pltpu.make_async_copy(source, target, sems.at[place])
-        for place, (source, target) in enumerate(
+        pltpu.make_async_copy(source, target, sems.at[number])
+        for number, (source, target) in enumerate(
             (
                 (tokens_hbm, tokens_ref),
                 (out_hbm, out_ref),
@@ -208,33 +213,34 @@
         )
     ]
 
-    @pl.when(step == 3)
+    @pl.when(step == 4)
     def _():
         for copy in copies:
             copy.start()
 
-    @pl.when(step < 2)
+    @pl.when(place < 2)
     def _():
         queries = dot(normed_ref[:ROWS], weight_ref[0]).astype(BF16)
-        projected_ref[step, :ROWS] = queries
+        projected_ref[place, :ROWS] = queries
         projected_out[0, :ROWS] = queries
         projected_out[0, ROWS:] = jnp.zeros((2 * EDGE, GROUP), BF16)
 
-    @pl.when(step >= 2)
+    @pl.when(place >= 2)
     def _():
         pairs = dot(normed_ref[...], weight_ref[0]).astype(BF16)
-        projected_ref[step] = pairs
+        projected_ref[place] = pairs
         projected_out[0] = pairs
 
+    @pl.when(step == 3)
+    def _():
+        attended_ref[...] = forward_group(projected_ref[0, :ROWS], projected_ref[2], projected_ref[4])
+
     @pl.when(step == 5)
     def _():
-        attended = [
-            forward_group(projected_ref[group, :ROWS], projected_ref[2 + group], projected_ref[4 + group])
-            for group in range(2)
-        ]
+        attended = forward_group(projected_ref[1, :ROWS], projected_ref[3], projected_ref[5])
         for copy in copies:
             copy.wait()
-        mixed = dot(attended[0], out_ref[:GROUP]) + dot(attended[1], out_ref[GROUP:])
+        mixed = dot(attended_ref[...], out_ref[:GROUP]) + dot(attended, out_ref[GROUP:])
         hidden = (tokens_ref[...].astype(F32) + mixed).astype(BF16)
         products[...] = dot_first(hidden, rows_ref[...])
         for core in range(CORES):
@@ -279,16 +285,17 @@
         grid=(6,),
         in_specs=[
             whole_block((KEYS, D)),
-            pl.BlockSpec((1, D, GROUP), lambda n: (n // 3, 0, n % 3)),
+            pl.BlockSpec((1, D, GROUP), lambda n: (column_block(n) // 3, 0, column_block(n) % 3)),
         ]
         + [pl.BlockSpec(memory_space=pl.ANY)] * 5,
         out_specs=(
-            pl.BlockSpec((1, KEYS, GROUP), lambda n: (n, 0, 0)),
+            pl.BlockSpec((1, KEYS, GROUP), lambda n: (column_block(n), 0, 0)),
             whole_block(fine),
             pl.BlockSpec(memory_space=pl.ANY),
         ),
         scratch_shapes=[
             pltpu.VMEM(projected, BF16),
+            pltpu.VMEM((ROWS, GROUP), BF16),
             pltpu.VMEM(pieces, BF16),
             pltpu.VMEM((ROWS, D), BF16),
             pltpu.VMEM((INNER, D), BF16),

time: 179 us -> 178 us (level)
  no operation moved by 1% of the time
where the time goes in v8:
time: 178 us; the launch traced here: 177 us
  starting transfers between devices  49.9 us (28%)
  Pallas kernels  43.5 us (24%)
  waiting for transfers between devices  32.4 us (18%)
  blocking collectives  24.4 us (14%)
  between operations  14.3 us (8%)
  local copies, waits for them, and re-layouts  8.74 us (5%)
  matrix products  3.88 us (2%)
    all_to_all x1, blocking collectives, to_all(): return lax.all_to_all(copies, axes, 0, 0, tiled=True)  24.4 us
    ppermute x6, starting transfers between devices, shifted(): lax.ppermute(value, TILE, [(i, (i + steps) % TILES) for i in range(TILES)])  19.6 us
    ppermute x6, waiting for transfers between devices, shifted(): lax.ppermute(value, TILE, [(i, (i + steps) % TILES) for i in range(TILES)])  14.3 us
    pallas_call x1, Pallas kernels, forward(): pl.pallas_call(forward_kernel, out_shape=(jax.ShapeDtypeStruct(projected,...  14 us
    all_to_all x2, starting transfers between devices, to_all(): return lax.all_to_all(copies, axes, 0, 0, tiled=True)  12.8 us
    pallas_call x1, Pallas kernels, norm_grad(): pl.pallas_call(norm_grad_kernel, out_shape=jax.ShapeDtypeStruct((ROWS, D)...  8.8 us
    all_to_all x1, starting transfers between devices, over_samples(): both = lax.all_to_all(summed, ('dp', 'z'), 0, 0, tiled=True)  7.9 us
    all_to_all x1, starting transfers between devices, shards(): pieces = lax.all_to_all(pieces, ('c',) + TILE, 0, 0, tiled=True)  7.58 us
  transfers between devices with their start and end apart: 12, of which 7 were waited for; matrix products, arithmetic and copies ran while one was open for 4% of the time, Pallas kernels for 15%

profile of v8, /device:TPU:2, one launch (start us, length us, event | category | flops | bytes accessed | tf_op | source)
XLA Modules:
  0.0 177.2 jit_solution(9718898289454131425)
XLA Ops:
  11.4 24.4 %all_to_all.25 = bf16[8,64,128]{2,1,0:T(8,128)(2,1)S(1)} all-to-all(bf16[8,64,128]{2,1,0:T(8,128)(2,1)S(1)} %broadcast_in_dim.80), channel_id=1, replica_groups=mesh['dp'=2,'z'=8,'c'=2,'y'=4,'x'=4] {'z'}, dimensions={0} | all-to-all | bytes 262144 | tf_op jit(solution)/shard_map/all_to_all | solution.py:509
  35.7 1.9 %broadcast_in_dim.81 = bf16[16,8,64,128]{3,2,1,0:T(8,128)(2,1)} broadcast(bf16[8,64,128]{2,1,0:T(8,128)(2,1)S(1)} %all_to_all.25), dimensions={1,2,3} | broadcast | bytes 2228224 | tf_op jit(solution)/shard_map/broadcast_in_dim | solution.py:508
  37.7 7.6 %all-to-all-start.1 = ((bf16[16,8,64,128]{3,2,1,0:T(8,128)(2,1)}), bf16[16,8,64,128]{3,2,1,0:T(8,128)(2,1)S(1)}, u32[]{:S(2)}, u32[]{:S(2)}) async-start(bf16[16,8,64,128]{3,2,1,0:T(8,128)(2,1)} %broadcast_in_dim.81), calls=%async_computation.1 | async-start | bytes 4194304 | tf_op jit(solution)/shard_map/all_to_all | solution.py:509
  45.4 3.4 %collective-permute-start.2 = (f32[20,8,1]{2,1,0:T(8,128)S(1)}, f32[20,8,1]{2,1,0:T(8,128)S(1)}, u32[]{:S(2)}, u32[]{:S(2)}) collective-permute-start(f32[20,8,1]{2,1,0:T(8,128)S(1)} %get-tuple-element.53), channel_id=1, source_target_pairs={{0,1},{1,2},{2,3},{3,4},{4,5},{5,6},{6,7},{7,8},{8,9},{9,10},{10,1... | collective-permute-start | bytes 1928 | tf_op jit(solution)/shard_map/ppermute | solution.py:476
  48.7 2.5 %collective-permute-start.3 = (f32[20,8,1]{2,1,0:T(8,128)S(1)}, f32[20,8,1]{2,1,0:T(8,128)S(1)}, u32[]{:S(2)}, u32[]{:S(2)}) collective-permute-start(f32[20,8,1]{2,1,0:T(8,128)S(1)} %get-tuple-element.54), channel_id=1, source_target_pairs={{0,15},{1,0},{2,1},{3,2},{4,3},{5,4},{6,5},{7,6},{8,7},{9,8},{10,9... | collective-permute-start | bytes 1928 | tf_op jit(solution)/shard_map/ppermute | solution.py:476
  51.3 5.3 %collective-permute-start.1 = (bf16[64,1536]{1,0:T(8,128)(2,1)S(1)}, bf16[64,1536]{1,0:T(8,128)(2,1)S(1)}, u32[]{:S(2)}, u32[]{:S(2)}) collective-permute-start(bf16[64,1536]{1,0:T(8,128)(2,1)S(1)} %get-tuple-element.51), channel_id=1, source_target_pairs={{0,15},{1,0},{2,1},{3,2},{4,3},{5,4},{6,5},{7,6},{8,7},{9,8},{10,9... | collective-permute-start | bytes 589832 | tf_op jit(solution)/shard_map/ppermute | solution.py:476
  59.2 11.1 %collective-permute-done.2 = f32[20,8,1]{2,1,0:T(8,128)S(1)} collective-permute-done((f32[20,8,1]{2,1,0:T(8,128)S(1)}, f32[20,8,1]{2,1,0:T(8,128)S(1)}, u32[]{:S(2)}, u32[]{:S(2)}) %collective-permute-start.2) | collective-permute-done | bytes 672 | tf_op jit(solution)/shard_map/ppermute | solution.py:476
  75.9 3.3 %prepare.1 = (bf16[384,1536]{1,0:T(8,128)(2,1)}, bf16[256,512]{1,0:T(8,128)(2,1)}) custom-call(bf16[256,1536]{1,0:T(8,128)(2,1)} %bitcast.44, bf16[64,1536]{1,0:T(8,128)(2,1)} %copy-done.8, bf16[64,1536]{1,0:T(8,128)(2,1)} %copy-done.7, f32[1,1536]{1,0:T(1,128)} %reshape.150.gain_ref, f32[20,32,128]{2,1,0:T(8,128)} %bitcast.56), custom_call_target="tpu_custom_call" | custom-call | tf_op jit(solution)/shard_map/prepare/pallas_call | solution.py:92
  79.3 1.9 %collective-permute-start.4 = (bf16[16,8,64,128]{3,2,1,0:T(8,128)(2,1)S(1)}, bf16[16,8,64,128]{3,2,1,0:T(8,128)(2,1)}, u32[]{:S(2)}, u32[]{:S(2)}) collective-permute-start(bf16[16,8,64,128]{3,2,1,0:T(8,128)(2,1)S(1)} %all-to-all-done.1.own_ref), channel_id=1, source_target_pairs={{0,16},{16,0},{1,17},{17,1},{2,18},{18,2},{3,19},{19,3},{4,20},{20... | collective-permute-start | bytes 6291464 | tf_op jit(solution)/shard_map/ppermute | solution.py:521
  81.2 4.3 %collective-permute-done.4.other_ref = bf16[16,8,64,128]{3,2,1,0:T(8,128)(2,1)} collective-permute-done((bf16[16,8,64,128]{3,2,1,0:T(8,128)(2,1)S(1)}, bf16[16,8,64,128]{3,2,1,0:T(8,128)(2,1)}, u32[]{:S(2)}, u32[]{:S(2)}) %collective-permute-start.4) | collective-permute-done | bytes 2097184 | tf_op jit(solution)/shard_map/ppermute | solution.py:521
  85.5 4.0 %unpack.1 = (bf16[768,1536]{1,0:T(8,128)(2,1)}, bf16[1536,512]{1,0:T(8,128)(2,1)}) custom-call(s32[1]{0:T(128)} %bitcast.6.core_ref, bf16[16,8,64,128]{3,2,1,0:T(8,128)(2,1)} %copy-done.2, bf16[16,8,64,128]{3,2,1,0:T(8,128)(2,1)} %collective-permute-done.4.other_ref), custom_call_target="tpu_custom_call" | custom-call | tf_op jit(solution)/shard_map/unpack/pallas_call | solution.py:121
  89.5 2.9 %all-gather.2.cloned.1.call-done = bf16[3072,1152]{1,0:T(8,128)(2,1)} async-done(((bf16[96,1152]{1,0:T(8,128)(2,1)}), bf16[3072,1152]{1,0:T(8,128)(2,1)}) %all-gather.2.cloned.1.call-update) | async-done | bytes 7077904 | tf_op jit(solution)/shard_map/all_gather | solution.py:503
  92.4 14.0 %forward.1 = (bf16[6,384,384]{2,1,0:T(8,128)(2,1)}, f32[20,32,128]{2,1,0:T(8,128)}, bf16[32,24,640]{2,1,0:T(8,128)(2,1)}) custom-call(bf16[384,1536]{1,0:T(8,128)(2,1)} %get-tuple-element.27.normed_ref, bf16[2,1536,1152]{2,1,0:T(8,128)(2,1)} %bitcast.41, bf16[256,1536]{1,0:T(8,128)(2,1)} %bitcast.45, bf16[768,1536]{1,0:T(8,128)(2,1)} %get-tuple-element.32.out_hbm.out_ref, ...), custom_call_target="tpu_custom_call" | custom-call | tf_op jit(solution)/shard_map/forward/pallas_call | solution.py:278
  106.5 7.6 %all-to-all-start.2 = ((bf16[32,24,640]{2,1,0:T(8,128)(2,1)}), bf16[32,24,640]{2,1,0:T(8,128)(2,1)S(1)}, u32[]{:S(2)}, u32[]{:S(2)}) async-start(bf16[32,24,640]{2,1,0:T(8,128)(2,1)} %get-tuple-element.42), calls=%async_computation.2 | async-start | bytes 1966080 | tf_op jit(solution)/shard_map/all_to_all | solution.py:547
  114.1 4.3 %hidden_grad.1 = (f32[256,1536]{1,0:T(8,128)}, bf16[256,768]{1,0:T(8,128)(2,1)}) custom-call(bf16[256,512]{1,0:T(8,128)(2,1)} %get-tuple-element.34.rows_hbm.rows_ref, bf16[1536,512]{1,0:T(8,128)(2,1)} %get-tuple-element.33.head_hbm.head_ref, bf16[768,1536]{1,0:T(8,128)(2,1)} %get-tuple-element.32.out_hbm.out_ref), custom_call_target="tpu_custom_call" | custom-call | tf_op jit(solution)/shard_map/hidden_grad/pallas_call | solution.py:144
  118.4 7.0 %attend_backward.1 = (bf16[256,768]{1,0:T(8,128)(2,1)}, f32[256,768]{1,0:T(8,128)}, f32[256,768]{1,0:T(8,128)}, bf16[2,64,768]{2,1,0:T(8,128)(2,1)}, bf16[2,64,768]{2,1,0:T(8,128)(2,1)}) custom-call(bf16[6,384,384]{2,1,0:T(8,128)(2,1)} %get-tuple-element.37.q_ref.k_ref.v_ref, bf16[6,384,384]{2,1,0:T(8,128)(2,1)} %get-tuple-element.37.q_ref.k_ref.v_ref, ...), custom_call_target="tpu_custom_call" | custom-call | tf_op jit(solution)/shard_map/attend_backward/pallas_call | solution.py:358
  125.4 3.3 %all-to-all-done.2.pieces_ref = bf16[32,24,640]{2,1,0:T(8,128)(2,1)S(1)} async-done(((bf16[32,24,640]{2,1,0:T(8,128)(2,1)}), bf16[32,24,640]{2,1,0:T(8,128)(2,1)S(1)}, u32[]{:S(2)}, u32[]{:S(2)}) %all-to-all-start.2) | async-done | bytes 983072 | tf_op jit(solution)/shard_map/all_to_all | solution.py:547
  129.7 2.1 %sum_pieces.1 = bf16[16,24,128]{2,1,0:T(8,128)(2,1)} custom-call(bf16[32,24,640]{2,1,0:T(8,128)(2,1)} %copy-done.3), custom_call_target="tpu_custom_call" | custom-call | tf_op jit(solution)/shard_map/sum_pieces/pallas_call | solution.py:451
  131.8 7.9 %all-to-all-start.3 = ((bf16[16,24,128]{2,1,0:T(8,128)(2,1)}), bf16[16,24,128]{2,1,0:T(8,128)(2,1)S(1)}, u32[]{:S(2)}, u32[]{:S(2)}) async-start(bf16[16,24,128]{2,1,0:T(8,128)(2,1)} %sum_pieces.1), calls=%async_computation.3 | async-start | bytes 196608 | tf_op jit(solution)/shard_map/all_to_all | solution.py:526
  139.7 3.5 %collective-permute-start.5 = (bf16[2,64,768]{2,1,0:T(8,128)(2,1)}, bf16[2,64,768]{2,1,0:T(8,128)(2,1)S(1)}, u32[]{:S(2)}, u32[]{:S(2)}) collective-permute-start(bf16[2,64,768]{2,1,0:T(8,128)(2,1)} %get-tuple-element.48), channel_id=1, source_target_pairs={{0,1},{1,2},{2,3},{3,4},{4,5},{5,6},{6,7},{7,8},{8,9},{9,10},{10,1... | collective-permute-start | bytes 589832 | tf_op jit(solution)/shard_map/ppermute | solution.py:476
  143.2 2.9 %collective-permute-start.6 = (bf16[2,64,768]{2,1,0:T(8,128)(2,1)}, bf16[2,64,768]{2,1,0:T(8,128)(2,1)S(1)}, u32[]{:S(2)}, u32[]{:S(2)}) collective-permute-start(bf16[2,64,768]{2,1,0:T(8,128)(2,1)} %get-tuple-element.49), channel_id=1, source_target_pairs={{0,15},{1,0},{2,1},{3,2},{4,3},{5,4},{6,5},{7,6},{8,7},{9,8},{10,9... | collective-permute-start | bytes 589832 | tf_op jit(solution)/shard_map/ppermute | solution.py:476
  146.2 7.5 %all-to-all-done.3 = bf16[16,24,128]{2,1,0:T(8,128)(2,1)S(1)} async-done(((bf16[16,24,128]{2,1,0:T(8,128)(2,1)}), bf16[16,24,128]{2,1,0:T(8,128)(2,1)S(1)}, u32[]{:S(2)}, u32[]{:S(2)}) %all-to-all-start.3) | async-done | bytes 98336 | tf_op jit(solution)/shard_map/all_to_all | solution.py:526
  154.4 5.2 %all-to-all-start.4 = ((f32[16,24,128]{2,1,0:T(8,128)}), f32[16,24,128]{2,1,0:T(8,128)S(1)}, u32[]{:S(2)}, u32[]{:S(2)}) async-start(f32[16,24,128]{2,1,0:T(8,128)} %broadcast_in_dim.89), calls=%async_computation.4 | async-start | bytes 393216 | tf_op jit(solution)/shard_map/all_to_all | solution.py:509
  160.4 8.8 %norm_grad.1 = bf16[256,1536]{1,0:T(8,128)(2,1)} custom-call(bf16[256,768]{1,0:T(8,128)(2,1)} %get-tuple-element.39.dq_ref, f32[256,768]{1,0:T(8,128)} %get-tuple-element.40.dk_ref, f32[256,768]{1,0:T(8,128)} %get-tuple-element.41.dv_ref, bf16[2,64,768]{2,1,0:T(8,128)(2,1)} %copy-done.5, bf16[2,64,768]{2,1,0:T(8,128)(2,1)} %copy-done.6, ...), custom_call_target="tpu_custom_call" | custom-call | tf_op jit(solution)/shard_map/norm_grad/pallas_call | solution.py:411
  (53 shorter events, 16.0 us)
Async XLA Ops:
  7.2 1.0 copy-start
  7.2 85.2 %all-gather.2.cloned.1.call-start = ((), (), s32[]{:S(2)}) async-start(), calls=%async_computation.5 | async-start | bytes 7299072 | tf_op jit(solution)/shard_map/all_gather | solution.py:503
  37.7 7.6 %copy-start.4 = (f32[1,20,8,32]{3,2,1,0:T(8,128)S(1)}, f32[1,20,8,32]{3,2,1,0:T(8,128)}, u32[]{:S(2)}) copy-start(f32[1,20,8,32]{3,2,1,0:T(8,128)} %param.12) | copy-start | bytes 61444
  37.7 13.6 %copy-start.1 = (bf16[1,8,32,1536]{3,2,1,0:T(8,128)(2,1)S(1)}, bf16[1,8,32,1536]{3,2,1,0:T(8,128)(2,1)}, u32[]{:S(2)}) copy-start(bf16[1,8,32,1536]{3,2,1,0:T(8,128)(2,1)} %param.7) | copy-start | bytes 2359300
  37.7 20.9 %copy-start.9 = (f32[1536]{0:T(1024)S(1)}, f32[1536]{0:T(1024)}, u32[]{:S(2)}) copy-start(f32[1536]{0:T(1024)} %param.8) | copy-start | bytes 18436
  37.7 41.6 %all-to-all-start.1 = ((bf16[16,8,64,128]{3,2,1,0:T(8,128)(2,1)}), bf16[16,8,64,128]{3,2,1,0:T(8,128)(2,1)S(1)}, u32[]{:S(2)}, u32[]{:S(2)}) async-start(bf16[16,8,64,128]{3,2,1,0:T(8,128)(2,1)} %broadcast_in_dim.81), calls=%async_computation.1 | async-start | bytes 4194304 | tf_op jit(solution)/shard_map/all_to_all | solution.py:509
  45.4 25.0 %collective-permute-start.2 = (f32[20,8,1]{2,1,0:T(8,128)S(1)}, f32[20,8,1]{2,1,0:T(8,128)S(1)}, u32[]{:S(2)}, u32[]{:S(2)}) collective-permute-start(f32[20,8,1]{2,1,0:T(8,128)S(1)} %get-tuple-element.53), channel_id=1, source_target_pairs={{0,1},{1,2},{2,3},{3,4},{4,5},{5,6},{6,7},{7,8},{8,9},{9,10},{10,1... | collective-permute-start | bytes 1928 | tf_op jit(solution)/shard_map/ppermute | solution.py:476
  48.7 23.1 %collective-permute-start.3 = (f32[20,8,1]{2,1,0:T(8,128)S(1)}, f32[20,8,1]{2,1,0:T(8,128)S(1)}, u32[]{:S(2)}, u32[]{:S(2)}) collective-permute-start(f32[20,8,1]{2,1,0:T(8,128)S(1)} %get-tuple-element.54), channel_id=1, source_target_pairs={{0,15},{1,0},{2,1},{3,2},{4,3},{5,4},{6,5},{7,6},{8,7},{9,8},{10,9... | collective-permute-start | bytes 1928 | tf_op jit(solution)/shard_map/ppermute | solution.py:476
  51.3 23.9 %collective-permute-start.1 = (bf16[64,1536]{1,0:T(8,128)(2,1)S(1)}, bf16[64,1536]{1,0:T(8,128)(2,1)S(1)}, u32[]{:S(2)}, u32[]{:S(2)}) collective-permute-start(bf16[64,1536]{1,0:T(8,128)(2,1)S(1)} %get-tuple-element.51), channel_id=1, source_target_pairs={{0,15},{1,0},{2,1},{3,2},{4,3},{5,4},{6,5},{7,6},{8,7},{9,8},{10,9... | collective-permute-start | bytes 589832 | tf_op jit(solution)/shard_map/ppermute | solution.py:476
  56.6 18.6 %collective-permute-start = (bf16[64,1536]{1,0:T(8,128)(2,1)S(1)}, bf16[64,1536]{1,0:T(8,128)(2,1)S(1)}, u32[]{:S(2)}, u32[]{:S(2)}) collective-permute-start(bf16[64,1536]{1,0:T(8,128)(2,1)S(1)} %get-tuple-element.52), channel_id=1, source_target_pairs={{0,1},{1,2},{2,3},{3,4},{4,5},{5,6},{6,7},{7,8},{8,9},{9,10},{10,1... | collective-permute-start | bytes 589832 | tf_op jit(solution)/shard_map/ppermute | solution.py:476
  75.2 0.7 copy-start.7
  75.2 0.7 copy-start.8
  79.3 6.3 %copy-start.2 = (bf16[16,8,64,128]{3,2,1,0:T(8,128)(2,1)}, bf16[16,8,64,128]{3,2,1,0:T(8,128)(2,1)S(1)}, u32[]{:S(2)}) copy-start(bf16[16,8,64,128]{3,2,1,0:T(8,128)(2,1)S(1)} %all-to-all-done.1.own_ref) | copy-start | bytes 6291460
  79.3 6.3 %collective-permute-start.4 = (bf16[16,8,64,128]{3,2,1,0:T(8,128)(2,1)S(1)}, bf16[16,8,64,128]{3,2,1,0:T(8,128)(2,1)}, u32[]{:S(2)}, u32[]{:S(2)}) collective-permute-start(bf16[16,8,64,128]{3,2,1,0:T(8,128)(2,1)S(1)} %all-to-all-done.1.own_ref), channel_id=1, source_target_pairs={{0,16},{16,0},{1,17},{17,1},{2,18},{18,2},{3,19},{19,3},{4,20},{20... | collective-permute-start | bytes 6291464 | tf_op jit(solution)/shard_map/ppermute | solution.py:521
  106.5 22.2 %all-to-all-start.2 = ((bf16[32,24,640]{2,1,0:T(8,128)(2,1)}), bf16[32,24,640]{2,1,0:T(8,128)(2,1)S(1)}, u32[]{:S(2)}, u32[]{:S(2)}) async-start(bf16[32,24,640]{2,1,0:T(8,128)(2,1)} %get-tuple-element.42), calls=%async_computation.2 | async-start | bytes 1966080 | tf_op jit(solution)/shard_map/all_to_all | solution.py:547
  128.7 1.0 copy-start.3
  131.8 21.9 %all-to-all-start.3 = ((bf16[16,24,128]{2,1,0:T(8,128)(2,1)}), bf16[16,24,128]{2,1,0:T(8,128)(2,1)S(1)}, u32[]{:S(2)}, u32[]{:S(2)}) async-start(bf16[16,24,128]{2,1,0:T(8,128)(2,1)} %sum_pieces.1), calls=%async_computation.3 | async-start | bytes 196608 | tf_op jit(solution)/shard_map/all_to_all | solution.py:526
  139.7 19.9 %collective-permute-start.5 = (bf16[2,64,768]{2,1,0:T(8,128)(2,1)}, bf16[2,64,768]{2,1,0:T(8,128)(2,1)S(1)}, u32[]{:S(2)}, u32[]{:S(2)}) collective-permute-start(bf16[2,64,768]{2,1,0:T(8,128)(2,1)} %get-tuple-element.48), channel_id=1, source_target_pairs={{0,1},{1,2},{2,3},{3,4},{4,5},{5,6},{6,7},{7,8},{8,9},{9,10},{10,1... | collective-permute-start | bytes 589832 | tf_op jit(solution)/shard_map/ppermute | solution.py:476
  143.2 16.4 %collective-permute-start.6 = (bf16[2,64,768]{2,1,0:T(8,128)(2,1)}, bf16[2,64,768]{2,1,0:T(8,128)(2,1)S(1)}, u32[]{:S(2)}, u32[]{:S(2)}) collective-permute-start(bf16[2,64,768]{2,1,0:T(8,128)(2,1)} %get-tuple-element.49), channel_id=1, source_target_pairs={{0,15},{1,0},{2,1},{3,2},{4,3},{5,4},{6,5},{7,6},{8,7},{9,8},{10,9... | collective-permute-start | bytes 589832 | tf_op jit(solution)/shard_map/ppermute | solution.py:476
  154.4 14.8 %all-to-all-start.4 = ((f32[16,24,128]{2,1,0:T(8,128)}), f32[16,24,128]{2,1,0:T(8,128)S(1)}, u32[]{:S(2)}, u32[]{:S(2)}) async-start(f32[16,24,128]{2,1,0:T(8,128)} %broadcast_in_dim.89), calls=%async_computation.4 | async-start | bytes 393216 | tf_op jit(solution)/shard_map/all_to_all | solution.py:509
  159.6 0.7 copy-start.5
  159.6 0.7 copy-start.6
Sparse Core Ops, SparseCore 0:
  10.7 81.6 all-gather.1

commit v9 on v8

--- a/solution.py
+++ b/solution.py
@@ -436,10 +436,8 @@
     )(dq, dk, dv, from_left, from_right, full, full, gain, tokens, grad_hidden)
 
 
-def sum_kernel(pieces_ref, out_ref):
-    total = pieces_ref[0].astype(F32)
-    for place in range(1, CORES * TILES):
-        total = total + pieces_ref[place].astype(F32)
+def spread_kernel(total_ref, out_ref):
+    total = total_ref[...]
     empty = jnp.zeros((24, LANES - CHANNELS), F32)
     for z in range(ZS):
         part = jnp.concatenate([total[:, z * CHANNELS : (z + 1) * CHANNELS], empty], axis=1).astype(BF16)
@@ -449,12 +447,12 @@
 
 def sum_pieces(pieces):
     return pl.pallas_call(
-        sum_kernel,
+        spread_kernel,
         out_shape=jax.ShapeDtypeStruct((2 * ZS, 24, LANES), BF16),
         in_specs=[WHOLE],
         out_specs=WHOLE,
         name="sum_pieces",
-    )(pieces)
+    )(jnp.sum(pieces.astype(F32), axis=0))
 
 
 def interp_weights(fine_index):

time: 178 us -> 177 us (level)
  transfers between devices with their start and end apart: 12 -> 12, of which waited for: 7 -> 7; matrix products, arithmetic and copies ran while one was open for 4% -> 4% of each run, Pallas kernels for 15% -> 16%
where the time goes in v9:
time: 177 us; the launch traced here: 176 us
  starting transfers between devices  49.8 us (28%)
  Pallas kernels  43 us (24%)
  waiting for transfers between devices  32.4 us (18%)
  blocking collectives  24.4 us (14%)
  between operations  14.3 us (8%)
  local copies, waits for them, and re-layouts  7.73 us (4%)
  matrix products  3.88 us (2%)
    all_to_all x1, blocking collectives, to_all(): return lax.all_to_all(copies, axes, 0, 0, tiled=True)  24.4 us
    ppermute x6, starting transfers between devices, shifted(): lax.ppermute(value, TILE, [(i, (i + steps) % TILES) for i in range(TILES)])  19.6 us
    ppermute x6, waiting for transfers between devices, shifted(): lax.ppermute(value, TILE, [(i, (i + steps) % TILES) for i in range(TILES)])  14.3 us
    pallas_call x1, Pallas kernels, forward(): pl.pallas_call(forward_kernel, out_shape=(jax.ShapeDtypeStruct(projected,...  14 us
    all_to_all x2, starting transfers between devices, to_all(): return lax.all_to_all(copies, axes, 0, 0, tiled=True)  12.8 us
    pallas_call x1, Pallas kernels, norm_grad(): pl.pallas_call(norm_grad_kernel, out_shape=jax.ShapeDtypeStruct((ROWS, D)...  8.8 us
    all_to_all x1, starting transfers between devices, over_samples(): both = lax.all_to_all(summed, ('dp', 'z'), 0, 0, tiled=True)  7.9 us
    all_to_all x1, starting transfers between devices, shards(): pieces = lax.all_to_all(pieces, ('c',) + TILE, 0, 0, tiled=True)  7.55 us
  transfers between devices with their start and end apart: 12, of which 7 were waited for; matrix products, arithmetic and copies ran while one was open for 4% of the time, Pallas kernels for 16%

profile of v9, /device:TPU:2, one launch (start us, length us, event | category | flops | bytes accessed | tf_op | source)
XLA Modules:
  0.0 176.5 jit_solution(8519410894719276019)
XLA Ops:
  11.4 24.4 %all_to_all.25 = bf16[8,64,128]{2,1,0:T(8,128)(2,1)S(1)} all-to-all(bf16[8,64,128]{2,1,0:T(8,128)(2,1)S(1)} %broadcast_in_dim.80), channel_id=1, replica_groups=mesh['dp'=2,'z'=8,'c'=2,'y'=4,'x'=4] {'z'}, dimensions={0} | all-to-all | bytes 262144 | tf_op jit(solution)/shard_map/all_to_all | solution.py:507
  35.7 1.9 %broadcast_in_dim.81 = bf16[16,8,64,128]{3,2,1,0:T(8,128)(2,1)} broadcast(bf16[8,64,128]{2,1,0:T(8,128)(2,1)S(1)} %all_to_all.25), dimensions={1,2,3} | broadcast | bytes 2228224 | tf_op jit(solution)/shard_map/broadcast_in_dim | solution.py:506
  37.7 7.6 %all-to-all-start.1 = ((bf16[16,8,64,128]{3,2,1,0:T(8,128)(2,1)}), bf16[16,8,64,128]{3,2,1,0:T(8,128)(2,1)S(1)}, u32[]{:S(2)}, u32[]{:S(2)}) async-start(bf16[16,8,64,128]{3,2,1,0:T(8,128)(2,1)} %broadcast_in_dim.81), calls=%async_computation.1 | async-start | bytes 4194304 | tf_op jit(solution)/shard_map/all_to_all | solution.py:507
  45.3 3.4 %collective-permute-start.2 = (f32[20,8,1]{2,1,0:T(8,128)S(1)}, f32[20,8,1]{2,1,0:T(8,128)S(1)}, u32[]{:S(2)}, u32[]{:S(2)}) collective-permute-start(f32[20,8,1]{2,1,0:T(8,128)S(1)} %get-tuple-element.53), channel_id=1, source_target_pairs={{0,1},{1,2},{2,3},{3,4},{4,5},{5,6},{6,7},{7,8},{8,9},{9,10},{10,1... | collective-permute-start | bytes 1928 | tf_op jit(solution)/shard_map/ppermute | solution.py:474
  48.7 2.5 %collective-permute-start.3 = (f32[20,8,1]{2,1,0:T(8,128)S(1)}, f32[20,8,1]{2,1,0:T(8,128)S(1)}, u32[]{:S(2)}, u32[]{:S(2)}) collective-permute-start(f32[20,8,1]{2,1,0:T(8,128)S(1)} %get-tuple-element.54), channel_id=1, source_target_pairs={{0,15},{1,0},{2,1},{3,2},{4,3},{5,4},{6,5},{7,6},{8,7},{9,8},{10,9... | collective-permute-start | bytes 1928 | tf_op jit(solution)/shard_map/ppermute | solution.py:474
  51.3 5.3 %collective-permute-start.1 = (bf16[64,1536]{1,0:T(8,128)(2,1)S(1)}, bf16[64,1536]{1,0:T(8,128)(2,1)S(1)}, u32[]{:S(2)}, u32[]{:S(2)}) collective-permute-start(bf16[64,1536]{1,0:T(8,128)(2,1)S(1)} %get-tuple-element.51), channel_id=1, source_target_pairs={{0,15},{1,0},{2,1},{3,2},{4,3},{5,4},{6,5},{7,6},{8,7},{9,8},{10,9... | collective-permute-start | bytes 589832 | tf_op jit(solution)/shard_map/ppermute | solution.py:474
  56.6 1.9 %collective-permute-start = (bf16[64,1536]{1,0:T(8,128)(2,1)S(1)}, bf16[64,1536]{1,0:T(8,128)(2,1)S(1)}, u32[]{:S(2)}, u32[]{:S(2)}) collective-permute-start(bf16[64,1536]{1,0:T(8,128)(2,1)S(1)} %get-tuple-element.52), channel_id=1, source_target_pairs={{0,1},{1,2},{2,3},{3,4},{4,5},{5,6},{6,7},{7,8},{8,9},{9,10},{10,1... | collective-permute-start | bytes 589832 | tf_op jit(solution)/shard_map/ppermute | solution.py:474
  59.2 11.1 %collective-permute-done.2 = f32[20,8,1]{2,1,0:T(8,128)S(1)} collective-permute-done((f32[20,8,1]{2,1,0:T(8,128)S(1)}, f32[20,8,1]{2,1,0:T(8,128)S(1)}, u32[]{:S(2)}, u32[]{:S(2)}) %collective-permute-start.2) | collective-permute-done | bytes 672 | tf_op jit(solution)/shard_map/ppermute | solution.py:474
  75.9 3.3 %prepare.1 = (bf16[384,1536]{1,0:T(8,128)(2,1)}, bf16[256,512]{1,0:T(8,128)(2,1)}) custom-call(bf16[256,1536]{1,0:T(8,128)(2,1)} %bitcast.44, bf16[64,1536]{1,0:T(8,128)(2,1)} %copy-done.7, bf16[64,1536]{1,0:T(8,128)(2,1)} %copy-done.6, f32[1,1536]{1,0:T(1,128)} %reshape.150.gain_ref, f32[20,32,128]{2,1,0:T(8,128)} %bitcast.56), custom_call_target="tpu_custom_call" | custom-call | tf_op jit(solution)/shard_map/prepare/pallas_call | solution.py:92
  79.3 1.9 %collective-permute-start.4 = (bf16[16,8,64,128]{3,2,1,0:T(8,128)(2,1)S(1)}, bf16[16,8,64,128]{3,2,1,0:T(8,128)(2,1)}, u32[]{:S(2)}, u32[]{:S(2)}) collective-permute-start(bf16[16,8,64,128]{3,2,1,0:T(8,128)(2,1)S(1)} %all-to-all-done.1.own_ref), channel_id=1, source_target_pairs={{0,16},{16,0},{1,17},{17,1},{2,18},{18,2},{3,19},{19,3},{4,20},{20... | collective-permute-start | bytes 6291464 | tf_op jit(solution)/shard_map/ppermute | solution.py:519
  81.2 4.3 %collective-permute-done.4.other_ref = bf16[16,8,64,128]{3,2,1,0:T(8,128)(2,1)} collective-permute-done((bf16[16,8,64,128]{3,2,1,0:T(8,128)(2,1)S(1)}, bf16[16,8,64,128]{3,2,1,0:T(8,128)(2,1)}, u32[]{:S(2)}, u32[]{:S(2)}) %collective-permute-start.4) | collective-permute-done | bytes 2097184 | tf_op jit(solution)/shard_map/ppermute | solution.py:519
  85.5 4.0 %unpack.1 = (bf16[768,1536]{1,0:T(8,128)(2,1)}, bf16[1536,512]{1,0:T(8,128)(2,1)}) custom-call(s32[1]{0:T(128)} %bitcast.6.core_ref, bf16[16,8,64,128]{3,2,1,0:T(8,128)(2,1)} %copy-done.2, bf16[16,8,64,128]{3,2,1,0:T(8,128)(2,1)} %collective-permute-done.4.other_ref), custom_call_target="tpu_custom_call" | custom-call | tf_op jit(solution)/shard_map/unpack/pallas_call | solution.py:121
  89.5 2.9 %all-gather.2.cloned.1.call-done = bf16[3072,1152]{1,0:T(8,128)(2,1)} async-done(((bf16[96,1152]{1,0:T(8,128)(2,1)}), bf16[3072,1152]{1,0:T(8,128)(2,1)}) %all-gather.2.cloned.1.call-update) | async-done | bytes 7077904 | tf_op jit(solution)/shard_map/all_gather | solution.py:501
  92.5 14.0 %forward.1 = (bf16[6,384,384]{2,1,0:T(8,128)(2,1)}, f32[20,32,128]{2,1,0:T(8,128)}, bf16[32,24,640]{2,1,0:T(8,128)(2,1)}) custom-call(bf16[384,1536]{1,0:T(8,128)(2,1)} %get-tuple-element.27.normed_ref, bf16[2,1536,1152]{2,1,0:T(8,128)(2,1)} %bitcast.41, bf16[256,1536]{1,0:T(8,128)(2,1)} %bitcast.45, bf16[768,1536]{1,0:T(8,128)(2,1)} %get-tuple-element.32.out_hbm.out_ref, ...), custom_call_target="tpu_custom_call" | custom-call | tf_op jit(solution)/shard_map/forward/pallas_call | solution.py:278
  106.5 7.5 %all-to-all-start.2 = ((bf16[32,24,640]{2,1,0:T(8,128)(2,1)}), bf16[32,24,640]{2,1,0:T(8,128)(2,1)S(1)}, u32[]{:S(2)}, u32[]{:S(2)}) async-start(bf16[32,24,640]{2,1,0:T(8,128)(2,1)} %get-tuple-element.42), calls=%async_computation.2 | async-start | bytes 1966080 | tf_op jit(solution)/shard_map/all_to_all | solution.py:545
  114.0 4.3 %hidden_grad.1 = (f32[256,1536]{1,0:T(8,128)}, bf16[256,768]{1,0:T(8,128)(2,1)}) custom-call(bf16[256,512]{1,0:T(8,128)(2,1)} %get-tuple-element.34.rows_hbm.rows_ref, bf16[1536,512]{1,0:T(8,128)(2,1)} %get-tuple-element.33.head_hbm.head_ref, bf16[768,1536]{1,0:T(8,128)(2,1)} %get-tuple-element.32.out_hbm.out_ref), custom_call_target="tpu_custom_call" | custom-call | tf_op jit(solution)/shard_map/hidden_grad/pallas_call | solution.py:144
  118.4 7.0 %attend_backward.1 = (bf16[256,768]{1,0:T(8,128)(2,1)}, f32[256,768]{1,0:T(8,128)}, f32[256,768]{1,0:T(8,128)}, bf16[2,64,768]{2,1,0:T(8,128)(2,1)}, bf16[2,64,768]{2,1,0:T(8,128)(2,1)}) custom-call(bf16[6,384,384]{2,1,0:T(8,128)(2,1)} %get-tuple-element.37.q_ref.k_ref.v_ref, bf16[6,384,384]{2,1,0:T(8,128)(2,1)} %get-tuple-element.37.q_ref.k_ref.v_ref, ...), custom_call_target="tpu_custom_call" | custom-call | tf_op jit(solution)/shard_map/attend_backward/pallas_call | solution.py:358
  125.4 3.3 %all-to-all-done.2 = bf16[32,24,640]{2,1,0:T(8,128)(2,1)S(1)} async-done(((bf16[32,24,640]{2,1,0:T(8,128)(2,1)}), bf16[32,24,640]{2,1,0:T(8,128)(2,1)S(1)}, u32[]{:S(2)}, u32[]{:S(2)}) %all-to-all-start.2) | async-done | bytes 983072 | tf_op jit(solution)/shard_map/all_to_all | solution.py:545
  131.0 7.9 %all-to-all-start.3 = ((bf16[16,24,128]{2,1,0:T(8,128)(2,1)}), bf16[16,24,128]{2,1,0:T(8,128)(2,1)S(1)}, u32[]{:S(2)}, u32[]{:S(2)}) async-start(bf16[16,24,128]{2,1,0:T(8,128)(2,1)} %sum_pieces.1), calls=%async_computation.3 | async-start | bytes 196608 | tf_op jit(solution)/shard_map/all_to_all | solution.py:524
  138.9 3.5 %collective-permute-start.5 = (bf16[2,64,768]{2,1,0:T(8,128)(2,1)}, bf16[2,64,768]{2,1,0:T(8,128)(2,1)S(1)}, u32[]{:S(2)}, u32[]{:S(2)}) collective-permute-start(bf16[2,64,768]{2,1,0:T(8,128)(2,1)} %get-tuple-element.48), channel_id=1, source_target_pairs={{0,1},{1,2},{2,3},{3,4},{4,5},{5,6},{6,7},{7,8},{8,9},{9,10},{10,1... | collective-permute-start | bytes 589832 | tf_op jit(solution)/shard_map/ppermute | solution.py:474
  142.5 2.9 %collective-permute-start.6 = (bf16[2,64,768]{2,1,0:T(8,128)(2,1)}, bf16[2,64,768]{2,1,0:T(8,128)(2,1)S(1)}, u32[]{:S(2)}, u32[]{:S(2)}) collective-permute-start(bf16[2,64,768]{2,1,0:T(8,128)(2,1)} %get-tuple-element.49), channel_id=1, source_target_pairs={{0,15},{1,0},{2,1},{3,2},{4,3},{5,4},{6,5},{7,6},{8,7},{9,8},{10,9... | collective-permute-start | bytes 589832 | tf_op jit(solution)/shard_map/ppermute | solution.py:474
  145.4 7.5 %all-to-all-done.3 = bf16[16,24,128]{2,1,0:T(8,128)(2,1)S(1)} async-done(((bf16[16,24,128]{2,1,0:T(8,128)(2,1)}), bf16[16,24,128]{2,1,0:T(8,128)(2,1)S(1)}, u32[]{:S(2)}, u32[]{:S(2)}) %all-to-all-start.3) | async-done | bytes 98336 | tf_op jit(solution)/shard_map/all_to_all | solution.py:524
  153.6 5.2 %all-to-all-start.4 = ((f32[16,24,128]{2,1,0:T(8,128)}), f32[16,24,128]{2,1,0:T(8,128)S(1)}, u32[]{:S(2)}, u32[]{:S(2)}) async-start(f32[16,24,128]{2,1,0:T(8,128)} %broadcast_in_dim.89), calls=%async_computation.4 | async-start | bytes 393216 | tf_op jit(solution)/shard_map/all_to_all | solution.py:507
  159.6 8.8 %norm_grad.1 = bf16[256,1536]{1,0:T(8,128)(2,1)} custom-call(bf16[256,768]{1,0:T(8,128)(2,1)} %get-tuple-element.39.dq_ref, f32[256,768]{1,0:T(8,128)} %get-tuple-element.40.dk_ref, f32[256,768]{1,0:T(8,128)} %get-tuple-element.41.dv_ref, bf16[2,64,768]{2,1,0:T(8,128)(2,1)} %copy-done.4, bf16[2,64,768]{2,1,0:T(8,128)(2,1)} %copy-done.5, ...), custom_call_target="tpu_custom_call" | custom-call | tf_op jit(solution)/shard_map/norm_grad/pallas_call | solution.py:411
  (52 shorter events, 15.4 us)
Async XLA Ops:
  7.2 1.0 copy-start
  7.2 85.3 %all-gather.2.cloned.1.call-start = ((), (), s32[]{:S(2)}) async-start(), calls=%async_computation.5 | async-start | bytes 7299072 | tf_op jit(solution)/shard_map/all_gather | solution.py:501
  37.6 7.6 %copy-start.3 = (f32[1,20,8,32]{3,2,1,0:T(8,128)S(1)}, f32[1,20,8,32]{3,2,1,0:T(8,128)}, u32[]{:S(2)}) copy-start(f32[1,20,8,32]{3,2,1,0:T(8,128)} %param.12) | copy-start | bytes 61444
  37.6 13.6 %copy-start.1 = (bf16[1,8,32,1536]{3,2,1,0:T(8,128)(2,1)S(1)}, bf16[1,8,32,1536]{3,2,1,0:T(8,128)(2,1)}, u32[]{:S(2)}) copy-start(bf16[1,8,32,1536]{3,2,1,0:T(8,128)(2,1)} %param.7) | copy-start | bytes 2359300
  37.6 20.9 %copy-start.8 = (f32[1536]{0:T(1024)S(1)}, f32[1536]{0:T(1024)}, u32[]{:S(2)}) copy-start(f32[1536]{0:T(1024)} %param.8) | copy-start | bytes 18436
  37.7 41.6 %all-to-all-start.1 = ((bf16[16,8,64,128]{3,2,1,0:T(8,128)(2,1)}), bf16[16,8,64,128]{3,2,1,0:T(8,128)(2,1)S(1)}, u32[]{:S(2)}, u32[]{:S(2)}) async-start(bf16[16,8,64,128]{3,2,1,0:T(8,128)(2,1)} %broadcast_in_dim.81), calls=%async_computation.1 | async-start | bytes 4194304 | tf_op jit(solution)/shard_map/all_to_all | solution.py:507
  45.3 25.0 %collective-permute-start.2 = (f32[20,8,1]{2,1,0:T(8,128)S(1)}, f32[20,8,1]{2,1,0:T(8,128)S(1)}, u32[]{:S(2)}, u32[]{:S(2)}) collective-permute-start(f32[20,8,1]{2,1,0:T(8,128)S(1)} %get-tuple-element.53), channel_id=1, source_target_pairs={{0,1},{1,2},{2,3},{3,4},{4,5},{5,6},{6,7},{7,8},{8,9},{9,10},{10,1... | collective-permute-start | bytes 1928 | tf_op jit(solution)/shard_map/ppermute | solution.py:474
  48.7 23.1 %collective-permute-start.3 = (f32[20,8,1]{2,1,0:T(8,128)S(1)}, f32[20,8,1]{2,1,0:T(8,128)S(1)}, u32[]{:S(2)}, u32[]{:S(2)}) collective-permute-start(f32[20,8,1]{2,1,0:T(8,128)S(1)} %get-tuple-element.54), channel_id=1, source_target_pairs={{0,15},{1,0},{2,1},{3,2},{4,3},{5,4},{6,5},{7,6},{8,7},{9,8},{10,9... | collective-permute-start | bytes 1928 | tf_op jit(solution)/shard_map/ppermute | solution.py:474
  51.3 23.9 %collective-permute-start.1 = (bf16[64,1536]{1,0:T(8,128)(2,1)S(1)}, bf16[64,1536]{1,0:T(8,128)(2,1)S(1)}, u32[]{:S(2)}, u32[]{:S(2)}) collective-permute-start(bf16[64,1536]{1,0:T(8,128)(2,1)S(1)} %get-tuple-element.51), channel_id=1, source_target_pairs={{0,15},{1,0},{2,1},{3,2},{4,3},{5,4},{6,5},{7,6},{8,7},{9,8},{10,9... | collective-permute-start | bytes 589832 | tf_op jit(solution)/shard_map/ppermute | solution.py:474
  56.6 18.6 %collective-permute-start = (bf16[64,1536]{1,0:T(8,128)(2,1)S(1)}, bf16[64,1536]{1,0:T(8,128)(2,1)S(1)}, u32[]{:S(2)}, u32[]{:S(2)}) collective-permute-start(bf16[64,1536]{1,0:T(8,128)(2,1)S(1)} %get-tuple-element.52), channel_id=1, source_target_pairs={{0,1},{1,2},{2,3},{3,4},{4,5},{5,6},{6,7},{7,8},{8,9},{9,10},{10,1... | collective-permute-start | bytes 589832 | tf_op jit(solution)/shard_map/ppermute | solution.py:474
  75.2 0.7 copy-start.6
  75.2 0.7 copy-start.7
  79.2 6.3 %copy-start.2 = (bf16[16,8,64,128]{3,2,1,0:T(8,128)(2,1)}, bf16[16,8,64,128]{3,2,1,0:T(8,128)(2,1)S(1)}, u32[]{:S(2)}) copy-start(bf16[16,8,64,128]{3,2,1,0:T(8,128)(2,1)S(1)} %all-to-all-done.1.own_ref) | copy-start | bytes 6291460
  79.3 6.3 %collective-permute-start.4 = (bf16[16,8,64,128]{3,2,1,0:T(8,128)(2,1)S(1)}, bf16[16,8,64,128]{3,2,1,0:T(8,128)(2,1)}, u32[]{:S(2)}, u32[]{:S(2)}) collective-permute-start(bf16[16,8,64,128]{3,2,1,0:T(8,128)(2,1)S(1)} %all-to-all-done.1.own_ref), channel_id=1, source_target_pairs={{0,16},{16,0},{1,17},{17,1},{2,18},{18,2},{3,19},{19,3},{4,20},{20... | collective-permute-start | bytes 6291464 | tf_op jit(solution)/shard_map/ppermute | solution.py:519
  106.5 22.2 %all-to-all-start.2 = ((bf16[32,24,640]{2,1,0:T(8,128)(2,1)}), bf16[32,24,640]{2,1,0:T(8,128)(2,1)S(1)}, u32[]{:S(2)}, u32[]{:S(2)}) async-start(bf16[32,24,640]{2,1,0:T(8,128)(2,1)} %get-tuple-element.42), calls=%async_computation.2 | async-start | bytes 1966080 | tf_op jit(solution)/shard_map/all_to_all | solution.py:545
  131.0 21.9 %all-to-all-start.3 = ((bf16[16,24,128]{2,1,0:T(8,128)(2,1)}), bf16[16,24,128]{2,1,0:T(8,128)(2,1)S(1)}, u32[]{:S(2)}, u32[]{:S(2)}) async-start(bf16[16,24,128]{2,1,0:T(8,128)(2,1)} %sum_pieces.1), calls=%async_computation.3 | async-start | bytes 196608 | tf_op jit(solution)/shard_map/all_to_all | solution.py:524
  138.9 19.9 %collective-permute-start.5 = (bf16[2,64,768]{2,1,0:T(8,128)(2,1)}, bf16[2,64,768]{2,1,0:T(8,128)(2,1)S(1)}, u32[]{:S(2)}, u32[]{:S(2)}) collective-permute-start(bf16[2,64,768]{2,1,0:T(8,128)(2,1)} %get-tuple-element.48), channel_id=1, source_target_pairs={{0,1},{1,2},{2,3},{3,4},{4,5},{5,6},{6,7},{7,8},{8,9},{9,10},{10,1... | collective-permute-start | bytes 589832 | tf_op jit(solution)/shard_map/ppermute | solution.py:474
  142.5 16.4 %collective-permute-start.6 = (bf16[2,64,768]{2,1,0:T(8,128)(2,1)}, bf16[2,64,768]{2,1,0:T(8,128)(2,1)S(1)}, u32[]{:S(2)}, u32[]{:S(2)}) collective-permute-start(bf16[2,64,768]{2,1,0:T(8,128)(2,1)} %get-tuple-element.49), channel_id=1, source_target_pairs={{0,15},{1,0},{2,1},{3,2},{4,3},{5,4},{6,5},{7,6},{8,7},{9,8},{10,9... | collective-permute-start | bytes 589832 | tf_op jit(solution)/shard_map/ppermute | solution.py:474
  153.6 14.8 %all-to-all-start.4 = ((f32[16,24,128]{2,1,0:T(8,128)}), f32[16,24,128]{2,1,0:T(8,128)S(1)}, u32[]{:S(2)}, u32[]{:S(2)}) async-start(f32[16,24,128]{2,1,0:T(8,128)} %broadcast_in_dim.89), calls=%async_computation.4 | async-start | bytes 393216 | tf_op jit(solution)/shard_map/all_to_all | solution.py:507
  158.8 0.7 copy-start.4
  158.9 0.8 copy-start.5
Sparse Core Ops, SparseCore 0:
  10.7 81.7 all-gather.1
